TPU v7x, 512 devices: a whole 4x8x8 slice. The times are simulated.
512 devices in a mesh: prow: 32 (over x, z), pcol: 16 (over y, core).
Axes of the slice: x: 4, y: 8, z: 8, core: 2. Of those that a mesh axis runs over, the one named last changes fastest.
Arguments:
- pool_inverse: float32 [8192, 8192], P('prow', 'pcol'), may hold values from -6 to 6
- panel_blocks: float32 [1, 8192, 512], P(None, 'prow'), may hold values from -0.09375 to 0.09375
- prev_panel: float32 [1, 512, 512], P(None, 'prow'), may hold values from -0.25 to 0.25
- pivot_inverse: float32 [1, 512, 512], P(None, 'pcol'), may hold values from -6 to 6
- top_column: float32 [512, 8192], P('pcol', 'prow'), may hold values from -6 to 6
- top_diag: float32 [512, 512], P('pcol'), may hold values from -6 to 6
- slot_blocks: int32 [1, 64], replicated, may hold values from -1 to 63, as said below
Outputs:
- column_out: float32 [1, 512, 8192], P(None, 'pcol', 'prow')
- cross_out: float32 [1, 512, 512], P(None, 'pcol')
- diag_out: float32 [1, 512, 512], P(None, 'pcol')
Inputs may be any that keep to these rules, and one draw needn't show every extreme that they name: `slot_blocks`: row owner r's slots, entries r * 2 to r * 2 + 1 of a supernode's list, name distinct pool blocks of r * 2 to r * 2 + 1 in ascending order, followed by -1 for unused slots. In every supernode the 2 row owners of some aligned group of 2 use all their slots.
All inputs are finite; a program needn't handle non-finite values.
Results may differ from a plain program's by a relative error of at most 0.0001.
Values sent between devices are 32-bit elements; how exact they have to be, the bound alone decides.
No kernel may reach another device: no remote copies, remote signals or barrier semaphores. Data moves between devices by JAX's collectives and lax.ppermute only.
A program may use at most 64 MiB of HBM per device.

v0:
```python
import jax
import jax.numpy as jnp
from jax import lax
from jax.sharding import PartitionSpec as P

BLK = 128
SLOTS = 2


highest = lax.Precision.HIGHEST


def broadcast(value, axis, source):
    kept = jnp.where(lax.axis_index(axis) == source, value, 0).astype(value.dtype)
    return lax.psum(kept, axis)


def matmul(left, right):
    return jnp.dot(left, right, precision=highest, preferred_element_type=jnp.float32)


def contract_first(left, right):
    return lax.dot_general(
        left, right, (((0,), (0,)), ((), ())), precision=highest, preferred_element_type=jnp.float32
    )


def body(pool_inverse, panel_blocks, prev_panel, pivot_inverse, top_column, top_diag, slot_blocks):
    row_rank = lax.axis_index("prow")
    col_rank = lax.axis_index("pcol")
    groups = lax.axis_size("prow") // lax.axis_size("pcol")
    row_count = pool_inverse.shape[0]
    col_blocks = pool_inverse.shape[1] // BLK
    row_blocks = row_count // BLK
    col_width = pivot_inverse.shape[1]
    thin_rows = prev_panel.shape[1]

    def own_slots(supernode):
        return lax.dynamic_slice_in_dim(slot_blocks[supernode], row_rank * SLOTS, SLOTS)

    def own_panel(supernode):
        keep_rows = jnp.repeat((own_slots(supernode) >= 0).astype(jnp.float32), BLK)
        return panel_blocks[supernode] * keep_rows[:, None]

    diag_rows = top_diag
    supernode = 0
    source = (own_panel(supernode), prev_panel[supernode])
    panels = []
    factors = []
    for member in range(groups):
        received = (
            broadcast(source[0], "prow", groups * col_rank + member),
            broadcast(source[1], "prow", groups * col_rank + member),
        )
        panels.append(received[0])
        factors.append(received[1])
    col_panel = jnp.concatenate(panels, 0)
    col_factor = jnp.concatenate(factors, 0)
    column_ids = lax.dynamic_slice_in_dim(
        slot_blocks[supernode], groups * col_rank * SLOTS, groups * SLOTS
    )
    column_local = jnp.clip(column_ids - col_rank * col_blocks, 0, col_blocks - 1)
    picked = jnp.take(
        pool_inverse.reshape(row_count, col_blocks, BLK), column_local, axis=1
    ).reshape(row_count, -1)
    first_part = lax.dot_general(
        col_panel,
        picked,
        (((0,), (1,)), ((), ())),
        precision=highest,
        preferred_element_type=jnp.float32,
    )
    fresh_column = -lax.psum_scatter(
        first_part + contract_first(col_factor, top_column), "pcol", scatter_dimension=0, tiled=True
    )
    panel_own = own_panel(supernode)
    factor_own = prev_panel[supernode]
    row_local = jnp.clip(own_slots(supernode) - row_rank * row_blocks, 0, row_blocks - 1)

    def pick_rows(source_field):
        return jnp.take(
            source_field.reshape(col_width, row_blocks, BLK), row_local, axis=1
        ).reshape(col_width, -1)

    diag_slice = lax.dynamic_slice_in_dim(diag_rows, row_rank * thin_rows, thin_rows, 1)
    cross_term = matmul(pick_rows(top_column), panel_own) + matmul(diag_slice, factor_own)
    cross_rows = -lax.psum(cross_term, "prow")
    turned = lax.all_to_all(cross_rows, "pcol", split_axis=1, concat_axis=0, tiled=True)
    cross_piece = lax.dynamic_slice_in_dim(turned, row_rank * thin_rows, thin_rows, 0)
    diag_term = matmul(pick_rows(fresh_column), panel_own) + contract_first(cross_piece, factor_own)
    new_diag = pivot_inverse[supernode] - lax.psum(diag_term, "prow")
    cross_rows, diag_rows = (cross_rows, new_diag)
    columns_out = [fresh_column]
    cross_out = [cross_rows]
    diag_out = [diag_rows]
    return (jnp.stack(columns_out), jnp.stack(cross_out), jnp.stack(diag_out))


def solution(mesh):
    in_specs = (
        P("prow", "pcol"),
        P(None, "prow", None),
        P(None, "prow", None),
        P(None, "pcol", None),
        P("pcol", "prow"),
        P("pcol", None),
        P(),
    )
    out_specs = (P(None, "pcol", "prow"), P(None, "pcol", None), P(None, "pcol", None))
    return jax.shard_map(body, mesh=mesh, in_specs=in_specs, out_specs=out_specs, check_vma=False)
```

profile of v0, /device:TPU:24, one launch (start us, length us, event | category | flops | bytes accessed | tf_op | source)
XLA Modules:
  0.0 559.1 jit_solution(11155858880508380020)
XLA Ops:
  7.2 0.0 copy-start
  7.2 0.0 all-reduce.8.cloned.1.call-start
  7.2 1.4 bitcast_select_fusion.2
  8.6 0.0 copy-start.4
  8.6 0.0 all-reduce.8.cloned.1.call-update
  8.7 0.0 all-reduce.10.cloned.1.call-start
  8.7 0.0 copy-start.7
  8.7 0.6 copy-done.7
  9.4 0.1 compare_and_fusion
  9.4 0.1 fusion.30
  9.5 0.0 copy-done.4
  9.5 0.1 broadcast_bitcast_fusion.1
  9.6 0.5 gather_fusion.1
  10.2 0.0 copy-start.1
  10.2 2.2 fusion.8
  12.4 0.0 copy-done.1
  12.4 0.0 copy-start.3
  12.4 0.5 fusion.5
  12.9 0.0 copy-done
  12.9 0.2 copy-done.3
  13.2 0.9 convolution_add_fusion.2
  14.1 0.0 copy-start.2
  14.1 0.0 all-reduce.10.cloned.1.call-update
  14.1 0.0 reduce-scatter.2.cloned.1.call-start
  14.1 1.0 copy-done.2
  15.1 0.2 copy.20
  15.3 0.2 copy.21
  15.5 0.1 compare_and_fusion.1
  15.6 0.6 gather_fusion
  16.2 0.2 copy.22
  16.4 0.1 broadcast_bitcast_fusion
  16.5 0.1 bitcast_select_fusion
  16.6 152.9 %all-reduce.8.cloned.1.call-done = (f32[16,512]{1,0:T(8,128)}, f32[16,512]{1,0:T(8,128)}) async-done(((f32[16,512]{1,0:T(8,128)}, f32[16,512]{1,0:T(8,128)}), (f32[16,512]{1,0:T(8,128)}, f32[16,512]{1,0:T(8,128)})) %all-reduce.8.cloned.1.call-update) | async-done | bytes 65552 | tf_op jit(solution)/shard_map/psum | solution.py:15
  169.5 1.4 fusion.13
  170.9 163.5 %all-reduce.10.cloned.1.call-done = (f32[256,512]{1,0:T(8,128)}, f32[256,512]{1,0:T(8,128)}, f32[32,512]{1,0:T(8,128)}) async-done(((f32[256,512]{1,0:T(8,128)}, f32[256,512]{1,0:T(8,128)}, f32[32,512]{1,0:T(8,128)}), (f32[256,512]{1,0:T(8,128)}, f32[256,512]{1,0:T(8,128)}, f32[32,512]{1,0:T(8,128)})) %all-reduce.10.cloned.1.call-update) | async-done | bytes 1114128 | tf_op jit(solution)/shard_map/psum | solution.py:15
  334.4 3.8 convolution_add_fusion
  338.3 0.0 copy-start.6
  338.3 0.0 reduce-scatter.2.cloned.1.call-update
  338.3 0.0 all-reduce.6.cloned.1.call-start
  338.3 0.8 copy-done.6
  339.1 0.6 fusion.35
  339.7 0.1 copy.29
  339.9 0.2 reshape.134
  340.0 12.0 %all_to_all.19 = f32[16,1,1024]{2,1,0:T(1,128)S(1)} all-to-all(f32[16,1,1024]{2,1,0:T(1,128)S(1)} %reshape.134), channel_id=1, replica_groups=mesh['prow'=32,'pcol'=16] {'pcol'}, dimensions={0} | all-to-all | bytes 131072 | tf_op jit(solution)/shard_map/all_to_all | solution.py:88
  352.0 0.5 broadcast.155
  352.6 0.8 reduce
  353.4 0.1 reshape.135
  353.5 0.2 copy.28
  353.7 0.1 all_to_all.17
  353.8 38.3 %reduce-scatter.2.cloned.1.call-done = f32[32,256]{1,0:T(8,128)} async-done(((f32[512,256]{1,0:T(8,128)}), f32[32,256]{1,0:T(8,128)}) %reduce-scatter.2.cloned.1.call-update) | async-done | bytes 32784 | tf_op jit(solution)/shard_map/reduce_scatter | solution.py:73
  392.1 1.4 negate_bitcast_fusion
  393.4 0.5 gather_fusion.2
  394.0 0.5 fusion.3
  394.5 0.9 convolution_add_fusion.1
  395.4 0.0 copy-start.5
  395.4 0.0 all-reduce.6.cloned.1.call-update
  395.4 155.7 %all-reduce.6.cloned.1.call-done = f32[32,512]{1,0:T(8,128)} async-done(((f32[32,512]{1,0:T(8,128)}), f32[32,512]{1,0:T(8,128)}) %all-reduce.6.cloned.1.call-update) | async-done | bytes 65552 | tf_op jit(solution)/shard_map/psum | solution.py:91
  551.1 0.0 copy-done.5
  551.1 1.5 fusion.17
  (6 shorter events, 0.0 us)
Async XLA Ops:
  7.2 5.8 %copy-start = (f32[32,512]{1,0:T(8,128)S(1)}, f32[32,512]{1,0:T(8,128)}, u32[]{:S(2)}) copy-start(f32[32,512]{1,0:T(8,128)} %param.14) | copy-start | bytes 196612
  7.2 162.3 %all-reduce.8.cloned.1.call-start = ((), (), s32[]{:S(2)}) async-start(), calls=%async_computation.4 | async-start | bytes 131072 | tf_op jit(solution)/shard_map/psum | solution.py:15
  8.6 0.9 copy-start.4
  8.7 325.8 %all-reduce.10.cloned.1.call-start = ((), (), s32[]{:S(2)}) async-start(), calls=%async_computation.5 | async-start | bytes 2228224 | tf_op jit(solution)/shard_map/psum | solution.py:15
  8.7 0.7 copy-start.7
  10.2 2.2 copy-start.1
  12.4 0.8 copy-start.3
  14.1 1.0 copy-start.2
  14.1 378.0 %reduce-scatter.2.cloned.1.call-start = ((), (), s32[]{:S(2)}) async-start(), calls=%async_computation.2 | async-start | bytes 557056 | tf_op jit(solution)/shard_map/reduce_scatter | solution.py:73
  338.3 0.8 copy-start.6
  338.3 212.8 %all-reduce.6.cloned.1.call-start = ((), (), s32[]{:S(2)}) async-start(), calls=%async_computation.3 | async-start | bytes 131072 | tf_op jit(solution)/shard_map/psum | solution.py:91
  395.4 155.7 %copy-start.5 = (f32[1,32,512]{2,1,0:T(8,128)S(1)}, f32[1,32,512]{2,1,0:T(8,128)}, u32[]{:S(2)}) copy-start(f32[1,32,512]{2,1,0:T(8,128)} %param.12) | copy-start | bytes 196612
Sparse Core Ops, SparseCore 0:
  12.1 157.3 all-reduce.7
  173.8 160.5 all-reduce.9
  338.4 53.6 reduce-scatter.1
  395.9 155.0 all-reduce.5
where the time goes:
time: 560 us; the launch traced here: 559 us
  waiting for transfers between devices  510 us (91%)
  between operations  13.9 us (2%)
  blocking collectives  12 us (2%)
  other arithmetic  8.31 us (1%)
  matrix products  8.01 us (1%)
  local copies, waits for them, and re-layouts  6.29 us (1%)
    psum x2, waiting for transfers between devices, broadcast(): return lax.psum(kept, axis)  316 us
    psum x1, waiting for transfers between devices, body(): new_diag = pivot_inverse[supernode] - lax.psum(diag_term, 'prow')  156 us
    reduce_scatter x1, waiting for transfers between devices, body(): lax.psum_scatter(first_part + contract_first(col_factor, top_column), 'pc...  38.3 us
    all_to_all x1, blocking collectives, body(): lax.all_to_all(cross_rows, 'pcol', split_axis=1, concat_axis=0, tiled=True)  12 us
  transfers between devices with their start and end apart: 4, of which 4 were waited for; matrix products, arithmetic and copies ran while one was open for 2% of the time, Pallas kernels for 0%

commit v1 on v0

v1 whole, which is shorter than its diff:
```python
import jax
import jax.numpy as jnp
from jax import lax
from jax.sharding import PartitionSpec as P

BLK = 128
ROWS = 32
COLS = 16
YS = 8

highest = lax.Precision.HIGHEST


def matmul(left, right):
    return jnp.dot(left, right, precision=highest, preferred_element_type=jnp.float32)


def contract(left, right, ldim, rdim):
    return lax.dot_general(
        left, right, (((ldim,), (rdim,)), ((), ())), precision=highest, preferred_element_type=jnp.float32
    )


def spread_pairs():
    pairs = []
    for row in range(ROWS):
        for col in range(COLS):
            y, q, z = row // 4, row % 4, row % 8
            t = (col // 2 - y - 4 + z) % 8
            pairs.append((row * COLS + col, (8 * q + t) * COLS + 2 * y + col % 2))
    return pairs


def body(pool_inverse, panel_blocks, prev_panel, pivot_inverse, top_column, top_diag, slot_blocks):
    row = lax.axis_index("prow")
    col = lax.axis_index("pcol")
    y = col // 2
    core = col % 2
    partner = [(i, i ^ 1) for i in range(COLS)]

    ids = lax.dynamic_slice_in_dim(slot_blocks[0], row * 2, 2)
    first, second = panel_blocks[0, :BLK], panel_blocks[0, BLK:]
    zero = jnp.zeros_like(first)
    factor = jnp.concatenate(
        [
            jnp.where(ids[0] == 2 * row, first, zero),
            jnp.where(ids[0] == 2 * row + 1, first, jnp.where(ids[1] == 2 * row + 1, second, zero)),
        ],
        0,
    )
    prev = prev_panel[0]

    def split_cols(value):
        return value.reshape(value.shape[0], YS, 2, 32)

    def pick_core(value, which):
        return lax.dynamic_index_in_dim(split_cols(value), which, 2, keepdims=False).reshape(value.shape[0], 256)

    piece = (y - row // 4 - 4 + row % 8) % 8
    own_piece = jnp.concatenate(
        [
            lax.dynamic_slice_in_dim(factor, 32 * piece, 32, 0),
            lax.dynamic_slice_in_dim(prev, 2 * piece, 2, 0),
            jnp.zeros((6, 512), jnp.float32),
        ],
        0,
    )
    spread = lax.ppermute(pick_core(own_piece, core), ("prow", "pcol"), spread_pairs())
    pool_other = lax.ppermute(pool_inverse, "pcol", partner)

    diag_slice = lax.dynamic_slice_in_dim(top_diag, row * 16, 16, 1)
    cross_part = matmul(top_column, factor) + matmul(diag_slice, prev)
    swapped = lax.ppermute(
        jnp.concatenate([top_column, pick_core(cross_part, 1 - core)], 1), "pcol", partner
    )
    column_other = swapped[:, :256]
    cross_own = pick_core(cross_part, core)
    cross_other = swapped[:, 256:]
    cross_pair = jnp.where(
        core == 0, jnp.stack([cross_own, cross_other], 1), jnp.stack([cross_other, cross_own], 1)
    )
    prev_rows = prev.reshape(16, 2, 256)
    extra = jnp.concatenate(
        [cross_pair, jnp.concatenate([prev_rows, prev_rows], 0), cross_part.reshape(32, 2, 256)], 1
    )
    send = jnp.concatenate([jnp.broadcast_to(spread[None, :34], (ROWS, 34, 256)), extra], 1)
    got = lax.all_to_all(send, "prow", 0, 0, tiled=True)

    rows_all = got[:, :32].reshape(1024, 256)
    prev_all = got[:, 32:34].reshape(64, 256)
    cross_rows = -jnp.sum(got[:, 34:36], 0)
    prev_stride = lax.dynamic_index_in_dim(
        got.reshape(16, 2, 40, 256)[:, :, 36:38], row // 16, 1, keepdims=False
    ).reshape(16, 512)
    cross_full = -jnp.sum(got[:, 38:40], 0)

    own_rows = lax.dynamic_slice_in_dim(rows_all, 512 * core, 512, 0)
    other_rows = lax.dynamic_slice_in_dim(rows_all, 512 * (1 - core), 512, 0)
    own_prev = lax.dynamic_slice_in_dim(prev_all, 32 * core, 32, 0)
    other_prev = lax.dynamic_slice_in_dim(prev_all, 32 * (1 - core), 32, 0)
    part = (
        contract(own_rows, pool_inverse, 0, 1)
        + contract(other_rows, pool_other, 0, 1)
        + contract(own_prev, top_column, 0, 0)
        + contract(other_prev, column_other, 0, 0)
    )
    cross_send = cross_rows.reshape(2, YS, 32).transpose(1, 0, 2).reshape(YS, 1, 64)
    send = jnp.concatenate(
        [part.reshape(YS, 32, 256), jnp.pad(cross_send, ((0, 0), (0, 7), (0, 192)))], 1
    )
    groups = [[2 * i + k for i in range(YS)] for k in range(2)]
    got = lax.all_to_all(send, "pcol", 0, 0, tiled=True, axis_index_groups=groups)
    fresh = -jnp.sum(got[:, :32], 0)
    cross_cols = got[:, 32, :64].reshape(16, 32)

    diag_part = matmul(fresh, factor) + contract(cross_cols, prev_stride, 0, 0)
    send = jnp.concatenate(
        [
            diag_part.reshape(ROWS, 4, 128),
            jnp.broadcast_to(cross_full.reshape(1, 4, 128), (ROWS, 4, 128)),
        ],
        1,
    )
    got = lax.all_to_all(send, "prow", 0, 0, tiled=True)
    cross_out = got[:, 4:].reshape(1, 32, 512)
    total = jnp.sum(got[:, :4], 0)
    got = lax.all_to_all(jnp.broadcast_to(total, (ROWS, 4, 128)), "prow", 0, 0, tiled=True)
    diag_out = pivot_inverse - got.reshape(1, 32, 512)
    return fresh[None], cross_out, diag_out


def solution(mesh):
    in_specs = (
        P("prow", "pcol"),
        P(None, "prow", None),
        P(None, "prow", None),
        P(None, "pcol", None),
        P("pcol", "prow"),
        P("pcol", None),
        P(),
    )
    out_specs = (P(None, "pcol", "prow"), P(None, "pcol", None), P(None, "pcol", None))
    return jax.shard_map(body, mesh=mesh, in_specs=in_specs, out_specs=out_specs, check_vma=False)
```

time: 560 us -> 133 us (0.24)
  the two profiles are of different devices: /device:TPU:24 before, /device:TPU:2 now
where the time goes in v1:
time: 133 us; the launch traced here: 132 us
  waiting for transfers between devices  50.6 us (38%)
  starting transfers between devices  44.6 us (34%)
  blocking collectives  18.5 us (14%)
  other arithmetic  5.17 us (4%)
  local copies, waits for them, and re-layouts  5.13 us (4%)
  matrix products  4.97 us (4%)
  between operations  3.12 us (2%)
    all_to_all x1, waiting for transfers between devices, body(): got = lax.all_to_all(send, 'prow', 0, 0, tiled=True)  29.5 us
    all_to_all x1, starting transfers between devices, body(): got = lax.all_to_all(send, 'prow', 0, 0, tiled=True)  21.1 us
    all_to_all x1, blocking collectives, body(): got = lax.all_to_all(send, 'prow', 0, 0, tiled=True)  18.5 us
    all_to_all x1, waiting for transfers between devices, body(): lax.all_to_all(send, 'pcol', 0, 0, tiled=True, axis_index_groups=groups)  11.1 us
    ppermute x1, starting transfers between devices, body(): lax.ppermute(pick_core(own_piece, core), ('prow', 'pcol'), spread_pairs())  8.09 us
    all_to_all x1, waiting for transfers between devices, body(): lax.all_to_all(jnp.broadcast_to(total, (ROWS, 4, 128)), 'prow', 0, 0, til...  7.65 us
    all_to_all x1, starting transfers between devices, body(): lax.all_to_all(send, 'pcol', 0, 0, tiled=True, axis_index_groups=groups)  6.58 us
    all_to_all x1, starting transfers between devices, body(): lax.all_to_all(jnp.broadcast_to(total, (ROWS, 4, 128)), 'prow', 0, 0, til...  4.96 us
  transfers between devices with their start and end apart: 6, of which 4 were waited for; matrix products, arithmetic and copies ran while one was open for 3% of the time, Pallas kernels for 0%

profile of v1, /device:TPU:2, one launch (start us, length us, event | category | flops | bytes accessed | tf_op | source)
XLA Modules:
  0.0 132.1 jit_solution(13651438257806243696)
XLA Ops:
  0.6 0.0 copy-start
  0.6 0.0 copy-start.3
  0.7 0.7 constant_dynamic-slice_fusion.2
  1.4 0.6 fusion.19
  3.9 0.0 copy-start.2
  4.0 1.1 select_bitcast_fusion.1
  5.0 1.2 convolution_bitcast_fusion
  6.2 0.0 copy-done
  6.3 0.0 copy-done.3
  6.3 0.3 convolution_add_fusion.4
  6.5 0.2 reshape.89
  6.8 0.8 dynamic-slice_reduce_fusion.1
  7.6 0.1 reshape.90
  7.7 0.0 copy-done.2
  7.7 1.9 %collective-permute-start.1 = (f32[32,512]{1,0:T(8,128)S(1)}, f32[32,512]{1,0:T(8,128)S(1)}, u32[]{:S(2)}, u32[]{:S(2)}) collective-permute-start(f32[32,512]{1,0:T(8,128)S(1)} %pad_maximum_fusion.5), channel_id=1, source_target_pairs={{0,1},{1,0},{2,3},{3,2},{4,5},{5,4},{6,7},{7,6},{8,9},{9,8},{10,11... | collective-permute-start | bytes 196616 | tf_op jit(solution)/shard_map/ppermute | solution.py:73
  9.7 0.2 concatenate.27
  10.0 0.1 concatenate.28
  10.1 0.1 pad.22.clone
  10.2 0.6 maximum_reduce_fusion
  10.7 0.1 reshape.88
  10.8 8.1 %collective-permute-start = (f32[40,256]{1,0:T(8,128)S(1)}, f32[40,256]{1,0:T(8,128)S(1)}, u32[]{:S(2)}, u32[]{:S(2)}) collective-permute-start(f32[40,256]{1,0:T(8,128)S(1)} %reshape.88), channel_id=1, source_target_pairs={{0,64},{1,65},{2,80},{3,81},{4,96},{5,97},{6,112},{7,113},{8,0},{9... | collective-permute-start | bytes 122888 | tf_op jit(solution)/shard_map/ppermute | solution.py:68
  19.0 0.1 stack_reshape.4
  19.2 0.0 collective-permute-done.1
  19.2 0.1 maximum_select_fusion
  19.3 2.3 %collective-permute-done = f32[40,256]{1,0:T(8,128)S(1)} collective-permute-done((f32[40,256]{1,0:T(8,128)S(1)}, f32[40,256]{1,0:T(8,128)S(1)}, u32[]{:S(2)}, u32[]{:S(2)}) %collective-permute-start) | collective-permute-done | bytes 40992 | tf_op jit(solution)/shard_map/ppermute | solution.py:68
  21.6 0.1 broadcast_in_dim.23
  21.7 1.2 pad_maximum_fusion
  22.9 0.0 copy-start.1
  22.9 21.1 %all-to-all-start = ((f32[32,40,256]{2,1,0:T(8,128)}), f32[32,40,256]{2,1,0:T(8,128)S(1)}, u32[]{:S(2)}, u32[]{:S(2)}) async-start(f32[32,40,256]{2,1,0:T(8,128)} %pad_maximum_fusion), calls=%async_computation | async-start | bytes 2621440 | tf_op jit(solution)/shard_map/all_to_all | solution.py:87
  44.0 0.0 copy-done.1
  44.0 1.9 %collective-permute-start.2 = (f32[256,512]{1,0:T(8,128)S(1)}, f32[256,512]{1,0:T(8,128)S(1)}, u32[]{:S(2)}, u32[]{:S(2)}) collective-permute-start(f32[256,512]{1,0:T(8,128)S(1)} %copy-done.1), channel_id=1, source_target_pairs={{0,1},{1,0},{2,3},{3,2},{4,5},{5,4},{6,7},{7,6},{8,9},{9,8},{10,11... | collective-permute-start | bytes 1572872 | tf_op jit(solution)/shard_map/ppermute | solution.py:69
  46.0 29.5 %all-to-all-done = f32[32,40,256]{2,1,0:T(8,128)S(1)} async-done(((f32[32,40,256]{2,1,0:T(8,128)}), f32[32,40,256]{2,1,0:T(8,128)S(1)}, u32[]{:S(2)}, u32[]{:S(2)}) %all-to-all-start) | async-done | bytes 1310752 | tf_op jit(solution)/shard_map/all_to_all | solution.py:87
  75.5 0.1 slice_reduce_fusion.2
  75.7 0.1 neg.31
  75.8 0.1 reshape.95
  75.9 0.1 slice.69
  76.0 1.0 fusion.1
  77.0 0.0 collective-permute-done.2
  77.0 1.0 convolution_add_fusion.2
  78.0 0.4 convolution_add_fusion.1
  78.5 0.4 convolution_add_fusion
  78.9 0.7 select_maximum_fusion
  79.6 6.6 %all-to-all-start.1 = ((f32[8,40,256]{2,1,0:T(8,128)}), f32[8,40,256]{2,1,0:T(8,128)S(1)}, u32[]{:S(2)}, u32[]{:S(2)}) async-start(f32[8,40,256]{2,1,0:T(8,128)} %select_maximum_fusion), calls=%async_computation.1 | async-start | bytes 655360 | tf_op jit(solution)/shard_map/all_to_all | solution.py:112
  86.3 0.0 copy-start.4
  86.3 11.1 %all-to-all-done.1 = f32[8,40,256]{2,1,0:T(8,128)S(1)} async-done(((f32[8,40,256]{2,1,0:T(8,128)}), f32[8,40,256]{2,1,0:T(8,128)S(1)}, u32[]{:S(2)}, u32[]{:S(2)}) %all-to-all-start.1) | async-done | bytes 327712 | tf_op jit(solution)/shard_map/all_to_all | solution.py:112
  97.4 0.4 fusion.3
  97.9 0.1 reshape_squeeze.7
  97.9 0.3 convolution_add_fusion.3
  98.3 18.5 %all_to_all.20 = f32[32,8,128]{2,1,0:T(8,128)S(1)} all-to-all(f32[32,8,128]{2,1,0:T(8,128)S(1)} %pad_maximum_fusion.4), channel_id=1, replica_groups=mesh['prow'=32,'pcol'=16] {'prow'}, dimensions={0} | all-to-all | bytes 262144 | tf_op jit(solution)/shard_map/all_to_all | solution.py:124
  116.8 0.6 broadcast_in_dim.25
  117.5 5.0 %all-to-all-start.3 = ((f32[32,4,128]{2,1,0:T(4,128)}), f32[32,4,128]{2,1,0:T(4,128)S(1)}, u32[]{:S(2)}, u32[]{:S(2)}) async-start(f32[32,4,128]{2,1,0:T(4,128)} %broadcast_in_dim.25), calls=%async_computation.3 | async-start | bytes 131072 | tf_op jit(solution)/shard_map/all_to_all | solution.py:127
  122.5 0.6 negate_bitcast_fusion
  123.1 0.7 reshape.99
  123.7 7.6 %all-to-all-done.3 = f32[32,4,128]{2,1,0:T(4,128)S(1)} async-done(((f32[32,4,128]{2,1,0:T(4,128)}), f32[32,4,128]{2,1,0:T(4,128)S(1)}, u32[]{:S(2)}, u32[]{:S(2)}) %all-to-all-start.3) | async-done | bytes 65568 | tf_op jit(solution)/shard_map/all_to_all | solution.py:127
  131.4 0.0 copy-done.4
  131.4 0.6 sub.30
  (23 shorter events, 0.4 us)
Async XLA Ops:
  0.6 5.6 %copy-start = (f32[32,512]{1,0:T(8,128)S(1)}, f32[32,512]{1,0:T(8,128)}, u32[]{:S(2)}) copy-start(f32[32,512]{1,0:T(8,128)} %param.12) | copy-start | bytes 196612
  0.6 5.6 %copy-start.3 = (f32[1,16,512]{2,1,0:T(8,128)S(1)}, f32[1,16,512]{2,1,0:T(8,128)}, u32[]{:S(2)}) copy-start(f32[1,16,512]{2,1,0:T(8,128)} %param.9) | copy-start | bytes 98308
  3.9 3.7 %copy-start.2 = (f32[32,256]{1,0:T(8,128)S(1)}, f32[32,256]{1,0:T(8,128)}, u32[]{:S(2)}) copy-start(f32[32,256]{1,0:T(8,128)} %param.11) | copy-start | bytes 98308
  7.7 11.4 %collective-permute-start.1 = (f32[32,512]{1,0:T(8,128)S(1)}, f32[32,512]{1,0:T(8,128)S(1)}, u32[]{:S(2)}, u32[]{:S(2)}) collective-permute-start(f32[32,512]{1,0:T(8,128)S(1)} %pad_maximum_fusion.5), channel_id=1, source_target_pairs={{0,1},{1,0},{2,3},{3,2},{4,5},{5,4},{6,7},{7,6},{8,9},{9,8},{10,11... | collective-permute-start | bytes 196616 | tf_op jit(solution)/shard_map/ppermute | solution.py:73
  10.8 10.8 %collective-permute-start = (f32[40,256]{1,0:T(8,128)S(1)}, f32[40,256]{1,0:T(8,128)S(1)}, u32[]{:S(2)}, u32[]{:S(2)}) collective-permute-start(f32[40,256]{1,0:T(8,128)S(1)} %reshape.88), channel_id=1, source_target_pairs={{0,64},{1,65},{2,80},{3,81},{4,96},{5,97},{6,112},{7,113},{8,0},{9... | collective-permute-start | bytes 122888 | tf_op jit(solution)/shard_map/ppermute | solution.py:68
  22.9 21.1 %copy-start.1 = (f32[256,512]{1,0:T(8,128)S(1)}, f32[256,512]{1,0:T(8,128)}, u32[]{:S(2)}) copy-start(f32[256,512]{1,0:T(8,128)} %param.7) | copy-start | bytes 1572868
  22.9 52.6 %all-to-all-start = ((f32[32,40,256]{2,1,0:T(8,128)}), f32[32,40,256]{2,1,0:T(8,128)S(1)}, u32[]{:S(2)}, u32[]{:S(2)}) async-start(f32[32,40,256]{2,1,0:T(8,128)} %pad_maximum_fusion), calls=%async_computation | async-start | bytes 2621440 | tf_op jit(solution)/shard_map/all_to_all | solution.py:87
  44.0 33.0 %collective-permute-start.2 = (f32[256,512]{1,0:T(8,128)S(1)}, f32[256,512]{1,0:T(8,128)S(1)}, u32[]{:S(2)}, u32[]{:S(2)}) collective-permute-start(f32[256,512]{1,0:T(8,128)S(1)} %copy-done.1), channel_id=1, source_target_pairs={{0,1},{1,0},{2,3},{3,2},{4,5},{5,4},{6,7},{7,6},{8,9},{9,8},{10,11... | collective-permute-start | bytes 1572872 | tf_op jit(solution)/shard_map/ppermute | solution.py:69
  79.6 17.8 %all-to-all-start.1 = ((f32[8,40,256]{2,1,0:T(8,128)}), f32[8,40,256]{2,1,0:T(8,128)S(1)}, u32[]{:S(2)}, u32[]{:S(2)}) async-start(f32[8,40,256]{2,1,0:T(8,128)} %select_maximum_fusion), calls=%async_computation.1 | async-start | bytes 655360 | tf_op jit(solution)/shard_map/all_to_all | solution.py:112
  86.3 45.1 %copy-start.4 = (f32[1,32,512]{2,1,0:T(8,128)S(1)}, f32[1,32,512]{2,1,0:T(8,128)}, u32[]{:S(2)}) copy-start(f32[1,32,512]{2,1,0:T(8,128)} %param.10) | copy-start | bytes 196612
  117.5 13.9 %all-to-all-start.3 = ((f32[32,4,128]{2,1,0:T(4,128)}), f32[32,4,128]{2,1,0:T(4,128)S(1)}, u32[]{:S(2)}, u32[]{:S(2)}) async-start(f32[32,4,128]{2,1,0:T(4,128)} %broadcast_in_dim.25), calls=%async_computation.3 | async-start | bytes 131072 | tf_op jit(solution)/shard_map/all_to_all | solution.py:127

commit v2 on v1

v2 whole, which is shorter than its diff:
```python
import jax
import jax.numpy as jnp
from jax import lax
from jax.experimental import pallas as pl
from jax.experimental.pallas import tpu as pltpu
from jax.sharding import PartitionSpec as P


BLK = 128
ROWS = 32
COLS = 16
YS = 8

highest = lax.Precision.HIGHEST
kernel_params = pltpu.CompilerParams(vmem_limit_bytes=16 << 20)


def matmul(left, right):
    return jnp.dot(left, right, precision=highest, preferred_element_type=jnp.float32)


def spread_pairs():
    pairs = []
    for row in range(ROWS):
        for col in range(COLS):
            y, q, z = row // 4, row % 4, row % 8
            t = (col // 2 - y - 4 + z) % 8
            pairs.append((row * COLS + col, (8 * q + t) * COLS + 2 * y + col % 2))
    return pairs


def select_columns(core):
    source = lax.broadcasted_iota(jnp.int32, (512, 256), 0)
    n = lax.broadcasted_iota(jnp.int32, (512, 256), 1)
    wanted = 64 * ((n % 128) // 16) + 32 * core + 16 * (n // 128) + n % 16
    return (source == wanted).astype(jnp.float32)


def dot(left, right):
    return jnp.dot(left, right, precision=highest, preferred_element_type=jnp.float32)


def piece_kernel(slots, panel, prev, out, buffer, sems):
    row = lax.axis_index("prow")
    col = lax.axis_index("pcol")
    piece = (col // 2 + 16 - row // 4 - 4 + row % 8) % 8
    offset = 32 * (piece % 4)
    copies = [
        pltpu.make_async_copy(panel.at[0, pl.ds(BLK * k + offset, 32), :], buffer.at[k], sems.at[k]) for k in range(2)
    ]
    for copy in copies:
        copy.start()
    wanted = 2 * row + piece // 4
    rolled = pltpu.roll(prev[0], (16 - 2 * piece) % 16, 0)
    columns = select_columns(col % 2)
    for copy in copies:
        copy.wait()
    zero = jnp.zeros((32, 512), jnp.float32)
    chunk = jnp.where(slots[0, 2 * row] == wanted, buffer[0], zero)
    chunk = jnp.where(slots[0, 2 * row + 1] == wanted, buffer[1], chunk)
    out[...] = dot(jnp.concatenate([chunk, rolled[:8]], 0), columns)


def own_piece(slot_blocks, panel_blocks, prev_panel):
    return pl.pallas_call(
        piece_kernel,
        out_shape=jax.ShapeDtypeStruct((40, 256), jnp.float32),
        in_specs=[
            pl.BlockSpec(memory_space=pltpu.SMEM),
            pl.BlockSpec(memory_space=pl.ANY),
            pl.BlockSpec(memory_space=pltpu.VMEM),
        ],
        out_specs=pl.BlockSpec(memory_space=pltpu.VMEM),
        scratch_shapes=[pltpu.VMEM((2, 32, 512), jnp.float32), pltpu.SemaphoreType.DMA((2,))],
        compiler_params=kernel_params,
        name="own_piece",
    )(slot_blocks, panel_blocks, prev_panel)


def gather_kernel(spread, cross_own, cross_other, cross_part, prev, out):
    core = lax.axis_index("pcol") % 2
    for k in range(ROWS):
        out[k, :40, :] = spread[:, 128 * (k % 2) : 128 * (k % 2) + 128]
        out[k, 40:, :] = jnp.zeros((8, 128), jnp.float32)
    mine, others = cross_own[...], cross_other[...]
    pair = [jnp.where(core == 0, mine, others), jnp.where(core == 0, others, mine)]
    part = cross_part[...]
    for k in range(ROWS):
        for lane in range(2):
            for who in range(2):
                at = 34 + 2 * who + lane
                out[k, at : at + 1, :] = pair[who][k : k + 1, 128 * lane : 128 * lane + 128]
        for lane in range(4):
            span = slice(128 * lane, 128 * lane + 128)
            out[k, 38 + lane : 39 + lane, :] = prev[0, k % 16 : k % 16 + 1, span]
            out[k, 42 + lane : 43 + lane, :] = part[k : k + 1, span]


def gather_operand(spread, cross_own, cross_other, cross_part, prev_panel):
    return pl.pallas_call(
        gather_kernel,
        out_shape=jax.ShapeDtypeStruct((ROWS, 48, 128), jnp.float32),
        in_specs=[pl.BlockSpec(memory_space=pltpu.VMEM)] * 5,
        out_specs=pl.BlockSpec(memory_space=pltpu.VMEM),
        compiler_params=kernel_params,
        name="gather_operand",
    )(spread, cross_own, cross_other, cross_part, prev_panel)


def product_kernel(got, mine, mine_b, next_z, next_zb, out, cross_full, stride, prev_rows):
    row = lax.axis_index("prow")
    core = lax.axis_index("pcol") % 2
    half = row % 2
    for k in range(ROWS):
        prev_rows[2 * k : 2 * k + 2, :] = got[k, 32:34, :]
    own = got[pl.ds(16 * core, 16), :32, :].reshape(512, 128)
    other = got[pl.ds(16 - 16 * core, 16), :32, :].reshape(512, 128)
    own_prev = prev_rows[pl.ds(pl.multiple_of(32 * core, 32), 32), :]
    other_prev = prev_rows[pl.ds(pl.multiple_of(32 - 32 * core, 32), 32), :]
    prev = jnp.concatenate([own_prev, other_prev], 0)
    sums = -jnp.sum(got[:, 32:48, :], 0)
    cross = jnp.concatenate([sums[2:6], jnp.zeros((4, 128), jnp.float32)], 0)
    cross = jnp.concatenate([cross, jnp.zeros((8, 128), jnp.float32)], 1)
    cross_full[...] = sums[10:14]
    for c in range(COLS):
        stride[4 * c : 4 * c + 4, :] = got[2 * c + row // 16, 38:42, :]
    for left, right, which in ((mine, mine_b, half), (next_z, next_zb, 1 - half)):
        top = jnp.concatenate([left[256:, :256], left[256:, 256:], right[256:, :256], right[256:, 256:]], 0)
        part = dot(left[:256, :], own) + dot(right[:256, :], other) + dot(top.T, prev)
        part = part.T
        for y in range(YS):
            out[2 * y + which, :16, :] = part[16 * y : 16 * y + 16, :]
            out[2 * y + which, 16:, :] = cross


def column_product(got, mine, mine_b, next_z, next_zb):
    return pl.pallas_call(
        product_kernel,
        out_shape=(
            jax.ShapeDtypeStruct((16, 24, 256), jnp.float32),
            jax.ShapeDtypeStruct((4, 128), jnp.float32),
            jax.ShapeDtypeStruct((64, 128), jnp.float32),
        ),
        in_specs=[pl.BlockSpec(memory_space=pltpu.VMEM)] * 5,
        out_specs=(pl.BlockSpec(memory_space=pltpu.VMEM),) * 3,
        scratch_shapes=[pltpu.VMEM((64, 128), jnp.float32)],
        compiler_params=kernel_params,
        name="column_product",
    )(got, mine, mine_b, next_z, next_zb)


def diag_kernel(got, factor, cross_full, stride, fresh_out, out, columns):
    half = lax.axis_index("prow") % 2
    y = lax.axis_index("pcol") // 2
    fresh = []
    for h in range(2):
        total = got[h, :16, :]
        for k in range(1, YS):
            total = total + got[2 * k + h, :16, :]
        fresh.append(-total)
    fresh = jnp.concatenate(fresh, 0)
    fresh_out[0] = fresh
    part = dot(fresh, factor[...])
    for k in range(YS):
        block = got[2 * k + half, 16:24, :128]
        for who in range(2):
            for h in range(2):
                columns[h, 2 * k + who : 2 * k + who + 1, :] = block[2 * who + h : 2 * who + h + 1]
    rows = jnp.concatenate([stride[pl.ds(lane, 16, stride=4), :] for lane in range(4)], 1)
    own = []
    for h in range(2):
        columns[2 + h, :, :] = jnp.zeros((128, 128), jnp.float32)
        columns[2 + h, :, :16] = columns[h, :16, :].T
        picked = columns[2 + h, pl.ds(pl.multiple_of(16 * y, 16), 16), :]
        own.append(dot(picked[:, :16], rows))
    part = part + jnp.concatenate(own, 0)
    for k in range(ROWS):
        for lane in range(4):
            out[k, lane : lane + 1, :] = part[k : k + 1, 128 * lane : 128 * lane + 128]
        out[k, 4:8, :] = cross_full[...]


def diag_operand(got, factor, cross_full, stride):
    return pl.pallas_call(
        diag_kernel,
        out_shape=(
            jax.ShapeDtypeStruct((1, 32, 256), jnp.float32),
            jax.ShapeDtypeStruct((ROWS, 8, 128), jnp.float32),
        ),
        in_specs=[pl.BlockSpec(memory_space=pltpu.VMEM)] * 4,
        out_specs=(pl.BlockSpec(memory_space=pltpu.VMEM),) * 2,
        scratch_shapes=[pltpu.VMEM((4, 128, 128), jnp.float32)],
        compiler_params=kernel_params,
        name="diag_operand",
    )(got, factor, cross_full, stride)


def step(pool_inverse, panel_blocks, prev_panel, pivot_inverse, top_column, top_diag, slot_blocks):
    row = lax.axis_index("prow")
    core = lax.axis_index("pcol") % 2
    core_swap = [(i, i ^ 1) for i in range(COLS)]
    row_swap = [(i, i ^ 1) for i in range(ROWS)]

    sent = own_piece(slot_blocks, panel_blocks, prev_panel)
    sent, top_column, top_diag = lax.optimization_barrier((sent, top_column, top_diag))
    spread = lax.ppermute(sent, ("prow", "pcol"), spread_pairs())

    blocks = jnp.concatenate([pool_inverse, jnp.concatenate([top_column[:16], top_column[16:]], 1)], 0)
    blocks_z = lax.ppermute(blocks, "prow", row_swap)
    blocks_b = lax.ppermute(blocks, "pcol", core_swap)

    ids = lax.dynamic_slice_in_dim(slot_blocks[0], row * 2, 2)
    first, second = panel_blocks[0, :BLK], panel_blocks[0, BLK:]
    zero = jnp.zeros_like(first)
    factor = jnp.concatenate(
        [
            jnp.where(ids[0] == 2 * row, first, zero),
            jnp.where(ids[0] == 2 * row + 1, first, jnp.where(ids[1] == 2 * row + 1, second, zero)),
        ],
        0,
    )
    diag_slice = lax.dynamic_slice_in_dim(top_diag, row * 16, 16, 1)
    cross_part = matmul(top_column, factor) + matmul(diag_slice, prev_panel[0])
    cross_sent = matmul(cross_part, select_columns(1 - core))
    cross_own = matmul(cross_part, select_columns(core))
    cross_other = lax.ppermute(cross_sent, "pcol", core_swap)

    spread, blocks_z, blocks_b, cross_other = lax.optimization_barrier((spread, blocks_z, blocks_b, cross_other))
    send = gather_operand(spread, cross_own, cross_other, cross_part, prev_panel)
    got = lax.all_to_all(send, "prow", 0, 0, tiled=True)
    blocks_zb = lax.ppermute(blocks_z, "pcol", core_swap)

    send, cross_full, stride = column_product(got, blocks, blocks_b, blocks_z, blocks_zb)
    groups = [
        [(x * 8 + 2 * z + h) * COLS + 2 * i + k for i in range(YS) for h in range(2)]
        for x in range(4)
        for z in range(4)
        for k in range(2)
    ]
    got = lax.all_to_all(send, ("prow", "pcol"), 0, 0, tiled=True, axis_index_groups=groups)
    fresh, send = diag_operand(got, factor, cross_full, stride)
    got = lax.all_to_all(send, "prow", 0, 0, tiled=True)
    cross_out = got[:, 4:].reshape(1, 32, 512)
    total = jnp.sum(got[:, :4], 0)
    got = lax.all_to_all(jnp.broadcast_to(total, (ROWS, 4, 128)), "prow", 0, 0, tiled=True)
    diag_out = pivot_inverse - got.reshape(1, 32, 512)
    return fresh, cross_out, diag_out


def solution(mesh):
    in_specs = (
        P("prow", "pcol"),
        P(None, "prow", None),
        P(None, "prow", None),
        P(None, "pcol", None),
        P("pcol", "prow"),
        P("pcol", None),
        P(),
    )
    out_specs = (P(None, "pcol", "prow"), P(None, "pcol", None), P(None, "pcol", None))
    return jax.shard_map(step, mesh=mesh, in_specs=in_specs, out_specs=out_specs, check_vma=False)
```

time: 133 us -> 126 us (0.947)
  waiting for transfers between devices: 50.6 us -> 41 us
  starting transfers between devices: 44.6 us -> 51.7 us
  Pallas kernels: 0 us -> 6.13 us
  other arithmetic: 5.17 us -> 0.82 us
  matrix products: 4.97 us -> 1.27 us
  blocking collectives: 18.5 us -> 15.9 us
    all_to_all x3, waiting for transfers between devices: 48.3 us -> 37.8 us  [the longest x1 16.9 us: step(): got = lax.all_to_all(send, 'prow', 0, 0, tiled=True)]
    ppermute x3 -> x5, starting transfers between devices: 11.9 us -> 18.7 us  [the longest x1 8.09 us: step(): spread = lax.ppermute(sent, ('prow', 'pcol'), spread_pairs())]
    pallas_call x0 -> x4, Pallas kernels: none -> 6.13 us  [the longest x1 2.92 us: column_product(): pl.pallas_call(product_kernel, out_shape=(jax.ShapeDtypeStruct((16, 24, 2...]
    unnamed x11 -> x24, local copies, waits for them, and re-layouts: 0.03 us -> 3.53 us
    dot_general x5 -> x0, matrix products: 3.12 us -> none  [contract(): lax.dot_general(left, right, (((ldim,), (rdim,)), ((), ())), precision=hi...]
    all_to_all x1, blocking collectives: 18.5 us -> 15.9 us  [step(): got = lax.all_to_all(send, 'prow', 0, 0, tiled=True)]
    concatenate x6 -> x2, other arithmetic: 2.58 us -> 0.08 us  [the longest x1 0.04 us: step(): jnp.concatenate([pool_inverse, jnp.concatenate([top_column[:16], top_colu...]
    dynamic_slice x4 -> x1, local copies, waits for them, and re-layouts: 1.55 us -> 0.07 us  [step(): ids = lax.dynamic_slice_in_dim(slot_blocks[0], row * 2, 2)]
  transfers between devices with their start and end apart: 6 -> 8, of which waited for: 4 -> 5; matrix products, arithmetic and copies ran while one was open for 3% -> 2% of each run, Pallas kernels for 0% -> 0%
where the time goes in v2:
time: 126 us; the launch traced here: 125 us
  starting transfers between devices  51.7 us (41%)
  waiting for transfers between devices  41 us (33%)
  blocking collectives  15.9 us (13%)
  Pallas kernels  6.13 us (5%)
  local copies, waits for them, and re-layouts  5.52 us (4%)
  between operations  2.88 us (2%)
  matrix products  1.27 us (1%)
    all_to_all x1, starting transfers between devices, step(): got = lax.all_to_all(send, 'prow', 0, 0, tiled=True)  19.8 us
    all_to_all x1, waiting for transfers between devices, step(): got = lax.all_to_all(send, 'prow', 0, 0, tiled=True)  16.9 us
    all_to_all x1, blocking collectives, step(): got = lax.all_to_all(send, 'prow', 0, 0, tiled=True)  15.9 us
    all_to_all x1, waiting for transfers between devices, step(): lax.all_to_all(send, ('prow', 'pcol'), 0, 0, tiled=True, axis_index_group...  12.6 us
    all_to_all x1, waiting for transfers between devices, step(): lax.all_to_all(jnp.broadcast_to(total, (ROWS, 4, 128)), 'prow', 0, 0, til...  8.24 us
    all_to_all x1, starting transfers between devices, step(): lax.all_to_all(send, ('prow', 'pcol'), 0, 0, tiled=True, axis_index_group...  8.2 us
    ppermute x1, starting transfers between devices, step(): spread = lax.ppermute(sent, ('prow', 'pcol'), spread_pairs())  8.09 us
    all_to_all x1, starting transfers between devices, step(): lax.all_to_all(jnp.broadcast_to(total, (ROWS, 4, 128)), 'prow', 0, 0, til...  4.96 us
  transfers between devices with their start and end apart: 8, of which 5 were waited for; matrix products, arithmetic and copies ran while one was open for 2% of the time, Pallas kernels for 0%

profile of v2, /device:TPU:2, one launch (start us, length us, event | category | flops | bytes accessed | tf_op | source)
XLA Modules:
  0.0 125.3 jit_solution(5282044503903946248)
XLA Ops:
  0.6 0.0 copy-start
  0.6 0.0 copy-start.1
  0.7 1.1 copy-done.1
  1.7 0.0 copy-start.3
  1.7 0.8 copy-done.3
  2.5 0.0 copy-start.5
  2.5 0.7 copy-done.5
  3.1 0.0 copy-start.10
  3.1 0.0 copy-start.9
  3.1 1.3 %own_piece.1 = f32[40,256]{1,0:T(8,128)S(1)} custom-call(s32[1,64]{1,0:T(1,128)S(1)} %copy-done.5, f32[1,256,512]{2,1,0:T(8,128)S(1)} %copy-done.1, f32[1,16,512]{2,1,0:T(8,128)S(1)} %copy-done.3), custom_call_target="tpu_custom_call" | custom-call | tf_op jit(solution)/shard_map/own_piece/pallas_call | solution.py:65
  4.4 0.0 copy-done.10
  4.5 0.0 copy-done.9
  4.5 0.0 copy-start.2
  4.5 4.4 %collective-permute-start.1 = (f32[272,512]{1,0:T(8,128)S(1)}, f32[272,512]{1,0:T(8,128)S(1)}, u32[]{:S(2)}, u32[]{:S(2)}) collective-permute-start(f32[272,512]{1,0:T(8,128)S(1)} %maximum_maximum_fusion.mine), channel_id=1, source_target_pairs={{0,16},{16,0},{32,48},{48,32},{64,80},{80,64},{96,112},{112,96},{1... | collective-permute-start | bytes 1671176 | tf_op jit(solution)/shard_map/ppermute | solution.py:209
  8.9 1.9 %collective-permute-start.2 = (f32[272,512]{1,0:T(8,128)S(1)}, f32[272,512]{1,0:T(8,128)S(1)}, u32[]{:S(2)}, u32[]{:S(2)}) collective-permute-start(f32[272,512]{1,0:T(8,128)S(1)} %maximum_maximum_fusion.mine), channel_id=1, source_target_pairs={{0,1},{1,0},{2,3},{3,2},{4,5},{5,4},{6,7},{7,6},{8,9},{9,8},{10,11... | collective-permute-start | bytes 1671176 | tf_op jit(solution)/shard_map/ppermute | solution.py:210
  10.9 0.0 copy-start.6
  10.9 0.6 copy-done.6
  11.6 0.1 constant_dynamic-slice_fusion
  11.7 0.6 fusion.52
  14.2 0.0 copy-done.2
  14.3 0.0 copy-start.7
  14.3 0.0 copy-start.4
  14.3 0.4 fusion.50
  14.7 0.3 copy-done.7
  15.0 0.0 copy-done
  15.0 0.1 copy-done.4
  15.1 0.3 convolution_add_fusion.cross_part
  15.3 0.3 fusion.10
  15.6 2.4 %collective-permute-start.3 = (f32[32,256]{1,0:T(8,128)S(1)}, f32[32,256]{1,0:T(8,128)S(1)}, u32[]{:S(2)}, u32[]{:S(2)}) collective-permute-start(f32[32,256]{1,0:T(8,128)S(1)} %fusion.10), channel_id=1, source_target_pairs={{0,1},{1,0},{2,3},{3,2},{4,5},{5,4},{6,7},{7,6},{8,9},{9,8},{10,11... | collective-permute-start | bytes 98312 | tf_op jit(solution)/shard_map/ppermute | solution.py:226
  18.1 8.1 %collective-permute-start = (f32[40,256]{1,0:T(8,128)S(1)}, f32[40,256]{1,0:T(8,128)S(1)}, u32[]{:S(2)}, u32[]{:S(2)}) collective-permute-start(f32[40,256]{1,0:T(8,128)S(1)} %own_piece.1), channel_id=1, source_target_pairs={{0,64},{1,65},{2,80},{3,81},{4,96},{5,97},{6,112},{7,113},{8,0},{9... | collective-permute-start | bytes 122888 | tf_op jit(solution)/shard_map/ppermute | solution.py:206
  26.2 0.3 fusion.8.cross_own
  26.5 0.0 collective-permute-done.3.cross_other
  26.5 1.3 %collective-permute-done.spread = f32[40,256]{1,0:T(8,128)S(1)} collective-permute-done((f32[40,256]{1,0:T(8,128)S(1)}, f32[40,256]{1,0:T(8,128)S(1)}, u32[]{:S(2)}, u32[]{:S(2)}) %collective-permute-start) | collective-permute-done | bytes 40992 | tf_op jit(solution)/shard_map/ppermute | solution.py:206
  27.8 0.0 collective-permute-done.1.next_z
  27.8 0.0 collective-permute-done.2.mine_b
  27.8 1.0 gather_operand.1
  28.9 19.8 %all-to-all-start = ((f32[32,48,128]{2,1,0:T(8,128)}), f32[32,48,128]{2,1,0:T(8,128)S(1)}, u32[]{:S(2)}, u32[]{:S(2)}) async-start(f32[32,48,128]{2,1,0:T(8,128)} %gather_operand.1), calls=%async_computation | async-start | bytes 1572864 | tf_op jit(solution)/shard_map/all_to_all | solution.py:230
  48.6 1.9 %collective-permute-start.4 = (f32[272,512]{1,0:T(8,128)S(1)}, f32[272,512]{1,0:T(8,128)S(1)}, u32[]{:S(2)}, u32[]{:S(2)}) collective-permute-start(f32[272,512]{1,0:T(8,128)S(1)} %collective-permute-done.1.next_z), channel_id=1, source_target_pairs={{0,1},{1,0},{2,3},{3,2},{4,5},{5,4},{6,7},{7,6},{8,9},{9,8},{10,11... | collective-permute-start | bytes 1671176 | tf_op jit(solution)/shard_map/ppermute | solution.py:231
  50.5 1.9 %collective-permute-done.4.next_zb = f32[272,512]{1,0:T(8,128)S(1)} collective-permute-done((f32[272,512]{1,0:T(8,128)S(1)}, f32[272,512]{1,0:T(8,128)S(1)}, u32[]{:S(2)}, u32[]{:S(2)}) %collective-permute-start.4) | collective-permute-done | bytes 557088 | tf_op jit(solution)/shard_map/ppermute | solution.py:231
  52.5 16.9 %all-to-all-done.got = f32[32,48,128]{2,1,0:T(8,128)S(1)} async-done(((f32[32,48,128]{2,1,0:T(8,128)}), f32[32,48,128]{2,1,0:T(8,128)S(1)}, u32[]{:S(2)}, u32[]{:S(2)}) %all-to-all-start) | async-done | bytes 786464 | tf_op jit(solution)/shard_map/all_to_all | solution.py:230
  69.4 2.9 %column_product.1 = (f32[16,24,256]{2,1,0:T(8,128)}, f32[4,128]{1,0:T(4,128)S(1)}, f32[64,128]{1,0:T(8,128)S(1)}) custom-call(f32[32,48,128]{2,1,0:T(8,128)S(1)} %all-to-all-done.got, f32[272,512]{1,0:T(8,128)S(1)} %maximum_maximum_fusion.mine, f32[272,512]{1,0:T(8,128)S(1)} %collective-permute-done.2.mine_b, f32[272,512]{1,0:T(8,128)S(1)} %collective-permute-done.1.next_z, ...), custom_call_target="tpu_custom_call" | custom-call | tf_op jit(solution)/shard_map/column_product/pallas_call | solution.py:137
  72.3 0.0 copy-start.8
  72.3 8.2 %all-to-all-start.1 = ((f32[16,24,256]{2,1,0:T(8,128)}), f32[16,24,256]{2,1,0:T(8,128)S(1)}, u32[]{:S(2)}, u32[]{:S(2)}) async-start(f32[16,24,256]{2,1,0:T(8,128)} %get-tuple-element.22), calls=%async_computation.1 | async-start | bytes 786432 | tf_op jit(solution)/shard_map/all_to_all | solution.py:240
  80.5 0.0 copy-done.8
  80.6 12.6 %all-to-all-done.1.got = f32[16,24,256]{2,1,0:T(8,128)S(1)} async-done(((f32[16,24,256]{2,1,0:T(8,128)}), f32[16,24,256]{2,1,0:T(8,128)S(1)}, u32[]{:S(2)}, u32[]{:S(2)}) %all-to-all-start.1) | async-done | bytes 393248 | tf_op jit(solution)/shard_map/all_to_all | solution.py:240
  93.2 0.9 diag_operand.1
  94.1 15.9 %all_to_all.20 = f32[32,8,128]{2,1,0:T(8,128)S(1)} all-to-all(f32[32,8,128]{2,1,0:T(8,128)S(1)} %get-tuple-element.26), channel_id=1, replica_groups=mesh['prow'=32,'pcol'=16] {'prow'}, dimensions={0} | all-to-all | bytes 262144 | tf_op jit(solution)/shard_map/all_to_all | solution.py:242
  110.1 0.6 broadcast_in_dim.7
  110.7 5.0 %all-to-all-start.3 = ((f32[32,4,128]{2,1,0:T(4,128)}), f32[32,4,128]{2,1,0:T(4,128)S(1)}, u32[]{:S(2)}, u32[]{:S(2)}) async-start(f32[32,4,128]{2,1,0:T(4,128)} %broadcast_in_dim.7), calls=%async_computation.3 | async-start | bytes 131072 | tf_op jit(solution)/shard_map/all_to_all | solution.py:245
  115.7 0.7 reshape.25
  116.3 0.0 copy-start.11
  116.3 8.2 %all-to-all-done.3 = f32[32,4,128]{2,1,0:T(4,128)S(1)} async-done(((f32[32,4,128]{2,1,0:T(4,128)}), f32[32,4,128]{2,1,0:T(4,128)S(1)}, u32[]{:S(2)}, u32[]{:S(2)}) %all-to-all-start.3) | async-done | bytes 65568 | tf_op jit(solution)/shard_map/all_to_all | solution.py:245
  124.6 0.0 copy-done.11
  124.6 0.6 sub.28
  (11 shorter events, 0.2 us)
Async XLA Ops:
  0.6 14.4 %copy-start = (f32[32,512]{1,0:T(8,128)S(1)}, f32[32,512]{1,0:T(8,128)}, u32[]{:S(2)}) copy-start(f32[32,512]{1,0:T(8,128)} %param.12) | copy-start | bytes 196612
  0.6 1.1 copy-start.1
  1.7 0.8 copy-start.3
  2.5 0.7 copy-start.5
  3.1 1.3 %copy-start.10 = (f32[32,256]{1,0:T(8,128)S(1)}, f32[32,256]{1,0:T(8,128)}, u32[]{:S(2)}) copy-start(f32[32,256]{1,0:T(8,128)} %param.11) | copy-start | bytes 98308
  3.1 1.3 %copy-start.9 = (f32[256,512]{1,0:T(8,128)S(1)}, f32[256,512]{1,0:T(8,128)}, u32[]{:S(2)}) copy-start(f32[256,512]{1,0:T(8,128)} %param.7) | copy-start | bytes 1572868
  4.5 9.7 %copy-start.2 = (f32[1,256,512]{2,1,0:T(8,128)S(1)}, f32[1,256,512]{2,1,0:T(8,128)}, u32[]{:S(2)}) copy-start(f32[1,256,512]{2,1,0:T(8,128)} %panel.1) | copy-start | bytes 1572868
  4.5 23.3 %collective-permute-start.1 = (f32[272,512]{1,0:T(8,128)S(1)}, f32[272,512]{1,0:T(8,128)S(1)}, u32[]{:S(2)}, u32[]{:S(2)}) collective-permute-start(f32[272,512]{1,0:T(8,128)S(1)} %maximum_maximum_fusion.mine), channel_id=1, source_target_pairs={{0,16},{16,0},{32,48},{48,32},{64,80},{80,64},{96,112},{112,96},{1... | collective-permute-start | bytes 1671176 | tf_op jit(solution)/shard_map/ppermute | solution.py:209
  8.9 18.9 %collective-permute-start.2 = (f32[272,512]{1,0:T(8,128)S(1)}, f32[272,512]{1,0:T(8,128)S(1)}, u32[]{:S(2)}, u32[]{:S(2)}) collective-permute-start(f32[272,512]{1,0:T(8,128)S(1)} %maximum_maximum_fusion.mine), channel_id=1, source_target_pairs={{0,1},{1,0},{2,3},{3,2},{4,5},{5,4},{6,7},{7,6},{8,9},{9,8},{10,11... | collective-permute-start | bytes 1671176 | tf_op jit(solution)/shard_map/ppermute | solution.py:210
  10.9 0.7 copy-start.6
  14.3 0.7 copy-start.7
  14.3 0.8 copy-start.4
  15.6 10.8 %collective-permute-start.3 = (f32[32,256]{1,0:T(8,128)S(1)}, f32[32,256]{1,0:T(8,128)S(1)}, u32[]{:S(2)}, u32[]{:S(2)}) collective-permute-start(f32[32,256]{1,0:T(8,128)S(1)} %fusion.10), channel_id=1, source_target_pairs={{0,1},{1,0},{2,3},{3,2},{4,5},{5,4},{6,7},{7,6},{8,9},{9,8},{10,11... | collective-permute-start | bytes 98312 | tf_op jit(solution)/shard_map/ppermute | solution.py:226
  18.1 9.7 %collective-permute-start = (f32[40,256]{1,0:T(8,128)S(1)}, f32[40,256]{1,0:T(8,128)S(1)}, u32[]{:S(2)}, u32[]{:S(2)}) collective-permute-start(f32[40,256]{1,0:T(8,128)S(1)} %own_piece.1), channel_id=1, source_target_pairs={{0,64},{1,65},{2,80},{3,81},{4,96},{5,97},{6,112},{7,113},{8,0},{9... | collective-permute-start | bytes 122888 | tf_op jit(solution)/shard_map/ppermute | solution.py:206
  28.9 40.5 %all-to-all-start = ((f32[32,48,128]{2,1,0:T(8,128)}), f32[32,48,128]{2,1,0:T(8,128)S(1)}, u32[]{:S(2)}, u32[]{:S(2)}) async-start(f32[32,48,128]{2,1,0:T(8,128)} %gather_operand.1), calls=%async_computation | async-start | bytes 1572864 | tf_op jit(solution)/shard_map/all_to_all | solution.py:230
  48.6 3.9 %collective-permute-start.4 = (f32[272,512]{1,0:T(8,128)S(1)}, f32[272,512]{1,0:T(8,128)S(1)}, u32[]{:S(2)}, u32[]{:S(2)}) collective-permute-start(f32[272,512]{1,0:T(8,128)S(1)} %collective-permute-done.1.next_z), channel_id=1, source_target_pairs={{0,1},{1,0},{2,3},{3,2},{4,5},{5,4},{6,7},{7,6},{8,9},{9,8},{10,11... | collective-permute-start | bytes 1671176 | tf_op jit(solution)/shard_map/ppermute | solution.py:231
  72.3 8.2 %copy-start.8 = (f32[128,512]{1,0:T(8,128)S(1)}, f32[128,512]{1,0:T(8,128)}, u32[]{:S(2)}) copy-start(f32[128,512]{1,0:T(8,128)} %copy-done.7) | copy-start | bytes 786436
  72.3 20.9 %all-to-all-start.1 = ((f32[16,24,256]{2,1,0:T(8,128)}), f32[16,24,256]{2,1,0:T(8,128)S(1)}, u32[]{:S(2)}, u32[]{:S(2)}) async-start(f32[16,24,256]{2,1,0:T(8,128)} %get-tuple-element.22), calls=%async_computation.1 | async-start | bytes 786432 | tf_op jit(solution)/shard_map/all_to_all | solution.py:240
  110.7 13.9 %all-to-all-start.3 = ((f32[32,4,128]{2,1,0:T(4,128)}), f32[32,4,128]{2,1,0:T(4,128)S(1)}, u32[]{:S(2)}, u32[]{:S(2)}) async-start(f32[32,4,128]{2,1,0:T(4,128)} %broadcast_in_dim.7), calls=%async_computation.3 | async-start | bytes 131072 | tf_op jit(solution)/shard_map/all_to_all | solution.py:245
  116.3 8.3 %copy-start.11 = (f32[1,32,512]{2,1,0:T(8,128)S(1)}, f32[1,32,512]{2,1,0:T(8,128)}, u32[]{:S(2)}) copy-start(f32[1,32,512]{2,1,0:T(8,128)} %param.10) | copy-start | bytes 196612

commit v3 on v2

--- a/solution.py
+++ b/solution.py
@@ -13,10 +13,6 @@
 
 highest = lax.Precision.HIGHEST
 kernel_params = pltpu.CompilerParams(vmem_limit_bytes=16 << 20)
-
-
-def matmul(left, right):
-    return jnp.dot(left, right, precision=highest, preferred_element_type=jnp.float32)
 
 
 def spread_pairs():
@@ -40,7 +36,7 @@
     return jnp.dot(left, right, precision=highest, preferred_element_type=jnp.float32)
 
 
-def piece_kernel(slots, panel, prev, out, buffer, sems):
+def piece_kernel(slots, panel, prev, out, ids, buffer, rows, sems):
     row = lax.axis_index("prow")
     col = lax.axis_index("pcol")
     piece = (col // 2 + 16 - row // 4 - 4 + row % 8) % 8
@@ -48,16 +44,18 @@
     copies = [
         pltpu.make_async_copy(panel.at[0, pl.ds(BLK * k + offset, 32), :], buffer.at[k], sems.at[k]) for k in range(2)
     ]
+    copies.append(pltpu.make_async_copy(prev.at[0], rows, sems.at[2]))
+    copies.append(pltpu.make_async_copy(slots, ids, sems.at[3]))
     for copy in copies:
         copy.start()
     wanted = 2 * row + piece // 4
-    rolled = pltpu.roll(prev[0], (16 - 2 * piece) % 16, 0)
     columns = select_columns(col % 2)
     for copy in copies:
         copy.wait()
+    rolled = pltpu.roll(rows[...], (16 - 2 * piece) % 16, 0)
     zero = jnp.zeros((32, 512), jnp.float32)
-    chunk = jnp.where(slots[0, 2 * row] == wanted, buffer[0], zero)
-    chunk = jnp.where(slots[0, 2 * row + 1] == wanted, buffer[1], chunk)
+    chunk = jnp.where(ids[0, 2 * row] == wanted, buffer[0], zero)
+    chunk = jnp.where(ids[0, 2 * row + 1] == wanted, buffer[1], chunk)
     out[...] = dot(jnp.concatenate([chunk, rolled[:8]], 0), columns)
 
 
@@ -65,16 +63,50 @@
     return pl.pallas_call(
         piece_kernel,
         out_shape=jax.ShapeDtypeStruct((40, 256), jnp.float32),
-        in_specs=[
-            pl.BlockSpec(memory_space=pltpu.SMEM),
-            pl.BlockSpec(memory_space=pl.ANY),
-            pl.BlockSpec(memory_space=pltpu.VMEM),
+        in_specs=[pl.BlockSpec(memory_space=pltpu.HBM)] * 3,
+        out_specs=pl.BlockSpec(memory_space=pltpu.VMEM),
+        scratch_shapes=[
+            pltpu.SMEM((1, 64), jnp.int32),
+            pltpu.VMEM((2, 32, 512), jnp.float32),
+            pltpu.VMEM((16, 512), jnp.float32),
+            pltpu.SemaphoreType.DMA((4,)),
         ],
-        out_specs=pl.BlockSpec(memory_space=pltpu.VMEM),
-        scratch_shapes=[pltpu.VMEM((2, 32, 512), jnp.float32), pltpu.SemaphoreType.DMA((2,))],
-        compiler_params=kernel_params,
         name="own_piece",
     )(slot_blocks, panel_blocks, prev_panel)
+
+
+def factor_halves(slots, panel, row):
+    first, second = panel[0, :BLK, :], panel[0, BLK:, :]
+    zero = jnp.zeros_like(first)
+    low = jnp.where(slots[0, 2 * row] == 2 * row, first, zero)
+    high = jnp.where(slots[0, 2 * row + 1] == 2 * row + 1, second, zero)
+    return low, jnp.where(slots[0, 2 * row] == 2 * row + 1, first, high)
+
+
+def cross_kernel(slots, panel, top_column, top_diag, prev, out, mine, others):
+    row = lax.axis_index("prow")
+    core = lax.axis_index("pcol") % 2
+    low, high = factor_halves(slots, panel, row)
+    diag = pltpu.roll(top_diag[...], (512 - 16 * row) % 512, 1)[:, :16]
+    part = dot(top_column[:, :BLK], low) + dot(top_column[:, BLK:], high) + dot(diag, prev[0])
+    out[...] = part
+    mine[...] = dot(part, select_columns(core))
+    others[...] = dot(part, select_columns(1 - core))
+
+
+def cross_rows(slot_blocks, panel_blocks, top_column, top_diag, prev_panel):
+    return pl.pallas_call(
+        cross_kernel,
+        out_shape=(
+            jax.ShapeDtypeStruct((32, 512), jnp.float32),
+            jax.ShapeDtypeStruct((32, 256), jnp.float32),
+            jax.ShapeDtypeStruct((32, 256), jnp.float32),
+        ),
+        in_specs=[pl.BlockSpec(memory_space=pltpu.SMEM)] + [pl.BlockSpec(memory_space=pltpu.VMEM)] * 4,
+        out_specs=(pl.BlockSpec(memory_space=pltpu.VMEM),) * 3,
+        compiler_params=kernel_params,
+        name="cross_rows",
+    )(slot_blocks, panel_blocks, top_column, top_diag, prev_panel)
 
 
 def gather_kernel(spread, cross_own, cross_other, cross_part, prev, out):
@@ -120,7 +152,6 @@
     prev = jnp.concatenate([own_prev, other_prev], 0)
     sums = -jnp.sum(got[:, 32:48, :], 0)
     cross = jnp.concatenate([sums[2:6], jnp.zeros((4, 128), jnp.float32)], 0)
-    cross = jnp.concatenate([cross, jnp.zeros((8, 128), jnp.float32)], 1)
     cross_full[...] = sums[10:14]
     for c in range(COLS):
         stride[4 * c : 4 * c + 4, :] = got[2 * c + row // 16, 38:42, :]
@@ -129,15 +160,16 @@
         part = dot(left[:256, :], own) + dot(right[:256, :], other) + dot(top.T, prev)
         part = part.T
         for y in range(YS):
-            out[2 * y + which, :16, :] = part[16 * y : 16 * y + 16, :]
-            out[2 * y + which, 16:, :] = cross
+            out[2 * y + which, :16, :] = part[16 * y : 16 * y + 16, :128]
+            out[2 * y + which, 16:32, :] = part[16 * y : 16 * y + 16, 128:]
+            out[2 * y + which, 32:, :] = cross
 
 
 def column_product(got, mine, mine_b, next_z, next_zb):
     return pl.pallas_call(
         product_kernel,
         out_shape=(
-            jax.ShapeDtypeStruct((16, 24, 256), jnp.float32),
+            jax.ShapeDtypeStruct((16, 40, 128), jnp.float32),
             jax.ShapeDtypeStruct((4, 128), jnp.float32),
             jax.ShapeDtypeStruct((64, 128), jnp.float32),
         ),
@@ -149,20 +181,22 @@
     )(got, mine, mine_b, next_z, next_zb)
 
 
-def diag_kernel(got, factor, cross_full, stride, fresh_out, out, columns):
-    half = lax.axis_index("prow") % 2
+def diag_kernel(slots, panel, got, cross_full, stride, fresh_out, out, columns):
+    row = lax.axis_index("prow")
+    half = row % 2
     y = lax.axis_index("pcol") // 2
     fresh = []
     for h in range(2):
-        total = got[h, :16, :]
+        total = got[h, :32, :]
         for k in range(1, YS):
-            total = total + got[2 * k + h, :16, :]
-        fresh.append(-total)
+            total = total + got[2 * k + h, :32, :]
+        fresh.append(jnp.concatenate([-total[:16], -total[16:]], 1))
     fresh = jnp.concatenate(fresh, 0)
     fresh_out[0] = fresh
-    part = dot(fresh, factor[...])
+    low, high = factor_halves(slots, panel, row)
+    part = dot(fresh[:, :BLK], low) + dot(fresh[:, BLK:], high)
     for k in range(YS):
-        block = got[2 * k + half, 16:24, :128]
+        block = got[2 * k + half, 32:40, :]
         for who in range(2):
             for h in range(2):
                 columns[h, 2 * k + who : 2 * k + who + 1, :] = block[2 * who + h : 2 * who + h + 1]
@@ -180,24 +214,22 @@
         out[k, 4:8, :] = cross_full[...]
 
 
-def diag_operand(got, factor, cross_full, stride):
+def diag_operand(slot_blocks, panel_blocks, got, cross_full, stride):
     return pl.pallas_call(
         diag_kernel,
         out_shape=(
             jax.ShapeDtypeStruct((1, 32, 256), jnp.float32),
             jax.ShapeDtypeStruct((ROWS, 8, 128), jnp.float32),
         ),
-        in_specs=[pl.BlockSpec(memory_space=pltpu.VMEM)] * 4,
+        in_specs=[pl.BlockSpec(memory_space=pltpu.SMEM)] + [pl.BlockSpec(memory_space=pltpu.VMEM)] * 4,
         out_specs=(pl.BlockSpec(memory_space=pltpu.VMEM),) * 2,
         scratch_shapes=[pltpu.VMEM((4, 128, 128), jnp.float32)],
         compiler_params=kernel_params,
         name="diag_operand",
-    )(got, factor, cross_full, stride)
+    )(slot_blocks, panel_blocks, got, cross_full, stride)
 
 
 def step(pool_inverse, panel_blocks, prev_panel, pivot_inverse, top_column, top_diag, slot_blocks):
-    row = lax.axis_index("prow")
-    core = lax.axis_index("pcol") % 2
     core_swap = [(i, i ^ 1) for i in range(COLS)]
     row_swap = [(i, i ^ 1) for i in range(ROWS)]
 
@@ -209,23 +241,9 @@
     blocks_z = lax.ppermute(blocks, "prow", row_swap)
     blocks_b = lax.ppermute(blocks, "pcol", core_swap)
 
-    ids = lax.dynamic_slice_in_dim(slot_blocks[0], row * 2, 2)
-    first, second = panel_blocks[0, :BLK], panel_blocks[0, BLK:]
-    zero = jnp.zeros_like(first)
-    factor = jnp.concatenate(
-        [
-            jnp.where(ids[0] == 2 * row, first, zero),
-            jnp.where(ids[0] == 2 * row + 1, first, jnp.where(ids[1] == 2 * row + 1, second, zero)),
-        ],
-        0,
-    )
-    diag_slice = lax.dynamic_slice_in_dim(top_diag, row * 16, 16, 1)
-    cross_part = matmul(top_column, factor) + matmul(diag_slice, prev_panel[0])
-    cross_sent = matmul(cross_part, select_columns(1 - core))
-    cross_own = matmul(cross_part, select_columns(core))
+    cross_part, cross_own, cross_sent = cross_rows(slot_blocks, panel_blocks, top_column, top_diag, prev_panel)
     cross_other = lax.ppermute(cross_sent, "pcol", core_swap)
 
-    spread, blocks_z, blocks_b, cross_other = lax.optimization_barrier((spread, blocks_z, blocks_b, cross_other))
     send = gather_operand(spread, cross_own, cross_other, cross_part, prev_panel)
     got = lax.all_to_all(send, "prow", 0, 0, tiled=True)
     blocks_zb = lax.ppermute(blocks_z, "pcol", core_swap)
@@ -238,7 +256,7 @@
         for k in range(2)
     ]
     got = lax.all_to_all(send, ("prow", "pcol"), 0, 0, tiled=True, axis_index_groups=groups)
-    fresh, send = diag_operand(got, factor, cross_full, stride)
+    fresh, send = diag_operand(slot_blocks, panel_blocks, got, cross_full, stride)
     got = lax.all_to_all(send, "prow", 0, 0, tiled=True)
     cross_out = got[:, 4:].reshape(1, 32, 512)
     total = jnp.sum(got[:, :4], 0)

time: 126 us -> 127 us (level)
  blocking collectives: 15.9 us -> 38.4 us
  starting transfers between devices: 51.7 us -> 39.8 us
  waiting for transfers between devices: 41 us -> 36.5 us
  local copies, waits for them, and re-layouts: 5.52 us -> 2.19 us
  Pallas kernels: 6.13 us -> 8.38 us
  between operations: 2.88 us -> 0.82 us
  matrix products: 1.27 us -> 0 us
    ppermute x1, waiting for transfers between devices: 0.01 us -> 25.1 us  [step(): blocks_z = lax.ppermute(blocks, 'prow', row_swap)]
    all_to_all x0 -> x1, blocking collectives: none -> 19.7 us  [step(): lax.all_to_all(send, ('prow', 'pcol'), 0, 0, tiled=True, axis_index_group...]
    all_to_all x1, waiting for transfers between devices: 16.9 us -> 0.01 us  [step(): got = lax.all_to_all(send, 'prow', 0, 0, tiled=True)]
    all_to_all x1 -> x0, waiting for transfers between devices: 12.6 us -> none  [step(): lax.all_to_all(send, ('prow', 'pcol'), 0, 0, tiled=True, axis_index_group...]
    all_to_all x1 -> x0, starting transfers between devices: 8.2 us -> none  [step(): lax.all_to_all(send, ('prow', 'pcol'), 0, 0, tiled=True, axis_index_group...]
    all_to_all x1, blocking collectives: 15.9 us -> 18.7 us  [step(): got = lax.all_to_all(send, 'prow', 0, 0, tiled=True)]
    unnamed x24 -> x14, local copies, waits for them, and re-layouts: 3.53 us -> 0.86 us
    all_to_all x1, starting transfers between devices: 19.8 us -> 17.7 us  [step(): got = lax.all_to_all(send, 'prow', 0, 0, tiled=True)]
  transfers between devices with their start and end apart: 8 -> 7, of which waited for: 5 -> 4; matrix products, arithmetic and copies ran while one was open for 2% -> 1% of each run, Pallas kernels for 0% -> 1%
where the time goes in v3:
time: 127 us
  starting transfers between devices  39.8 us (31%)
  blocking collectives  38.4 us (30%)
  waiting for transfers between devices  36.5 us (29%)
  Pallas kernels  8.38 us (7%)
  local copies, waits for them, and re-layouts  2.19 us (2%)
    ppermute x1, waiting for transfers between devices, step(): blocks_z = lax.ppermute(blocks, 'prow', row_swap)  25.1 us
    all_to_all x1, blocking collectives, step(): lax.all_to_all(send, ('prow', 'pcol'), 0, 0, tiled=True, axis_index_group...  19.7 us
    all_to_all x1, blocking collectives, step(): got = lax.all_to_all(send, 'prow', 0, 0, tiled=True)  18.7 us
    all_to_all x1, starting transfers between devices, step(): got = lax.all_to_all(send, 'prow', 0, 0, tiled=True)  17.7 us
    all_to_all x1, waiting for transfers between devices, step(): lax.all_to_all(jnp.broadcast_to(total, (ROWS, 4, 128)), 'prow', 0, 0, til...  8.24 us
    ppermute x1, starting transfers between devices, step(): spread = lax.ppermute(sent, ('prow', 'pcol'), spread_pairs())  8.09 us
    all_to_all x1, starting transfers between devices, step(): lax.all_to_all(jnp.broadcast_to(total, (ROWS, 4, 128)), 'prow', 0, 0, til...  4.96 us
    ppermute x1, starting transfers between devices, step(): blocks_z = lax.ppermute(blocks, 'prow', row_swap)  3.37 us
  transfers between devices with their start and end apart: 7, of which 4 were waited for; matrix products, arithmetic and copies ran while one was open for 1% of the time, Pallas kernels for 1%

profile of v3, /device:TPU:2, one launch (start us, length us, event | category | flops | bytes accessed | tf_op | source)
XLA Modules:
  0.0 126.8 jit_solution(14866737788524503751)
XLA Ops:
  0.6 0.0 copy-start.4
  0.6 0.0 copy-start
  0.7 0.0 copy-start.1
  0.7 0.0 copy-start.2
  0.7 2.0 %own_piece.1 = f32[40,256]{1,0:T(8,128)} custom-call(s32[1,64]{1,0:T(1,128)} %slots.5, f32[1,256,512]{2,1,0:T(8,128)} %panel.5, f32[1,16,512]{2,1,0:T(8,128)} %prev.5), custom_call_target="tpu_custom_call" | custom-call | tf_op jit(solution)/shard_map/own_piece/pallas_call | solution.py:63
  2.7 8.1 %collective-permute-start = (f32[40,256]{1,0:T(8,128)}, f32[40,256]{1,0:T(8,128)S(1)}, u32[]{:S(2)}, u32[]{:S(2)}) collective-permute-start(f32[40,256]{1,0:T(8,128)} %own_piece.1), channel_id=1, source_target_pairs={{0,64},{1,65},{2,80},{3,81},{4,96},{5,97},{6,112},{7,113},{8,0},{9... | collective-permute-start | bytes 122888 | tf_op jit(solution)/shard_map/ppermute | solution.py:238
  10.8 0.0 copy-done.4
  10.8 0.0 copy-done
  10.8 0.0 copy-done.1
  10.8 0.0 copy-done.2
  10.8 0.0 copy-start.3
  10.9 0.8 copy-done.3
  11.7 1.7 %cross_rows.1 = (f32[32,512]{1,0:T(8,128)S(1)}, f32[32,256]{1,0:T(8,128)S(1)}, f32[32,256]{1,0:T(8,128)S(1)}) custom-call(s32[1,64]{1,0:T(1,128)S(1)} %copy-done.4, f32[1,256,512]{2,1,0:T(8,128)S(1)} %copy-done, f32[32,256]{1,0:T(8,128)S(1)} %copy-done.2, f32[32,512]{1,0:T(8,128)S(1)} %copy-done.3, f32[1,16,512]{2,1,0:T(8,128)S(1)} %copy-done.1), custom_call_target="tpu_custom_call" | custom-call | tf_op jit(solution)/shard_map/cross_rows/pallas_call | solution.py:98
  13.4 1.9 %collective-permute-start.1 = (f32[32,256]{1,0:T(8,128)S(1)}, f32[32,256]{1,0:T(8,128)S(1)}, u32[]{:S(2)}, u32[]{:S(2)}) collective-permute-start(f32[32,256]{1,0:T(8,128)S(1)} %get-tuple-element.18), channel_id=1, source_target_pairs={{0,1},{1,0},{2,3},{3,2},{4,5},{5,4},{6,7},{7,6},{8,9},{9,8},{10,11... | collective-permute-start | bytes 98312 | tf_op jit(solution)/shard_map/ppermute | solution.py:245
  15.3 1.2 collective-permute-done.1.cross_other
  16.5 0.0 collective-permute-done.spread
  16.5 1.0 gather_operand.1
  17.5 0.0 copy-start.5
  17.5 17.7 %all-to-all-start = ((f32[32,48,128]{2,1,0:T(8,128)}), f32[32,48,128]{2,1,0:T(8,128)S(1)}, u32[]{:S(2)}, u32[]{:S(2)}) async-start(f32[32,48,128]{2,1,0:T(8,128)} %gather_operand.1), calls=%async_computation | async-start | bytes 1572864 | tf_op jit(solution)/shard_map/all_to_all | solution.py:248
  35.2 0.0 copy-done.5
  35.3 3.4 %collective-permute-start.3 = (f32[272,512]{1,0:T(8,128)S(1)}, f32[272,512]{1,0:T(8,128)S(1)}, u32[]{:S(2)}, u32[]{:S(2)}) collective-permute-start(f32[272,512]{1,0:T(8,128)S(1)} %maximum_maximum_fusion.mine), channel_id=1, source_target_pairs={{0,16},{16,0},{32,48},{48,32},{64,80},{80,64},{96,112},{112,96},{1... | collective-permute-start | bytes 1671176 | tf_op jit(solution)/shard_map/ppermute | solution.py:241
  38.6 1.9 %collective-permute-start.2 = (f32[272,512]{1,0:T(8,128)S(1)}, f32[272,512]{1,0:T(8,128)S(1)}, u32[]{:S(2)}, u32[]{:S(2)}) collective-permute-start(f32[272,512]{1,0:T(8,128)S(1)} %maximum_maximum_fusion.mine), channel_id=1, source_target_pairs={{0,1},{1,0},{2,3},{3,2},{4,5},{5,4},{6,7},{7,6},{8,9},{9,8},{10,11... | collective-permute-start | bytes 1671176 | tf_op jit(solution)/shard_map/ppermute | solution.py:242
  40.6 25.1 %collective-permute-done.3.next_z = f32[272,512]{1,0:T(8,128)S(1)} collective-permute-done((f32[272,512]{1,0:T(8,128)S(1)}, f32[272,512]{1,0:T(8,128)S(1)}, u32[]{:S(2)}, u32[]{:S(2)}) %collective-permute-start.3) | collective-permute-done | bytes 557088 | tf_op jit(solution)/shard_map/ppermute | solution.py:241
  65.7 1.9 %collective-permute-start.4 = (f32[272,512]{1,0:T(8,128)S(1)}, f32[272,512]{1,0:T(8,128)S(1)}, u32[]{:S(2)}, u32[]{:S(2)}) collective-permute-start(f32[272,512]{1,0:T(8,128)S(1)} %collective-permute-done.3.next_z), channel_id=1, source_target_pairs={{0,1},{1,0},{2,3},{3,2},{4,5},{5,4},{6,7},{7,6},{8,9},{9,8},{10,11... | collective-permute-start | bytes 1671176 | tf_op jit(solution)/shard_map/ppermute | solution.py:249
  67.6 0.0 collective-permute-done.2.mine_b
  67.6 1.9 %collective-permute-done.4.next_zb = f32[272,512]{1,0:T(8,128)S(1)} collective-permute-done((f32[272,512]{1,0:T(8,128)S(1)}, f32[272,512]{1,0:T(8,128)S(1)}, u32[]{:S(2)}, u32[]{:S(2)}) %collective-permute-start.4) | collective-permute-done | bytes 557088 | tf_op jit(solution)/shard_map/ppermute | solution.py:249
  69.5 0.0 all-to-all-done.got
  69.6 2.2 %column_product.1 = (f32[16,40,128]{2,1,0:T(8,128)S(1)}, f32[4,128]{1,0:T(4,128)S(1)}, f32[64,128]{1,0:T(8,128)S(1)}) custom-call(f32[32,48,128]{2,1,0:T(8,128)S(1)} %all-to-all-done.got, f32[272,512]{1,0:T(8,128)S(1)} %maximum_maximum_fusion.mine, f32[272,512]{1,0:T(8,128)S(1)} %collective-permute-done.2.mine_b, ...), custom_call_target="tpu_custom_call" | custom-call | tf_op jit(solution)/shard_map/column_product/pallas_call | solution.py:169
  71.7 19.7 %all_to_all.20.got = f32[16,40,128]{2,1,0:T(8,128)S(1)} all-to-all(f32[16,40,128]{2,1,0:T(8,128)S(1)} %get-tuple-element.20), channel_id=1, replica_groups={{0,16,2,18,4,20,6,22,8,24,10,26,12,28,14,30},{1,17,3,19,5,21,7,23,9,25,..., dimensions={0} | all-to-all | bytes 655360 | tf_op jit(solution)/shard_map/all_to_all | solution.py:258
  91.4 1.4 %diag_operand.1 = (f32[1,32,256]{2,1,0:T(8,128)}, f32[32,8,128]{2,1,0:T(8,128)S(1)}) custom-call(s32[1,64]{1,0:T(1,128)S(1)} %copy-done.4, f32[1,256,512]{2,1,0:T(8,128)S(1)} %copy-done, f32[16,40,128]{2,1,0:T(8,128)S(1)} %all_to_all.20.got, f32[4,128]{1,0:T(4,128)S(1)} %get-tuple-element.21.cross_full, f32[64,128]{1,0:T(8,128)S(1)} %get-tuple-element.22.stride), custom_call_target="tpu_custom_call" | custom-call | tf_op jit(solution)/shard_map/diag_operand/pallas_call | solution.py:218
  92.9 18.7 %all_to_all.21 = f32[32,8,128]{2,1,0:T(8,128)S(1)} all-to-all(f32[32,8,128]{2,1,0:T(8,128)S(1)} %get-tuple-element.24), channel_id=1, replica_groups=mesh['prow'=32,'pcol'=16] {'prow'}, dimensions={0} | all-to-all | bytes 262144 | tf_op jit(solution)/shard_map/all_to_all | solution.py:260
  111.6 0.6 broadcast_in_dim.3
  112.3 5.0 %all-to-all-start.3 = ((f32[32,4,128]{2,1,0:T(4,128)}), f32[32,4,128]{2,1,0:T(4,128)S(1)}, u32[]{:S(2)}, u32[]{:S(2)}) async-start(f32[32,4,128]{2,1,0:T(4,128)} %broadcast_in_dim.3), calls=%async_computation.3 | async-start | bytes 131072 | tf_op jit(solution)/shard_map/all_to_all | solution.py:263
  117.2 0.7 reshape.12
  117.9 0.0 copy-start.6
  117.9 8.2 %all-to-all-done.3 = f32[32,4,128]{2,1,0:T(4,128)S(1)} async-done(((f32[32,4,128]{2,1,0:T(4,128)}), f32[32,4,128]{2,1,0:T(4,128)S(1)}, u32[]{:S(2)}, u32[]{:S(2)}) %all-to-all-start.3) | async-done | bytes 65568 | tf_op jit(solution)/shard_map/all_to_all | solution.py:263
  126.2 0.0 copy-done.6
  126.2 0.6 sub.3
  (4 shorter events, 0.1 us)
Async XLA Ops:
  0.6 10.2 %copy-start.4 = (s32[1,64]{1,0:T(1,128)S(1)}, s32[1,64]{1,0:T(1,128)}, u32[]{:S(2)}) copy-start(s32[1,64]{1,0:T(1,128)} %slots.5) | copy-start | bytes 772
  0.6 10.2 %copy-start = (f32[1,256,512]{2,1,0:T(8,128)S(1)}, f32[1,256,512]{2,1,0:T(8,128)}, u32[]{:S(2)}) copy-start(f32[1,256,512]{2,1,0:T(8,128)} %panel.5) | copy-start | bytes 1572868
  0.7 10.2 %copy-start.1 = (f32[1,16,512]{2,1,0:T(8,128)S(1)}, f32[1,16,512]{2,1,0:T(8,128)}, u32[]{:S(2)}) copy-start(f32[1,16,512]{2,1,0:T(8,128)} %prev.5) | copy-start | bytes 98308
  0.7 10.2 %copy-start.2 = (f32[32,256]{1,0:T(8,128)S(1)}, f32[32,256]{1,0:T(8,128)}, u32[]{:S(2)}) copy-start(f32[32,256]{1,0:T(8,128)} %top_column) | copy-start | bytes 98308
  2.7 13.8 %collective-permute-start = (f32[40,256]{1,0:T(8,128)}, f32[40,256]{1,0:T(8,128)S(1)}, u32[]{:S(2)}, u32[]{:S(2)}) collective-permute-start(f32[40,256]{1,0:T(8,128)} %own_piece.1), channel_id=1, source_target_pairs={{0,64},{1,65},{2,80},{3,81},{4,96},{5,97},{6,112},{7,113},{8,0},{9... | collective-permute-start | bytes 122888 | tf_op jit(solution)/shard_map/ppermute | solution.py:238
  10.8 0.8 copy-start.3
  13.4 3.1 %collective-permute-start.1 = (f32[32,256]{1,0:T(8,128)S(1)}, f32[32,256]{1,0:T(8,128)S(1)}, u32[]{:S(2)}, u32[]{:S(2)}) collective-permute-start(f32[32,256]{1,0:T(8,128)S(1)} %get-tuple-element.18), channel_id=1, source_target_pairs={{0,1},{1,0},{2,3},{3,2},{4,5},{5,4},{6,7},{7,6},{8,9},{9,8},{10,11... | collective-permute-start | bytes 98312 | tf_op jit(solution)/shard_map/ppermute | solution.py:245
  17.5 17.7 %copy-start.5 = (f32[256,512]{1,0:T(8,128)S(1)}, f32[256,512]{1,0:T(8,128)}, u32[]{:S(2)}) copy-start(f32[256,512]{1,0:T(8,128)} %param.7) | copy-start | bytes 1572868
  17.5 52.0 %all-to-all-start = ((f32[32,48,128]{2,1,0:T(8,128)}), f32[32,48,128]{2,1,0:T(8,128)S(1)}, u32[]{:S(2)}, u32[]{:S(2)}) async-start(f32[32,48,128]{2,1,0:T(8,128)} %gather_operand.1), calls=%async_computation | async-start | bytes 1572864 | tf_op jit(solution)/shard_map/all_to_all | solution.py:248
  35.3 30.4 %collective-permute-start.3 = (f32[272,512]{1,0:T(8,128)S(1)}, f32[272,512]{1,0:T(8,128)S(1)}, u32[]{:S(2)}, u32[]{:S(2)}) collective-permute-start(f32[272,512]{1,0:T(8,128)S(1)} %maximum_maximum_fusion.mine), channel_id=1, source_target_pairs={{0,16},{16,0},{32,48},{48,32},{64,80},{80,64},{96,112},{112,96},{1... | collective-permute-start | bytes 1671176 | tf_op jit(solution)/shard_map/ppermute | solution.py:241
  38.6 29.0 %collective-permute-start.2 = (f32[272,512]{1,0:T(8,128)S(1)}, f32[272,512]{1,0:T(8,128)S(1)}, u32[]{:S(2)}, u32[]{:S(2)}) collective-permute-start(f32[272,512]{1,0:T(8,128)S(1)} %maximum_maximum_fusion.mine), channel_id=1, source_target_pairs={{0,1},{1,0},{2,3},{3,2},{4,5},{5,4},{6,7},{7,6},{8,9},{9,8},{10,11... | collective-permute-start | bytes 1671176 | tf_op jit(solution)/shard_map/ppermute | solution.py:242
  65.7 3.8 %collective-permute-start.4 = (f32[272,512]{1,0:T(8,128)S(1)}, f32[272,512]{1,0:T(8,128)S(1)}, u32[]{:S(2)}, u32[]{:S(2)}) collective-permute-start(f32[272,512]{1,0:T(8,128)S(1)} %collective-permute-done.3.next_z), channel_id=1, source_target_pairs={{0,1},{1,0},{2,3},{3,2},{4,5},{5,4},{6,7},{7,6},{8,9},{9,8},{10,11... | collective-permute-start | bytes 1671176 | tf_op jit(solution)/shard_map/ppermute | solution.py:249
  112.3 13.9 %all-to-all-start.3 = ((f32[32,4,128]{2,1,0:T(4,128)}), f32[32,4,128]{2,1,0:T(4,128)S(1)}, u32[]{:S(2)}, u32[]{:S(2)}) async-start(f32[32,4,128]{2,1,0:T(4,128)} %broadcast_in_dim.3), calls=%async_computation.3 | async-start | bytes 131072 | tf_op jit(solution)/shard_map/all_to_all | solution.py:263
  117.9 8.3 %copy-start.6 = (f32[1,32,512]{2,1,0:T(8,128)S(1)}, f32[1,32,512]{2,1,0:T(8,128)}, u32[]{:S(2)}) copy-start(f32[1,32,512]{2,1,0:T(8,128)} %param.10) | copy-start | bytes 196612

commit v4 on v3

--- a/solution.py
+++ b/solution.py
@@ -52,7 +52,7 @@
     columns = select_columns(col % 2)
     for copy in copies:
         copy.wait()
-    rolled = pltpu.roll(rows[...], (16 - 2 * piece) % 16, 0)
+    rolled = pltpu.roll(rows[...], (16 - 4 * (piece // 2)) % 16, 0)
     zero = jnp.zeros((32, 512), jnp.float32)
     chunk = jnp.where(ids[0, 2 * row] == wanted, buffer[0], zero)
     chunk = jnp.where(ids[0, 2 * row + 1] == wanted, buffer[1], chunk)
@@ -83,13 +83,12 @@
     return low, jnp.where(slots[0, 2 * row] == 2 * row + 1, first, high)
 
 
-def cross_kernel(slots, panel, top_column, top_diag, prev, out, mine, others):
+def cross_kernel(slots, panel, top_column, top_diag, prev, mine, others):
     row = lax.axis_index("prow")
     core = lax.axis_index("pcol") % 2
     low, high = factor_halves(slots, panel, row)
     diag = pltpu.roll(top_diag[...], (512 - 16 * row) % 512, 1)[:, :16]
     part = dot(top_column[:, :BLK], low) + dot(top_column[:, BLK:], high) + dot(diag, prev[0])
-    out[...] = part
     mine[...] = dot(part, select_columns(core))
     others[...] = dot(part, select_columns(1 - core))
 
@@ -98,63 +97,67 @@
     return pl.pallas_call(
         cross_kernel,
         out_shape=(
-            jax.ShapeDtypeStruct((32, 512), jnp.float32),
             jax.ShapeDtypeStruct((32, 256), jnp.float32),
             jax.ShapeDtypeStruct((32, 256), jnp.float32),
         ),
         in_specs=[pl.BlockSpec(memory_space=pltpu.SMEM)] + [pl.BlockSpec(memory_space=pltpu.VMEM)] * 4,
-        out_specs=(pl.BlockSpec(memory_space=pltpu.VMEM),) * 3,
+        out_specs=(pl.BlockSpec(memory_space=pltpu.VMEM),) * 2,
         compiler_params=kernel_params,
         name="cross_rows",
     )(slot_blocks, panel_blocks, top_column, top_diag, prev_panel)
 
 
-def gather_kernel(spread, cross_own, cross_other, cross_part, prev, out):
+def gather_kernel(spread, cross_own, cross_other, prev, out):
+    row = lax.axis_index("prow")
     core = lax.axis_index("pcol") % 2
-    for k in range(ROWS):
-        out[k, :40, :] = spread[:, 128 * (k % 2) : 128 * (k % 2) + 128]
-        out[k, 40:, :] = jnp.zeros((8, 128), jnp.float32)
     mine, others = cross_own[...], cross_other[...]
     pair = [jnp.where(core == 0, mine, others), jnp.where(core == 0, others, mine)]
-    part = cross_part[...]
     for k in range(ROWS):
+        out[k, :36, :] = spread[:36, 128 * (k % 2) : 128 * (k % 2) + 128]
         for lane in range(2):
             for who in range(2):
-                at = 34 + 2 * who + lane
+                at = 36 + 2 * who + lane
                 out[k, at : at + 1, :] = pair[who][k : k + 1, 128 * lane : 128 * lane + 128]
-        for lane in range(4):
-            span = slice(128 * lane, 128 * lane + 128)
-            out[k, 38 + lane : 39 + lane, :] = prev[0, k % 16 : k % 16 + 1, span]
-            out[k, 42 + lane : 43 + lane, :] = part[k : k + 1, span]
-
-
-def gather_operand(spread, cross_own, cross_other, cross_part, prev_panel):
+    for parity in range(2):
+
+        @pl.when(row % 2 == parity)
+        def _():
+            for k in range(16):
+                for lane in range(4):
+                    span = slice(128 * lane, 128 * lane + 128)
+                    out[16 * parity + k, 32 + lane : 33 + lane, :] = prev[0, k : k + 1, span]
+
+
+def gather_operand(spread, cross_own, cross_other, prev_panel):
     return pl.pallas_call(
         gather_kernel,
-        out_shape=jax.ShapeDtypeStruct((ROWS, 48, 128), jnp.float32),
-        in_specs=[pl.BlockSpec(memory_space=pltpu.VMEM)] * 5,
+        out_shape=jax.ShapeDtypeStruct((ROWS, 40, 128), jnp.float32),
+        in_specs=[pl.BlockSpec(memory_space=pltpu.VMEM)] * 4,
         out_specs=pl.BlockSpec(memory_space=pltpu.VMEM),
         compiler_params=kernel_params,
         name="gather_operand",
-    )(spread, cross_own, cross_other, cross_part, prev_panel)
-
-
-def product_kernel(got, mine, mine_b, next_z, next_zb, out, cross_full, stride, prev_rows):
+    )(spread, cross_own, cross_other, prev_panel)
+
+
+def product_kernel(got, mine, mine_b, next_z, next_zb, out, cross_keep, cross_give, stride, prev_rows):
     row = lax.axis_index("prow")
     core = lax.axis_index("pcol") % 2
     half = row % 2
-    for k in range(ROWS):
-        prev_rows[2 * k : 2 * k + 2, :] = got[k, 32:34, :]
+    strided = row // 16
+    for k in range(COLS):
+        stride[4 * k : 4 * k + 4, :] = got[2 * k + strided, 32:36, :]
+        prev_rows[4 * k : 4 * k + 4, :] = got[2 * k + 1 - strided, 32:36, :]
     own = got[pl.ds(16 * core, 16), :32, :].reshape(512, 128)
     other = got[pl.ds(16 - 16 * core, 16), :32, :].reshape(512, 128)
     own_prev = prev_rows[pl.ds(pl.multiple_of(32 * core, 32), 32), :]
     other_prev = prev_rows[pl.ds(pl.multiple_of(32 - 32 * core, 32), 32), :]
     prev = jnp.concatenate([own_prev, other_prev], 0)
-    sums = -jnp.sum(got[:, 32:48, :], 0)
-    cross = jnp.concatenate([sums[2:6], jnp.zeros((4, 128), jnp.float32)], 0)
-    cross_full[...] = sums[10:14]
-    for c in range(COLS):
-        stride[4 * c : 4 * c + 4, :] = got[2 * c + row // 16, 38:42, :]
+    sums = -jnp.sum(got[:, 32:40, :], 0)
+    pad = jnp.zeros((4, 128), jnp.float32)
+    cross = jnp.concatenate([sums[4:8], pad], 0)
+    swapped = jnp.concatenate([sums[6:8], sums[4:6], pad], 0)
+    cross_keep[...] = jnp.where(core == 0, cross, swapped)
+    cross_give[...] = jnp.where(core == 0, swapped, cross)
     for left, right, which in ((mine, mine_b, half), (next_z, next_zb, 1 - half)):
         top = jnp.concatenate([left[256:, :256], left[256:, 256:], right[256:, :256], right[256:, 256:]], 0)
         part = dot(left[:256, :], own) + dot(right[:256, :], other) + dot(top.T, prev)
@@ -170,21 +173,23 @@
         product_kernel,
         out_shape=(
             jax.ShapeDtypeStruct((16, 40, 128), jnp.float32),
-            jax.ShapeDtypeStruct((4, 128), jnp.float32),
+            jax.ShapeDtypeStruct((8, 128), jnp.float32),
+            jax.ShapeDtypeStruct((8, 128), jnp.float32),
             jax.ShapeDtypeStruct((64, 128), jnp.float32),
         ),
         in_specs=[pl.BlockSpec(memory_space=pltpu.VMEM)] * 5,
-        out_specs=(pl.BlockSpec(memory_space=pltpu.VMEM),) * 3,
+        out_specs=(pl.BlockSpec(memory_space=pltpu.VMEM),) * 4,
         scratch_shapes=[pltpu.VMEM((64, 128), jnp.float32)],
         compiler_params=kernel_params,
         name="column_product",
     )(got, mine, mine_b, next_z, next_zb)
 
 
-def diag_kernel(slots, panel, got, cross_full, stride, fresh_out, out, columns):
+def diag_kernel(slots, panel, got, cross_keep, cross_got, stride, fresh_out, out, columns):
     row = lax.axis_index("prow")
     half = row % 2
     y = lax.axis_index("pcol") // 2
+    core = lax.axis_index("pcol") % 2
     fresh = []
     for h in range(2):
         total = got[h, :32, :]
@@ -208,25 +213,72 @@
         picked = columns[2 + h, pl.ds(pl.multiple_of(16 * y, 16), 16), :]
         own.append(dot(picked[:, :16], rows))
     part = part + jnp.concatenate(own, 0)
+    lane = lax.broadcasted_iota(jnp.int32, (128, 512), 0)
+    spot = (lax.broadcasted_iota(jnp.int32, (128, 512), 1) == 64 * (lane // 16) + lane % 16).astype(jnp.float32)
+    placed = dot(jnp.concatenate([cross_keep[:2, :], cross_got[:2, :], jnp.zeros((4, 128), jnp.float32)], 0), spot)
+    ours = placed[0:1] + pltpu.roll(placed[1:2], 16, 1)
+    theirs = placed[2:3] + pltpu.roll(placed[3:4], 16, 1)
+    line = jnp.where(core == 0, ours + pltpu.roll(theirs, 32, 1), theirs + pltpu.roll(ours, 32, 1))
+    line = jnp.concatenate([line[:, 128 * k : 128 * k + 128] for k in range(4)], 0)
     for k in range(ROWS):
         for lane in range(4):
             out[k, lane : lane + 1, :] = part[k : k + 1, 128 * lane : 128 * lane + 128]
-        out[k, 4:8, :] = cross_full[...]
-
-
-def diag_operand(slot_blocks, panel_blocks, got, cross_full, stride):
+        out[k, 4:8, :] = line
+
+
+def diag_operand(slot_blocks, panel_blocks, got, cross_keep, cross_got, stride):
     return pl.pallas_call(
         diag_kernel,
         out_shape=(
             jax.ShapeDtypeStruct((1, 32, 256), jnp.float32),
             jax.ShapeDtypeStruct((ROWS, 8, 128), jnp.float32),
         ),
-        in_specs=[pl.BlockSpec(memory_space=pltpu.SMEM)] + [pl.BlockSpec(memory_space=pltpu.VMEM)] * 4,
+        in_specs=[pl.BlockSpec(memory_space=pltpu.SMEM)] + [pl.BlockSpec(memory_space=pltpu.VMEM)] * 5,
         out_specs=(pl.BlockSpec(memory_space=pltpu.VMEM),) * 2,
         scratch_shapes=[pltpu.VMEM((4, 128, 128), jnp.float32)],
         compiler_params=kernel_params,
         name="diag_operand",
-    )(slot_blocks, panel_blocks, got, cross_full, stride)
+    )(slot_blocks, panel_blocks, got, cross_keep, cross_got, stride)
+
+
+def total_kernel(got, out, cross_out):
+    total = jnp.sum(got[:, :4, :], 0)
+    for k in range(ROWS):
+        out[k] = total
+        for lane in range(4):
+            cross_out[0, k : k + 1, 128 * lane : 128 * lane + 128] = got[k, 4 + lane : 5 + lane, :]
+
+
+def total_operand(got):
+    return pl.pallas_call(
+        total_kernel,
+        out_shape=(
+            jax.ShapeDtypeStruct((ROWS, 4, 128), jnp.float32),
+            jax.ShapeDtypeStruct((1, 32, 512), jnp.float32),
+        ),
+        in_specs=[pl.BlockSpec(memory_space=pltpu.VMEM)],
+        out_specs=(pl.BlockSpec(memory_space=pltpu.VMEM),) * 2,
+        compiler_params=kernel_params,
+        name="total_operand",
+    )(got)
+
+
+def last_kernel(got, pivot, out):
+    for k in range(ROWS):
+        for lane in range(4):
+            span = slice(128 * lane, 128 * lane + 128)
+            out[0, k : k + 1, span] = pivot[0, k : k + 1, span] - got[k, lane : lane + 1, :]
+
+
+def last_step(got, pivot_inverse):
+    return pl.pallas_call(
+        last_kernel,
+        out_shape=jax.ShapeDtypeStruct((1, 32, 512), jnp.float32),
+        in_specs=[pl.BlockSpec(memory_space=pltpu.VMEM)] * 2,
+        out_specs=pl.BlockSpec(memory_space=pltpu.VMEM),
+        compiler_params=kernel_params,
+        name="last_step",
+    )(got, pivot_inverse)
 
 
 def step(pool_inverse, panel_blocks, prev_panel, pivot_inverse, top_column, top_diag, slot_blocks):
@@ -241,14 +293,14 @@
     blocks_z = lax.ppermute(blocks, "prow", row_swap)
     blocks_b = lax.ppermute(blocks, "pcol", core_swap)
 
-    cross_part, cross_own, cross_sent = cross_rows(slot_blocks, panel_blocks, top_column, top_diag, prev_panel)
+    cross_own, cross_sent = cross_rows(slot_blocks, panel_blocks, top_column, top_diag, prev_panel)
     cross_other = lax.ppermute(cross_sent, "pcol", core_swap)
 
-    send = gather_operand(spread, cross_own, cross_other, cross_part, prev_panel)
+    send = gather_operand(spread, cross_own, cross_other, prev_panel)
     got = lax.all_to_all(send, "prow", 0, 0, tiled=True)
     blocks_zb = lax.ppermute(blocks_z, "pcol", core_swap)
 
-    send, cross_full, stride = column_product(got, blocks, blocks_b, blocks_z, blocks_zb)
+    send, cross_keep, cross_give, stride = column_product(got, blocks, blocks_b, blocks_z, blocks_zb)
     groups = [
         [(x * 8 + 2 * z + h) * COLS + 2 * i + k for i in range(YS) for h in range(2)]
         for x in range(4)
@@ -256,13 +308,12 @@
         for k in range(2)
     ]
     got = lax.all_to_all(send, ("prow", "pcol"), 0, 0, tiled=True, axis_index_groups=groups)
-    fresh, send = diag_operand(slot_blocks, panel_blocks, got, cross_full, stride)
+    cross_got = lax.ppermute(cross_give, "pcol", core_swap)
+    fresh, send = diag_operand(slot_blocks, panel_blocks, got, cross_keep, cross_got, stride)
     got = lax.all_to_all(send, "prow", 0, 0, tiled=True)
-    cross_out = got[:, 4:].reshape(1, 32, 512)
-    total = jnp.sum(got[:, :4], 0)
-    got = lax.all_to_all(jnp.broadcast_to(total, (ROWS, 4, 128)), "prow", 0, 0, tiled=True)
-    diag_out = pivot_inverse - got.reshape(1, 32, 512)
-    return fresh, cross_out, diag_out
+    total, cross_out = total_operand(got)
+    got = lax.all_to_all(total, "prow", 0, 0, tiled=True)
+    return fresh, cross_out, last_step(got, pivot_inverse)
 
 
 def solution(mesh):

time: 127 us -> 125 us (0.984)
  blocking collectives: 38.4 us -> 32.3 us
  starting transfers between devices: 39.8 us -> 43.2 us
  Pallas kernels: 8.38 us -> 9.72 us
    all_to_all x1, blocking collectives: 19.7 us -> 13.6 us  [step(): got = lax.all_to_all(total, 'prow', 0, 0, tiled=True)]
    ppermute x1, waiting for transfers between devices: 25.1 us -> 22.3 us  [step(): blocks_z = lax.ppermute(blocks, 'prow', row_swap)]
    all_to_all x1, waiting for transfers between devices: 8.24 us -> 10.4 us  [step(): lax.all_to_all(send, ('prow', 'pcol'), 0, 0, tiled=True, axis_index_group...]
    ppermute x0 -> x1, starting transfers between devices: none -> 1.92 us  [step(): cross_got = lax.ppermute(cross_give, 'pcol', core_swap)]
    all_to_all x1, starting transfers between devices: 4.96 us -> 6.4 us  [step(): lax.all_to_all(send, ('prow', 'pcol'), 0, 0, tiled=True, axis_index_group...]
    pallas_call x2 -> x4, Pallas kernels: 2.74 us -> 4.03 us  [the longest x1 1.7 us: cross_rows(): pl.pallas_call(cross_kernel, out_shape=(jax.ShapeDtypeStruct((32, 256), j...]
  transfers between devices with their start and end apart: 7 -> 8, of which waited for: 4 -> 5; matrix products, arithmetic and copies ran while one was open for 1% -> 0% of each run, Pallas kernels for 1% -> 1%
where the time goes in v4:
time: 125 us
  starting transfers between devices  43.2 us (35%)
  waiting for transfers between devices  37 us (30%)
  blocking collectives  32.3 us (26%)
  Pallas kernels  9.72 us (8%)
  local copies, waits for them, and re-layouts  1.58 us (1%)
    ppermute x1, waiting for transfers between devices, step(): blocks_z = lax.ppermute(blocks, 'prow', row_swap)  22.3 us
    all_to_all x1, blocking collectives, step(): got = lax.all_to_all(send, 'prow', 0, 0, tiled=True)  18.7 us
    all_to_all x1, starting transfers between devices, step(): got = lax.all_to_all(send, 'prow', 0, 0, tiled=True)  17.7 us
    all_to_all x1, blocking collectives, step(): got = lax.all_to_all(total, 'prow', 0, 0, tiled=True)  13.6 us
    all_to_all x1, waiting for transfers between devices, step(): lax.all_to_all(send, ('prow', 'pcol'), 0, 0, tiled=True, axis_index_group...  10.4 us
    ppermute x1, starting transfers between devices, step(): spread = lax.ppermute(sent, ('prow', 'pcol'), spread_pairs())  8.09 us
    all_to_all x1, starting transfers between devices, step(): lax.all_to_all(send, ('prow', 'pcol'), 0, 0, tiled=True, axis_index_group...  6.4 us
    ppermute x1, starting transfers between devices, step(): blocks_z = lax.ppermute(blocks, 'prow', row_swap)  3.37 us
  transfers between devices with their start and end apart: 8, of which 5 were waited for; matrix products, arithmetic and copies ran while one was open for 0% of the time, Pallas kernels for 1%

profile of v4, /device:TPU:2, one launch (start us, length us, event | category | flops | bytes accessed | tf_op | source)
XLA Modules:
  0.0 124.7 jit_solution(9741347364501487871)
XLA Ops:
  0.6 0.0 copy-start.6
  0.6 0.0 copy-start.2
  0.7 0.0 copy-start
  0.7 0.0 copy-start.3
  0.7 2.0 %own_piece.1 = f32[40,256]{1,0:T(8,128)} custom-call(s32[1,64]{1,0:T(1,128)} %slots.5, f32[1,256,512]{2,1,0:T(8,128)} %panel.5, f32[1,16,512]{2,1,0:T(8,128)} %prev.5), custom_call_target="tpu_custom_call" | custom-call | tf_op jit(solution)/shard_map/own_piece/pallas_call | solution.py:63
  2.7 8.1 %collective-permute-start = (f32[40,256]{1,0:T(8,128)}, f32[40,256]{1,0:T(8,128)S(1)}, u32[]{:S(2)}, u32[]{:S(2)}) collective-permute-start(f32[40,256]{1,0:T(8,128)} %own_piece.1), channel_id=1, source_target_pairs={{0,64},{1,65},{2,80},{3,81},{4,96},{5,97},{6,112},{7,113},{8,0},{9... | collective-permute-start | bytes 122888 | tf_op jit(solution)/shard_map/ppermute | solution.py:290
  10.8 0.0 copy-done.6
  10.8 0.0 copy-done.2
  10.8 0.0 copy-done
  10.8 0.0 copy-done.3
  10.9 0.0 copy-start.4
  10.9 0.8 copy-done.4
  11.7 1.7 %cross_rows.1 = (f32[32,256]{1,0:T(8,128)S(1)}, f32[32,256]{1,0:T(8,128)S(1)}) custom-call(s32[1,64]{1,0:T(1,128)S(1)} %copy-done.6, f32[1,256,512]{2,1,0:T(8,128)S(1)} %copy-done, f32[32,256]{1,0:T(8,128)S(1)} %copy-done.3, f32[32,512]{1,0:T(8,128)S(1)} %copy-done.4, f32[1,16,512]{2,1,0:T(8,128)S(1)} %copy-done.2), custom_call_target="tpu_custom_call" | custom-call | tf_op jit(solution)/shard_map/cross_rows/pallas_call | solution.py:97
  13.4 1.9 %collective-permute-start.1 = (f32[32,256]{1,0:T(8,128)S(1)}, f32[32,256]{1,0:T(8,128)S(1)}, u32[]{:S(2)}, u32[]{:S(2)}) collective-permute-start(f32[32,256]{1,0:T(8,128)S(1)} %get-tuple-element.20), channel_id=1, source_target_pairs={{0,1},{1,0},{2,3},{3,2},{4,5},{5,4},{6,7},{7,6},{8,9},{9,8},{10,11... | collective-permute-start | bytes 98312 | tf_op jit(solution)/shard_map/ppermute | solution.py:297
  15.3 1.2 collective-permute-done.1.cross_other
  16.5 0.0 collective-permute-done.spread
  16.5 1.0 gather_operand.1
  17.4 0.0 copy-start.7
  17.5 17.7 %all-to-all-start = ((f32[32,40,128]{2,1,0:T(8,128)}), f32[32,40,128]{2,1,0:T(8,128)S(1)}, u32[]{:S(2)}, u32[]{:S(2)}) async-start(f32[32,40,128]{2,1,0:T(8,128)} %gather_operand.1), calls=%async_computation | async-start | bytes 1310720 | tf_op jit(solution)/shard_map/all_to_all | solution.py:300
  35.1 0.0 copy-done.7
  35.2 3.4 %collective-permute-start.3 = (f32[272,512]{1,0:T(8,128)S(1)}, f32[272,512]{1,0:T(8,128)S(1)}, u32[]{:S(2)}, u32[]{:S(2)}) collective-permute-start(f32[272,512]{1,0:T(8,128)S(1)} %maximum_maximum_fusion.mine), channel_id=1, source_target_pairs={{0,16},{16,0},{32,48},{48,32},{64,80},{80,64},{96,112},{112,96},{1... | collective-permute-start | bytes 1671176 | tf_op jit(solution)/shard_map/ppermute | solution.py:293
  38.6 1.9 %collective-permute-start.2 = (f32[272,512]{1,0:T(8,128)S(1)}, f32[272,512]{1,0:T(8,128)S(1)}, u32[]{:S(2)}, u32[]{:S(2)}) collective-permute-start(f32[272,512]{1,0:T(8,128)S(1)} %maximum_maximum_fusion.mine), channel_id=1, source_target_pairs={{0,1},{1,0},{2,3},{3,2},{4,5},{5,4},{6,7},{7,6},{8,9},{9,8},{10,11... | collective-permute-start | bytes 1671176 | tf_op jit(solution)/shard_map/ppermute | solution.py:294
  40.5 22.3 %collective-permute-done.3.next_z = f32[272,512]{1,0:T(8,128)S(1)} collective-permute-done((f32[272,512]{1,0:T(8,128)S(1)}, f32[272,512]{1,0:T(8,128)S(1)}, u32[]{:S(2)}, u32[]{:S(2)}) %collective-permute-start.3) | collective-permute-done | bytes 557088 | tf_op jit(solution)/shard_map/ppermute | solution.py:293
  62.8 1.9 %collective-permute-start.4 = (f32[272,512]{1,0:T(8,128)S(1)}, f32[272,512]{1,0:T(8,128)S(1)}, u32[]{:S(2)}, u32[]{:S(2)}) collective-permute-start(f32[272,512]{1,0:T(8,128)S(1)} %collective-permute-done.3.next_z), channel_id=1, source_target_pairs={{0,1},{1,0},{2,3},{3,2},{4,5},{5,4},{6,7},{7,6},{8,9},{9,8},{10,11... | collective-permute-start | bytes 1671176 | tf_op jit(solution)/shard_map/ppermute | solution.py:301
  64.7 0.0 collective-permute-done.2.mine_b
  64.8 1.9 %collective-permute-done.4.next_zb = f32[272,512]{1,0:T(8,128)S(1)} collective-permute-done((f32[272,512]{1,0:T(8,128)S(1)}, f32[272,512]{1,0:T(8,128)S(1)}, u32[]{:S(2)}, u32[]{:S(2)}) %collective-permute-start.4) | collective-permute-done | bytes 557088 | tf_op jit(solution)/shard_map/ppermute | solution.py:301
  66.7 0.0 all-to-all-done.got
  66.7 2.2 %column_product.1 = (f32[16,40,128]{2,1,0:T(8,128)S(1)}, f32[8,128]{1,0:T(8,128)S(1)}, f32[8,128]{1,0:T(8,128)S(1)}, f32[64,128]{1,0:T(8,128)S(1)}) custom-call(f32[32,40,128]{2,1,0:T(8,128)S(1)} %all-to-all-done.got, f32[272,512]{1,0:T(8,128)S(1)} %maximum_maximum_fusion.mine, f32[272,512]{1,0:T(8,128)S(1)} %collective-permute-done.2.mine_b, ...), custom_call_target="tpu_custom_call" | custom-call | tf_op jit(solution)/shard_map/column_product/pallas_call | solution.py:172
  68.9 0.0 copy-start.1
  68.9 0.7 copy-done.1
  69.6 6.4 %all-to-all-start.1 = ((f32[16,40,128]{2,1,0:T(8,128)}), f32[16,40,128]{2,1,0:T(8,128)S(1)}, u32[]{:S(2)}, u32[]{:S(2)}) async-start(f32[16,40,128]{2,1,0:T(8,128)} %copy-done.1), calls=%async_computation.1 | async-start | bytes 655360 | tf_op jit(solution)/shard_map/all_to_all | solution.py:310
  76.0 1.9 %collective-permute-start.5 = (f32[8,128]{1,0:T(8,128)S(1)}, f32[8,128]{1,0:T(8,128)S(1)}, u32[]{:S(2)}, u32[]{:S(2)}) collective-permute-start(f32[8,128]{1,0:T(8,128)S(1)} %get-tuple-element.23), channel_id=1, source_target_pairs={{0,1},{1,0},{2,3},{3,2},{4,5},{5,4},{6,7},{7,6},{8,9},{9,8},{10,11... | collective-permute-start | bytes 12296 | tf_op jit(solution)/shard_map/ppermute | solution.py:311
  77.9 1.1 collective-permute-done.5.cross_got
  79.1 10.4 %all-to-all-done.1.got = f32[16,40,128]{2,1,0:T(8,128)S(1)} async-done(((f32[16,40,128]{2,1,0:T(8,128)}), f32[16,40,128]{2,1,0:T(8,128)S(1)}, u32[]{:S(2)}, u32[]{:S(2)}) %all-to-all-start.1) | async-done | bytes 327712 | tf_op jit(solution)/shard_map/all_to_all | solution.py:310
  89.5 1.5 %diag_operand.1 = (f32[1,32,256]{2,1,0:T(8,128)}, f32[32,8,128]{2,1,0:T(8,128)S(1)}) custom-call(s32[1,64]{1,0:T(1,128)S(1)} %copy-done.6, f32[1,256,512]{2,1,0:T(8,128)S(1)} %copy-done, f32[16,40,128]{2,1,0:T(8,128)S(1)} %all-to-all-done.1.got, f32[8,128]{1,0:T(8,128)S(1)} %get-tuple-element.22.cross_keep, f32[8,128]{1,0:T(8,128)S(1)} %collective-permute-done.5.cross_got, ...), custom_call_target="tpu_custom_call" | custom-call | tf_op jit(solution)/shard_map/diag_operand/pallas_call | solution.py:230
  91.0 18.7 %all_to_all.20.got = f32[32,8,128]{2,1,0:T(8,128)S(1)} all-to-all(f32[32,8,128]{2,1,0:T(8,128)S(1)} %get-tuple-element.26), channel_id=1, replica_groups=mesh['prow'=32,'pcol'=16] {'prow'}, dimensions={0} | all-to-all | bytes 262144 | tf_op jit(solution)/shard_map/all_to_all | solution.py:313
  109.7 0.7 total_operand.1
  110.3 0.0 copy-start.5
  110.4 13.6 %all_to_all.21.got = f32[32,4,128]{2,1,0:T(4,128)S(1)} all-to-all(f32[32,4,128]{2,1,0:T(4,128)S(1)} %get-tuple-element.28), channel_id=1, replica_groups=mesh['prow'=32,'pcol'=16] {'prow'}, dimensions={0} | all-to-all | bytes 131072 | tf_op jit(solution)/shard_map/all_to_all | solution.py:315
  124.0 0.0 copy-done.5
  124.0 0.7 last_step.1
  (2 shorter events, 0.0 us)
Async XLA Ops:
  0.6 10.2 %copy-start.6 = (s32[1,64]{1,0:T(1,128)S(1)}, s32[1,64]{1,0:T(1,128)}, u32[]{:S(2)}) copy-start(s32[1,64]{1,0:T(1,128)} %slots.5) | copy-start | bytes 772
  0.6 10.2 %copy-start.2 = (f32[1,16,512]{2,1,0:T(8,128)S(1)}, f32[1,16,512]{2,1,0:T(8,128)}, u32[]{:S(2)}) copy-start(f32[1,16,512]{2,1,0:T(8,128)} %prev.5) | copy-start | bytes 98308
  0.7 10.2 %copy-start = (f32[1,256,512]{2,1,0:T(8,128)S(1)}, f32[1,256,512]{2,1,0:T(8,128)}, u32[]{:S(2)}) copy-start(f32[1,256,512]{2,1,0:T(8,128)} %panel.5) | copy-start | bytes 1572868
  0.7 10.2 %copy-start.3 = (f32[32,256]{1,0:T(8,128)S(1)}, f32[32,256]{1,0:T(8,128)}, u32[]{:S(2)}) copy-start(f32[32,256]{1,0:T(8,128)} %top_column) | copy-start | bytes 98308
  2.7 13.8 %collective-permute-start = (f32[40,256]{1,0:T(8,128)}, f32[40,256]{1,0:T(8,128)S(1)}, u32[]{:S(2)}, u32[]{:S(2)}) collective-permute-start(f32[40,256]{1,0:T(8,128)} %own_piece.1), channel_id=1, source_target_pairs={{0,64},{1,65},{2,80},{3,81},{4,96},{5,97},{6,112},{7,113},{8,0},{9... | collective-permute-start | bytes 122888 | tf_op jit(solution)/shard_map/ppermute | solution.py:290
  10.9 0.8 copy-start.4
  13.4 3.1 %collective-permute-start.1 = (f32[32,256]{1,0:T(8,128)S(1)}, f32[32,256]{1,0:T(8,128)S(1)}, u32[]{:S(2)}, u32[]{:S(2)}) collective-permute-start(f32[32,256]{1,0:T(8,128)S(1)} %get-tuple-element.20), channel_id=1, source_target_pairs={{0,1},{1,0},{2,3},{3,2},{4,5},{5,4},{6,7},{7,6},{8,9},{9,8},{10,11... | collective-permute-start | bytes 98312 | tf_op jit(solution)/shard_map/ppermute | solution.py:297
  17.4 17.7 %copy-start.7 = (f32[256,512]{1,0:T(8,128)S(1)}, f32[256,512]{1,0:T(8,128)}, u32[]{:S(2)}) copy-start(f32[256,512]{1,0:T(8,128)} %param.7) | copy-start | bytes 1572868
  17.5 49.2 %all-to-all-start = ((f32[32,40,128]{2,1,0:T(8,128)}), f32[32,40,128]{2,1,0:T(8,128)S(1)}, u32[]{:S(2)}, u32[]{:S(2)}) async-start(f32[32,40,128]{2,1,0:T(8,128)} %gather_operand.1), calls=%async_computation | async-start | bytes 1310720 | tf_op jit(solution)/shard_map/all_to_all | solution.py:300
  35.2 27.6 %collective-permute-start.3 = (f32[272,512]{1,0:T(8,128)S(1)}, f32[272,512]{1,0:T(8,128)S(1)}, u32[]{:S(2)}, u32[]{:S(2)}) collective-permute-start(f32[272,512]{1,0:T(8,128)S(1)} %maximum_maximum_fusion.mine), channel_id=1, source_target_pairs={{0,16},{16,0},{32,48},{48,32},{64,80},{80,64},{96,112},{112,96},{1... | collective-permute-start | bytes 1671176 | tf_op jit(solution)/shard_map/ppermute | solution.py:293
  38.6 26.2 %collective-permute-start.2 = (f32[272,512]{1,0:T(8,128)S(1)}, f32[272,512]{1,0:T(8,128)S(1)}, u32[]{:S(2)}, u32[]{:S(2)}) collective-permute-start(f32[272,512]{1,0:T(8,128)S(1)} %maximum_maximum_fusion.mine), channel_id=1, source_target_pairs={{0,1},{1,0},{2,3},{3,2},{4,5},{5,4},{6,7},{7,6},{8,9},{9,8},{10,11... | collective-permute-start | bytes 1671176 | tf_op jit(solution)/shard_map/ppermute | solution.py:294
  62.8 3.8 %collective-permute-start.4 = (f32[272,512]{1,0:T(8,128)S(1)}, f32[272,512]{1,0:T(8,128)S(1)}, u32[]{:S(2)}, u32[]{:S(2)}) collective-permute-start(f32[272,512]{1,0:T(8,128)S(1)} %collective-permute-done.3.next_z), channel_id=1, source_target_pairs={{0,1},{1,0},{2,3},{3,2},{4,5},{5,4},{6,7},{7,6},{8,9},{9,8},{10,11... | collective-permute-start | bytes 1671176 | tf_op jit(solution)/shard_map/ppermute | solution.py:301
  68.9 0.7 copy-start.1
  69.6 19.9 %all-to-all-start.1 = ((f32[16,40,128]{2,1,0:T(8,128)}), f32[16,40,128]{2,1,0:T(8,128)S(1)}, u32[]{:S(2)}, u32[]{:S(2)}) async-start(f32[16,40,128]{2,1,0:T(8,128)} %copy-done.1), calls=%async_computation.1 | async-start | bytes 655360 | tf_op jit(solution)/shard_map/all_to_all | solution.py:310
  76.0 3.1 %collective-permute-start.5 = (f32[8,128]{1,0:T(8,128)S(1)}, f32[8,128]{1,0:T(8,128)S(1)}, u32[]{:S(2)}, u32[]{:S(2)}) collective-permute-start(f32[8,128]{1,0:T(8,128)S(1)} %get-tuple-element.23), channel_id=1, source_target_pairs={{0,1},{1,0},{2,3},{3,2},{4,5},{5,4},{6,7},{7,6},{8,9},{9,8},{10,11... | collective-permute-start | bytes 12296 | tf_op jit(solution)/shard_map/ppermute | solution.py:311
  110.3 13.6 %copy-start.5 = (f32[1,32,512]{2,1,0:T(8,128)S(1)}, f32[1,32,512]{2,1,0:T(8,128)}, u32[]{:S(2)}) copy-start(f32[1,32,512]{2,1,0:T(8,128)} %pivot.1) | copy-start | bytes 196612

commit v5 on v4

--- a/solution.py
+++ b/solution.py
@@ -139,7 +139,7 @@
     )(spread, cross_own, cross_other, prev_panel)
 
 
-def product_kernel(got, mine, mine_b, next_z, next_zb, out, cross_keep, cross_give, stride, prev_rows):
+def product_kernel(got, mine, mine_b, next_z, next_zb, out, cross_pair, stride, prev_rows):
     row = lax.axis_index("prow")
     core = lax.axis_index("pcol") % 2
     half = row % 2
@@ -155,9 +155,7 @@
     sums = -jnp.sum(got[:, 32:40, :], 0)
     pad = jnp.zeros((4, 128), jnp.float32)
     cross = jnp.concatenate([sums[4:8], pad], 0)
-    swapped = jnp.concatenate([sums[6:8], sums[4:6], pad], 0)
-    cross_keep[...] = jnp.where(core == 0, cross, swapped)
-    cross_give[...] = jnp.where(core == 0, swapped, cross)
+    cross_pair[...] = cross
     for left, right, which in ((mine, mine_b, half), (next_z, next_zb, 1 - half)):
         top = jnp.concatenate([left[256:, :256], left[256:, 256:], right[256:, :256], right[256:, 256:]], 0)
         part = dot(left[:256, :], own) + dot(right[:256, :], other) + dot(top.T, prev)
@@ -174,22 +172,20 @@
         out_shape=(
             jax.ShapeDtypeStruct((16, 40, 128), jnp.float32),
             jax.ShapeDtypeStruct((8, 128), jnp.float32),
-            jax.ShapeDtypeStruct((8, 128), jnp.float32),
             jax.ShapeDtypeStruct((64, 128), jnp.float32),
         ),
         in_specs=[pl.BlockSpec(memory_space=pltpu.VMEM)] * 5,
-        out_specs=(pl.BlockSpec(memory_space=pltpu.VMEM),) * 4,
+        out_specs=(pl.BlockSpec(memory_space=pltpu.VMEM),) * 3,
         scratch_shapes=[pltpu.VMEM((64, 128), jnp.float32)],
         compiler_params=kernel_params,
         name="column_product",
     )(got, mine, mine_b, next_z, next_zb)
 
 
-def diag_kernel(slots, panel, got, cross_keep, cross_got, stride, fresh_out, out, columns):
+def diag_kernel(slots, panel, got, cross_pair, stride, fresh_out, out, columns):
     row = lax.axis_index("prow")
     half = row % 2
     y = lax.axis_index("pcol") // 2
-    core = lax.axis_index("pcol") % 2
     fresh = []
     for h in range(2):
         total = got[h, :32, :]
@@ -213,40 +209,37 @@
         picked = columns[2 + h, pl.ds(pl.multiple_of(16 * y, 16), 16), :]
         own.append(dot(picked[:, :16], rows))
     part = part + jnp.concatenate(own, 0)
-    lane = lax.broadcasted_iota(jnp.int32, (128, 512), 0)
-    spot = (lax.broadcasted_iota(jnp.int32, (128, 512), 1) == 64 * (lane // 16) + lane % 16).astype(jnp.float32)
-    placed = dot(jnp.concatenate([cross_keep[:2, :], cross_got[:2, :], jnp.zeros((4, 128), jnp.float32)], 0), spot)
-    ours = placed[0:1] + pltpu.roll(placed[1:2], 16, 1)
-    theirs = placed[2:3] + pltpu.roll(placed[3:4], 16, 1)
-    line = jnp.where(core == 0, ours + pltpu.roll(theirs, 32, 1), theirs + pltpu.roll(ours, 32, 1))
-    line = jnp.concatenate([line[:, 128 * k : 128 * k + 128] for k in range(4)], 0)
     for k in range(ROWS):
         for lane in range(4):
             out[k, lane : lane + 1, :] = part[k : k + 1, 128 * lane : 128 * lane + 128]
-        out[k, 4:8, :] = line
-
-
-def diag_operand(slot_blocks, panel_blocks, got, cross_keep, cross_got, stride):
+        out[k, 4:8, :] = cross_pair[:4, :]
+
+
+def diag_operand(slot_blocks, panel_blocks, got, cross_pair, stride):
     return pl.pallas_call(
         diag_kernel,
         out_shape=(
             jax.ShapeDtypeStruct((1, 32, 256), jnp.float32),
             jax.ShapeDtypeStruct((ROWS, 8, 128), jnp.float32),
         ),
-        in_specs=[pl.BlockSpec(memory_space=pltpu.SMEM)] + [pl.BlockSpec(memory_space=pltpu.VMEM)] * 5,
+        in_specs=[pl.BlockSpec(memory_space=pltpu.SMEM)] + [pl.BlockSpec(memory_space=pltpu.VMEM)] * 4,
         out_specs=(pl.BlockSpec(memory_space=pltpu.VMEM),) * 2,
         scratch_shapes=[pltpu.VMEM((4, 128, 128), jnp.float32)],
         compiler_params=kernel_params,
         name="diag_operand",
-    )(slot_blocks, panel_blocks, got, cross_keep, cross_got, stride)
-
-
-def total_kernel(got, out, cross_out):
+    )(slot_blocks, panel_blocks, got, cross_pair, stride)
+
+
+def total_kernel(got, out, keep, give):
+    core = lax.axis_index("pcol") % 2
     total = jnp.sum(got[:, :4, :], 0)
     for k in range(ROWS):
         out[k] = total
-        for lane in range(4):
-            cross_out[0, k : k + 1, 128 * lane : 128 * lane + 128] = got[k, 4 + lane : 5 + lane, :]
+        for lane in range(2):
+            span = slice(128 * lane, 128 * lane + 128)
+            first, second = got[k, 4 + lane : 5 + lane, :], got[k, 6 + lane : 7 + lane, :]
+            keep[k : k + 1, span] = jnp.where(core == 0, first, second)
+            give[k : k + 1, span] = jnp.where(core == 0, second, first)
 
 
 def total_operand(got):
@@ -254,13 +247,36 @@
         total_kernel,
         out_shape=(
             jax.ShapeDtypeStruct((ROWS, 4, 128), jnp.float32),
-            jax.ShapeDtypeStruct((1, 32, 512), jnp.float32),
+            jax.ShapeDtypeStruct((32, 256), jnp.float32),
+            jax.ShapeDtypeStruct((32, 256), jnp.float32),
         ),
         in_specs=[pl.BlockSpec(memory_space=pltpu.VMEM)],
-        out_specs=(pl.BlockSpec(memory_space=pltpu.VMEM),) * 2,
+        out_specs=(pl.BlockSpec(memory_space=pltpu.VMEM),) * 3,
         compiler_params=kernel_params,
         name="total_operand",
     )(got)
+
+
+def place_columns(core):
+    n = lax.broadcasted_iota(jnp.int32, (256, 512), 0)
+    target = lax.broadcasted_iota(jnp.int32, (256, 512), 1)
+    return (target == 64 * ((n % 128) // 16) + 32 * core + 16 * (n // 128) + n % 16).astype(jnp.float32)
+
+
+def line_kernel(keep, taken, out):
+    core = lax.axis_index("pcol") % 2
+    out[0] = dot(keep[...], place_columns(core)) + dot(taken[...], place_columns(1 - core))
+
+
+def cross_lines(keep, taken):
+    return pl.pallas_call(
+        line_kernel,
+        out_shape=jax.ShapeDtypeStruct((1, 32, 512), jnp.float32),
+        in_specs=[pl.BlockSpec(memory_space=pltpu.VMEM)] * 2,
+        out_specs=pl.BlockSpec(memory_space=pltpu.VMEM),
+        compiler_params=kernel_params,
+        name="cross_lines",
+    )(keep, taken)
 
 
 def last_kernel(got, pivot, out):
@@ -300,7 +316,7 @@
     got = lax.all_to_all(send, "prow", 0, 0, tiled=True)
     blocks_zb = lax.ppermute(blocks_z, "pcol", core_swap)
 
-    send, cross_keep, cross_give, stride = column_product(got, blocks, blocks_b, blocks_z, blocks_zb)
+    send, cross_pair, stride = column_product(got, blocks, blocks_b, blocks_z, blocks_zb)
     groups = [
         [(x * 8 + 2 * z + h) * COLS + 2 * i + k for i in range(YS) for h in range(2)]
         for x in range(4)
@@ -308,11 +324,12 @@
         for k in range(2)
     ]
     got = lax.all_to_all(send, ("prow", "pcol"), 0, 0, tiled=True, axis_index_groups=groups)
-    cross_got = lax.ppermute(cross_give, "pcol", core_swap)
-    fresh, send = diag_operand(slot_blocks, panel_blocks, got, cross_keep, cross_got, stride)
+    fresh, send = diag_operand(slot_blocks, panel_blocks, got, cross_pair, stride)
     got = lax.all_to_all(send, "prow", 0, 0, tiled=True)
-    total, cross_out = total_operand(got)
+    total, keep, give = total_operand(got)
     got = lax.all_to_all(total, "prow", 0, 0, tiled=True)
+    taken = lax.ppermute(give, "pcol", core_swap)
+    cross_out = cross_lines(keep, taken)
     return fresh, cross_out, last_step(got, pivot_inverse)
 
 

time: 125 us -> 125 us (level)
  blocking collectives: 32.3 us -> 38.4 us
  waiting for transfers between devices: 37 us -> 31 us
  starting transfers between devices: 43.2 us -> 41.7 us
  Pallas kernels: 9.72 us -> 11.1 us
    all_to_all x1, blocking collectives: 13.6 us -> 19.7 us  [step(): lax.all_to_all(send, ('prow', 'pcol'), 0, 0, tiled=True, axis_index_group...]
    all_to_all x1, waiting for transfers between devices: 10.4 us -> 4.36 us  [step(): got = lax.all_to_all(total, 'prow', 0, 0, tiled=True)]
    pallas_call x0 -> x1, Pallas kernels: none -> 1.44 us  [cross_lines(): pl.pallas_call(line_kernel, out_shape=jax.ShapeDtypeStruct((1, 32, 512),...]
    all_to_all x1, starting transfers between devices: 6.4 us -> 4.96 us  [step(): got = lax.all_to_all(total, 'prow', 0, 0, tiled=True)]
  transfers between devices with their start and end apart: 8 -> 8, of which waited for: 5 -> 5; matrix products, arithmetic and copies ran while one was open for 0% -> 0% of each run, Pallas kernels for 1% -> 3%
where the time goes in v5:
time: 125 us; the launch traced here: 124 us
  starting transfers between devices  41.7 us (33%)
  blocking collectives  38.4 us (31%)
  waiting for transfers between devices  31 us (25%)
  Pallas kernels  11.1 us (9%)
    ppermute x1, waiting for transfers between devices, step(): blocks_z = lax.ppermute(blocks, 'prow', row_swap)  22.3 us
    all_to_all x1, blocking collectives, step(): lax.all_to_all(send, ('prow', 'pcol'), 0, 0, tiled=True, axis_index_group...  19.7 us
    all_to_all x1, blocking collectives, step(): got = lax.all_to_all(send, 'prow', 0, 0, tiled=True)  18.7 us
    all_to_all x1, starting transfers between devices, step(): got = lax.all_to_all(send, 'prow', 0, 0, tiled=True)  17.7 us
    ppermute x1, starting transfers between devices, step(): spread = lax.ppermute(sent, ('prow', 'pcol'), spread_pairs())  8.09 us
    all_to_all x1, starting transfers between devices, step(): got = lax.all_to_all(total, 'prow', 0, 0, tiled=True)  4.96 us
    all_to_all x1, waiting for transfers between devices, step(): got = lax.all_to_all(total, 'prow', 0, 0, tiled=True)  4.36 us
    ppermute x1, starting transfers between devices, step(): blocks_z = lax.ppermute(blocks, 'prow', row_swap)  3.37 us
  transfers between devices with their start and end apart: 8, of which 5 were waited for; matrix products, arithmetic and copies ran while one was open for 0% of the time, Pallas kernels for 3%

profile of v5, /device:TPU:2, one launch (start us, length us, event | category | flops | bytes accessed | tf_op | source)
XLA Modules:
  0.0 124.0 jit_solution(414373885226649976)
XLA Ops:
  0.6 0.0 copy-start.5
  0.6 0.0 copy-start.1
  0.7 0.0 copy-start
  0.7 0.0 copy-start.2
  0.7 2.0 %own_piece.1 = f32[40,256]{1,0:T(8,128)} custom-call(s32[1,64]{1,0:T(1,128)} %slots.5, f32[1,256,512]{2,1,0:T(8,128)} %panel.5, f32[1,16,512]{2,1,0:T(8,128)} %prev.5), custom_call_target="tpu_custom_call" | custom-call | tf_op jit(solution)/shard_map/own_piece/pallas_call | solution.py:63
  2.7 8.1 %collective-permute-start = (f32[40,256]{1,0:T(8,128)}, f32[40,256]{1,0:T(8,128)S(1)}, u32[]{:S(2)}, u32[]{:S(2)}) collective-permute-start(f32[40,256]{1,0:T(8,128)} %own_piece.1), channel_id=1, source_target_pairs={{0,64},{1,65},{2,80},{3,81},{4,96},{5,97},{6,112},{7,113},{8,0},{9... | collective-permute-start | bytes 122888 | tf_op jit(solution)/shard_map/ppermute | solution.py:306
  10.8 0.0 copy-done.5
  10.8 0.0 copy-done.1
  10.8 0.0 copy-done
  10.8 0.0 copy-done.2
  10.9 0.0 copy-start.3
  10.9 0.8 copy-done.3
  11.7 1.7 %cross_rows.1 = (f32[32,256]{1,0:T(8,128)S(1)}, f32[32,256]{1,0:T(8,128)S(1)}) custom-call(s32[1,64]{1,0:T(1,128)S(1)} %copy-done.5, f32[1,256,512]{2,1,0:T(8,128)S(1)} %copy-done, f32[32,256]{1,0:T(8,128)S(1)} %copy-done.2, f32[32,512]{1,0:T(8,128)S(1)} %copy-done.3, f32[1,16,512]{2,1,0:T(8,128)S(1)} %copy-done.1), custom_call_target="tpu_custom_call" | custom-call | tf_op jit(solution)/shard_map/cross_rows/pallas_call | solution.py:97
  13.4 1.9 %collective-permute-start.1 = (f32[32,256]{1,0:T(8,128)S(1)}, f32[32,256]{1,0:T(8,128)S(1)}, u32[]{:S(2)}, u32[]{:S(2)}) collective-permute-start(f32[32,256]{1,0:T(8,128)S(1)} %get-tuple-element.20), channel_id=1, source_target_pairs={{0,1},{1,0},{2,3},{3,2},{4,5},{5,4},{6,7},{7,6},{8,9},{9,8},{10,11... | collective-permute-start | bytes 98312 | tf_op jit(solution)/shard_map/ppermute | solution.py:313
  15.3 1.2 collective-permute-done.1.cross_other
  16.5 0.0 collective-permute-done.spread
  16.5 0.9 gather_operand.1
  17.4 0.0 copy-start.6
  17.4 17.7 %all-to-all-start = ((f32[32,40,128]{2,1,0:T(8,128)}), f32[32,40,128]{2,1,0:T(8,128)S(1)}, u32[]{:S(2)}, u32[]{:S(2)}) async-start(f32[32,40,128]{2,1,0:T(8,128)} %gather_operand.1), calls=%async_computation | async-start | bytes 1310720 | tf_op jit(solution)/shard_map/all_to_all | solution.py:316
  35.1 0.0 copy-done.6
  35.2 3.4 %collective-permute-start.3 = (f32[272,512]{1,0:T(8,128)S(1)}, f32[272,512]{1,0:T(8,128)S(1)}, u32[]{:S(2)}, u32[]{:S(2)}) collective-permute-start(f32[272,512]{1,0:T(8,128)S(1)} %maximum_maximum_fusion.mine), channel_id=1, source_target_pairs={{0,16},{16,0},{32,48},{48,32},{64,80},{80,64},{96,112},{112,96},{1... | collective-permute-start | bytes 1671176 | tf_op jit(solution)/shard_map/ppermute | solution.py:309
  38.6 1.9 %collective-permute-start.2 = (f32[272,512]{1,0:T(8,128)S(1)}, f32[272,512]{1,0:T(8,128)S(1)}, u32[]{:S(2)}, u32[]{:S(2)}) collective-permute-start(f32[272,512]{1,0:T(8,128)S(1)} %maximum_maximum_fusion.mine), channel_id=1, source_target_pairs={{0,1},{1,0},{2,3},{3,2},{4,5},{5,4},{6,7},{7,6},{8,9},{9,8},{10,11... | collective-permute-start | bytes 1671176 | tf_op jit(solution)/shard_map/ppermute | solution.py:310
  40.5 22.3 %collective-permute-done.3.next_z = f32[272,512]{1,0:T(8,128)S(1)} collective-permute-done((f32[272,512]{1,0:T(8,128)S(1)}, f32[272,512]{1,0:T(8,128)S(1)}, u32[]{:S(2)}, u32[]{:S(2)}) %collective-permute-start.3) | collective-permute-done | bytes 557088 | tf_op jit(solution)/shard_map/ppermute | solution.py:309
  62.8 1.9 %collective-permute-start.4 = (f32[272,512]{1,0:T(8,128)S(1)}, f32[272,512]{1,0:T(8,128)S(1)}, u32[]{:S(2)}, u32[]{:S(2)}) collective-permute-start(f32[272,512]{1,0:T(8,128)S(1)} %collective-permute-done.3.next_z), channel_id=1, source_target_pairs={{0,1},{1,0},{2,3},{3,2},{4,5},{5,4},{6,7},{7,6},{8,9},{9,8},{10,11... | collective-permute-start | bytes 1671176 | tf_op jit(solution)/shard_map/ppermute | solution.py:317
  64.7 0.0 collective-permute-done.2.mine_b
  64.7 1.9 %collective-permute-done.4.next_zb = f32[272,512]{1,0:T(8,128)S(1)} collective-permute-done((f32[272,512]{1,0:T(8,128)S(1)}, f32[272,512]{1,0:T(8,128)S(1)}, u32[]{:S(2)}, u32[]{:S(2)}) %collective-permute-start.4) | collective-permute-done | bytes 557088 | tf_op jit(solution)/shard_map/ppermute | solution.py:317
  66.7 0.0 all-to-all-done.got
  66.7 2.2 %column_product.1 = (f32[16,40,128]{2,1,0:T(8,128)S(1)}, f32[8,128]{1,0:T(8,128)S(1)}, f32[64,128]{1,0:T(8,128)S(1)}) custom-call(f32[32,40,128]{2,1,0:T(8,128)S(1)} %all-to-all-done.got, f32[272,512]{1,0:T(8,128)S(1)} %maximum_maximum_fusion.mine, f32[272,512]{1,0:T(8,128)S(1)} %collective-permute-done.2.mine_b, ...), custom_call_target="tpu_custom_call" | custom-call | tf_op jit(solution)/shard_map/column_product/pallas_call | solution.py:170
  68.8 19.7 %all_to_all.20.got = f32[16,40,128]{2,1,0:T(8,128)S(1)} all-to-all(f32[16,40,128]{2,1,0:T(8,128)S(1)} %get-tuple-element.21), channel_id=1, replica_groups={{0,16,2,18,4,20,6,22,8,24,10,26,12,28,14,30},{1,17,3,19,5,21,7,23,9,25,..., dimensions={0} | all-to-all | bytes 655360 | tf_op jit(solution)/shard_map/all_to_all | solution.py:326
  88.5 1.5 %diag_operand.1 = (f32[1,32,256]{2,1,0:T(8,128)}, f32[32,8,128]{2,1,0:T(8,128)S(1)}) custom-call(s32[1,64]{1,0:T(1,128)S(1)} %copy-done.5, f32[1,256,512]{2,1,0:T(8,128)S(1)} %copy-done, f32[16,40,128]{2,1,0:T(8,128)S(1)} %all_to_all.20.got, f32[8,128]{1,0:T(8,128)S(1)} %get-tuple-element.22.cross_pair, f32[64,128]{1,0:T(8,128)S(1)} %get-tuple-element.23.stride), custom_call_target="tpu_custom_call" | custom-call | tf_op jit(solution)/shard_map/diag_operand/pallas_call | solution.py:219
  90.0 18.7 %all_to_all.21.got = f32[32,8,128]{2,1,0:T(8,128)S(1)} all-to-all(f32[32,8,128]{2,1,0:T(8,128)S(1)} %get-tuple-element.25), channel_id=1, replica_groups=mesh['prow'=32,'pcol'=16] {'prow'}, dimensions={0} | all-to-all | bytes 262144 | tf_op jit(solution)/shard_map/all_to_all | solution.py:328
  108.7 0.7 total_operand.1
  109.4 5.0 %all-to-all-start.3 = ((f32[32,4,128]{2,1,0:T(4,128)}), f32[32,4,128]{2,1,0:T(4,128)S(1)}, u32[]{:S(2)}, u32[]{:S(2)}) async-start(f32[32,4,128]{2,1,0:T(4,128)} %get-tuple-element.28), calls=%async_computation.3 | async-start | bytes 131072 | tf_op jit(solution)/shard_map/all_to_all | solution.py:330
  114.4 1.9 %collective-permute-start.5 = (f32[32,256]{1,0:T(8,128)S(1)}, f32[32,256]{1,0:T(8,128)S(1)}, u32[]{:S(2)}, u32[]{:S(2)}) collective-permute-start(f32[32,256]{1,0:T(8,128)S(1)} %get-tuple-element.27), channel_id=1, source_target_pairs={{0,1},{1,0},{2,3},{3,2},{4,5},{5,4},{6,7},{7,6},{8,9},{9,8},{10,11... | collective-permute-start | bytes 98312 | tf_op jit(solution)/shard_map/ppermute | solution.py:331
  116.3 1.2 collective-permute-done.5.taken
  117.5 0.0 copy-start.4
  117.5 1.4 %cross_lines.1 = f32[1,32,512]{2,1,0:T(8,128)} custom-call(f32[32,256]{1,0:T(8,128)S(1)} %get-tuple-element.26.keep, f32[32,256]{1,0:T(8,128)S(1)} %collective-permute-done.5.taken), custom_call_target="tpu_custom_call" | custom-call | tf_op jit(solution)/shard_map/cross_lines/pallas_call | solution.py:272
  118.9 4.4 %all-to-all-done.3.got = f32[32,4,128]{2,1,0:T(4,128)S(1)} async-done(((f32[32,4,128]{2,1,0:T(4,128)}), f32[32,4,128]{2,1,0:T(4,128)S(1)}, u32[]{:S(2)}, u32[]{:S(2)}) %all-to-all-start.3) | async-done | bytes 65568 | tf_op jit(solution)/shard_map/all_to_all | solution.py:330
  123.3 0.0 copy-done.4
  123.3 0.7 last_step.1
  (2 shorter events, 0.0 us)
Async XLA Ops:
  0.6 10.2 %copy-start.5 = (s32[1,64]{1,0:T(1,128)S(1)}, s32[1,64]{1,0:T(1,128)}, u32[]{:S(2)}) copy-start(s32[1,64]{1,0:T(1,128)} %slots.5) | copy-start | bytes 772
  0.6 10.2 %copy-start.1 = (f32[1,16,512]{2,1,0:T(8,128)S(1)}, f32[1,16,512]{2,1,0:T(8,128)}, u32[]{:S(2)}) copy-start(f32[1,16,512]{2,1,0:T(8,128)} %prev.5) | copy-start | bytes 98308
  0.7 10.2 %copy-start = (f32[1,256,512]{2,1,0:T(8,128)S(1)}, f32[1,256,512]{2,1,0:T(8,128)}, u32[]{:S(2)}) copy-start(f32[1,256,512]{2,1,0:T(8,128)} %panel.5) | copy-start | bytes 1572868
  0.7 10.2 %copy-start.2 = (f32[32,256]{1,0:T(8,128)S(1)}, f32[32,256]{1,0:T(8,128)}, u32[]{:S(2)}) copy-start(f32[32,256]{1,0:T(8,128)} %top_column) | copy-start | bytes 98308
  2.7 13.8 %collective-permute-start = (f32[40,256]{1,0:T(8,128)}, f32[40,256]{1,0:T(8,128)S(1)}, u32[]{:S(2)}, u32[]{:S(2)}) collective-permute-start(f32[40,256]{1,0:T(8,128)} %own_piece.1), channel_id=1, source_target_pairs={{0,64},{1,65},{2,80},{3,81},{4,96},{5,97},{6,112},{7,113},{8,0},{9... | collective-permute-start | bytes 122888 | tf_op jit(solution)/shard_map/ppermute | solution.py:306
  10.9 0.8 copy-start.3
  13.4 3.1 %collective-permute-start.1 = (f32[32,256]{1,0:T(8,128)S(1)}, f32[32,256]{1,0:T(8,128)S(1)}, u32[]{:S(2)}, u32[]{:S(2)}) collective-permute-start(f32[32,256]{1,0:T(8,128)S(1)} %get-tuple-element.20), channel_id=1, source_target_pairs={{0,1},{1,0},{2,3},{3,2},{4,5},{5,4},{6,7},{7,6},{8,9},{9,8},{10,11... | collective-permute-start | bytes 98312 | tf_op jit(solution)/shard_map/ppermute | solution.py:313
  17.4 17.7 %copy-start.6 = (f32[256,512]{1,0:T(8,128)S(1)}, f32[256,512]{1,0:T(8,128)}, u32[]{:S(2)}) copy-start(f32[256,512]{1,0:T(8,128)} %param.7) | copy-start | bytes 1572868
  17.4 49.2 %all-to-all-start = ((f32[32,40,128]{2,1,0:T(8,128)}), f32[32,40,128]{2,1,0:T(8,128)S(1)}, u32[]{:S(2)}, u32[]{:S(2)}) async-start(f32[32,40,128]{2,1,0:T(8,128)} %gather_operand.1), calls=%async_computation | async-start | bytes 1310720 | tf_op jit(solution)/shard_map/all_to_all | solution.py:316
  35.2 27.6 %collective-permute-start.3 = (f32[272,512]{1,0:T(8,128)S(1)}, f32[272,512]{1,0:T(8,128)S(1)}, u32[]{:S(2)}, u32[]{:S(2)}) collective-permute-start(f32[272,512]{1,0:T(8,128)S(1)} %maximum_maximum_fusion.mine), channel_id=1, source_target_pairs={{0,16},{16,0},{32,48},{48,32},{64,80},{80,64},{96,112},{112,96},{1... | collective-permute-start | bytes 1671176 | tf_op jit(solution)/shard_map/ppermute | solution.py:309
  38.6 26.2 %collective-permute-start.2 = (f32[272,512]{1,0:T(8,128)S(1)}, f32[272,512]{1,0:T(8,128)S(1)}, u32[]{:S(2)}, u32[]{:S(2)}) collective-permute-start(f32[272,512]{1,0:T(8,128)S(1)} %maximum_maximum_fusion.mine), channel_id=1, source_target_pairs={{0,1},{1,0},{2,3},{3,2},{4,5},{5,4},{6,7},{7,6},{8,9},{9,8},{10,11... | collective-permute-start | bytes 1671176 | tf_op jit(solution)/shard_map/ppermute | solution.py:310
  62.8 3.8 %collective-permute-start.4 = (f32[272,512]{1,0:T(8,128)S(1)}, f32[272,512]{1,0:T(8,128)S(1)}, u32[]{:S(2)}, u32[]{:S(2)}) collective-permute-start(f32[272,512]{1,0:T(8,128)S(1)} %collective-permute-done.3.next_z), channel_id=1, source_target_pairs={{0,1},{1,0},{2,3},{3,2},{4,5},{5,4},{6,7},{7,6},{8,9},{9,8},{10,11... | collective-permute-start | bytes 1671176 | tf_op jit(solution)/shard_map/ppermute | solution.py:317
  109.4 13.9 %all-to-all-start.3 = ((f32[32,4,128]{2,1,0:T(4,128)}), f32[32,4,128]{2,1,0:T(4,128)S(1)}, u32[]{:S(2)}, u32[]{:S(2)}) async-start(f32[32,4,128]{2,1,0:T(4,128)} %get-tuple-element.28), calls=%async_computation.3 | async-start | bytes 131072 | tf_op jit(solution)/shard_map/all_to_all | solution.py:330
  114.4 3.1 %collective-permute-start.5 = (f32[32,256]{1,0:T(8,128)S(1)}, f32[32,256]{1,0:T(8,128)S(1)}, u32[]{:S(2)}, u32[]{:S(2)}) collective-permute-start(f32[32,256]{1,0:T(8,128)S(1)} %get-tuple-element.27), channel_id=1, source_target_pairs={{0,1},{1,0},{2,3},{3,2},{4,5},{5,4},{6,7},{7,6},{8,9},{9,8},{10,11... | collective-permute-start | bytes 98312 | tf_op jit(solution)/shard_map/ppermute | solution.py:331
  117.5 5.8 %copy-start.4 = (f32[1,32,512]{2,1,0:T(8,128)S(1)}, f32[1,32,512]{2,1,0:T(8,128)}, u32[]{:S(2)}) copy-start(f32[1,32,512]{2,1,0:T(8,128)} %pivot.1) | copy-start | bytes 196612

commit v6 on v5

--- a/solution.py
+++ b/solution.py
@@ -89,8 +89,10 @@
     low, high = factor_halves(slots, panel, row)
     diag = pltpu.roll(top_diag[...], (512 - 16 * row) % 512, 1)[:, :16]
     part = dot(top_column[:, :BLK], low) + dot(top_column[:, BLK:], high) + dot(diag, prev[0])
-    mine[...] = dot(part, select_columns(core))
-    others[...] = dot(part, select_columns(1 - core))
+    shifted = jnp.where(core == 0, pltpu.roll(part, 480, 1), pltpu.roll(part, 32, 1))
+    both = dot(jnp.concatenate([part, shifted], 0), select_columns(core))
+    mine[...] = both[:32]
+    others[...] = both[32:]
 
 
 def cross_rows(slot_blocks, panel_blocks, top_column, top_diag, prev_panel):
@@ -302,7 +304,7 @@
     row_swap = [(i, i ^ 1) for i in range(ROWS)]
 
     sent = own_piece(slot_blocks, panel_blocks, prev_panel)
-    sent, top_column, top_diag = lax.optimization_barrier((sent, top_column, top_diag))
+    sent, top_column = lax.optimization_barrier((sent, top_column))
     spread = lax.ppermute(sent, ("prow", "pcol"), spread_pairs())
 
     blocks = jnp.concatenate([pool_inverse, jnp.concatenate([top_column[:16], top_column[16:]], 1)], 0)

time: 125 us -> 125 us (level)
  transfers between devices with their start and end apart: 8 -> 8, of which waited for: 5 -> 5; matrix products, arithmetic and copies ran while one was open for 0% -> 0% of each run, Pallas kernels for 3% -> 2%
where the time goes in v6:
time: 125 us; the launch traced here: 124 us
  starting transfers between devices  42 us (34%)
  blocking collectives  38.4 us (31%)
  waiting for transfers between devices  31 us (25%)
  Pallas kernels  10.9 us (9%)
    ppermute x1, waiting for transfers between devices, step(): blocks_z = lax.ppermute(blocks, 'prow', row_swap)  22.3 us
    all_to_all x1, blocking collectives, step(): lax.all_to_all(send, ('prow', 'pcol'), 0, 0, tiled=True, axis_index_group...  19.7 us
    all_to_all x1, blocking collectives, step(): got = lax.all_to_all(send, 'prow', 0, 0, tiled=True)  18.7 us
    all_to_all x1, starting transfers between devices, step(): got = lax.all_to_all(send, 'prow', 0, 0, tiled=True)  17.9 us
    ppermute x1, starting transfers between devices, step(): spread = lax.ppermute(sent, ('prow', 'pcol'), spread_pairs())  8.09 us
    all_to_all x1, starting transfers between devices, step(): got = lax.all_to_all(total, 'prow', 0, 0, tiled=True)  4.96 us
    all_to_all x1, waiting for transfers between devices, step(): got = lax.all_to_all(total, 'prow', 0, 0, tiled=True)  4.36 us
    ppermute x1, starting transfers between devices, step(): blocks_z = lax.ppermute(blocks, 'prow', row_swap)  3.37 us
  transfers between devices with their start and end apart: 8, of which 5 were waited for; matrix products, arithmetic and copies ran while one was open for 0% of the time, Pallas kernels for 2%

profile of v6, /device:TPU:2, one launch (start us, length us, event | category | flops | bytes accessed | tf_op | source)
XLA Modules:
  0.0 124.0 jit_solution(9923181304919506137)
XLA Ops:
  0.6 0.0 copy-start.5
  0.6 0.0 copy-start.1
  0.7 0.0 copy-start
  0.7 0.0 copy-start.2
  0.7 2.0 %own_piece.1 = f32[40,256]{1,0:T(8,128)} custom-call(s32[1,64]{1,0:T(1,128)} %slots.5, f32[1,256,512]{2,1,0:T(8,128)} %panel.5, f32[1,16,512]{2,1,0:T(8,128)} %prev.5), custom_call_target="tpu_custom_call" | custom-call | tf_op jit(solution)/shard_map/own_piece/pallas_call | solution.py:63
  2.7 8.1 %collective-permute-start = (f32[40,256]{1,0:T(8,128)}, f32[40,256]{1,0:T(8,128)S(1)}, u32[]{:S(2)}, u32[]{:S(2)}) collective-permute-start(f32[40,256]{1,0:T(8,128)} %own_piece.1), channel_id=1, source_target_pairs={{0,64},{1,65},{2,80},{3,81},{4,96},{5,97},{6,112},{7,113},{8,0},{9... | collective-permute-start | bytes 122888 | tf_op jit(solution)/shard_map/ppermute | solution.py:308
  10.8 0.0 copy-done.5
  10.8 0.0 copy-done.1
  10.8 0.0 copy-done
  10.8 0.0 copy-done.2
  10.9 0.0 copy-start.3
  10.9 0.8 copy-done.3
  11.7 1.4 %cross_rows.1 = (f32[32,256]{1,0:T(8,128)S(1)}, f32[32,256]{1,0:T(8,128)S(1)}) custom-call(s32[1,64]{1,0:T(1,128)S(1)} %copy-done.5, f32[1,256,512]{2,1,0:T(8,128)S(1)} %copy-done, f32[32,256]{1,0:T(8,128)S(1)} %copy-done.2, f32[32,512]{1,0:T(8,128)S(1)} %copy-done.3, f32[1,16,512]{2,1,0:T(8,128)S(1)} %copy-done.1), custom_call_target="tpu_custom_call" | custom-call | tf_op jit(solution)/shard_map/cross_rows/pallas_call | solution.py:99
  13.1 1.9 %collective-permute-start.1 = (f32[32,256]{1,0:T(8,128)S(1)}, f32[32,256]{1,0:T(8,128)S(1)}, u32[]{:S(2)}, u32[]{:S(2)}) collective-permute-start(f32[32,256]{1,0:T(8,128)S(1)} %get-tuple-element.18), channel_id=1, source_target_pairs={{0,1},{1,0},{2,3},{3,2},{4,5},{5,4},{6,7},{7,6},{8,9},{9,8},{10,11... | collective-permute-start | bytes 98312 | tf_op jit(solution)/shard_map/ppermute | solution.py:315
  15.0 1.2 collective-permute-done.1.cross_other
  16.2 0.0 collective-permute-done.spread
  16.2 0.9 gather_operand.1
  17.2 0.0 copy-start.6
  17.2 17.9 %all-to-all-start = ((f32[32,40,128]{2,1,0:T(8,128)}), f32[32,40,128]{2,1,0:T(8,128)S(1)}, u32[]{:S(2)}, u32[]{:S(2)}) async-start(f32[32,40,128]{2,1,0:T(8,128)} %gather_operand.1), calls=%async_computation | async-start | bytes 1310720 | tf_op jit(solution)/shard_map/all_to_all | solution.py:318
  35.1 0.0 copy-done.6
  35.2 3.4 %collective-permute-start.3 = (f32[272,512]{1,0:T(8,128)S(1)}, f32[272,512]{1,0:T(8,128)S(1)}, u32[]{:S(2)}, u32[]{:S(2)}) collective-permute-start(f32[272,512]{1,0:T(8,128)S(1)} %maximum_maximum_fusion.mine), channel_id=1, source_target_pairs={{0,16},{16,0},{32,48},{48,32},{64,80},{80,64},{96,112},{112,96},{1... | collective-permute-start | bytes 1671176 | tf_op jit(solution)/shard_map/ppermute | solution.py:311
  38.6 1.9 %collective-permute-start.2 = (f32[272,512]{1,0:T(8,128)S(1)}, f32[272,512]{1,0:T(8,128)S(1)}, u32[]{:S(2)}, u32[]{:S(2)}) collective-permute-start(f32[272,512]{1,0:T(8,128)S(1)} %maximum_maximum_fusion.mine), channel_id=1, source_target_pairs={{0,1},{1,0},{2,3},{3,2},{4,5},{5,4},{6,7},{7,6},{8,9},{9,8},{10,11... | collective-permute-start | bytes 1671176 | tf_op jit(solution)/shard_map/ppermute | solution.py:312
  40.5 22.3 %collective-permute-done.3.next_z = f32[272,512]{1,0:T(8,128)S(1)} collective-permute-done((f32[272,512]{1,0:T(8,128)S(1)}, f32[272,512]{1,0:T(8,128)S(1)}, u32[]{:S(2)}, u32[]{:S(2)}) %collective-permute-start.3) | collective-permute-done | bytes 557088 | tf_op jit(solution)/shard_map/ppermute | solution.py:311
  62.8 1.9 %collective-permute-start.4 = (f32[272,512]{1,0:T(8,128)S(1)}, f32[272,512]{1,0:T(8,128)S(1)}, u32[]{:S(2)}, u32[]{:S(2)}) collective-permute-start(f32[272,512]{1,0:T(8,128)S(1)} %collective-permute-done.3.next_z), channel_id=1, source_target_pairs={{0,1},{1,0},{2,3},{3,2},{4,5},{5,4},{6,7},{7,6},{8,9},{9,8},{10,11... | collective-permute-start | bytes 1671176 | tf_op jit(solution)/shard_map/ppermute | solution.py:319
  64.7 0.0 collective-permute-done.2.mine_b
  64.7 1.9 %collective-permute-done.4.next_zb = f32[272,512]{1,0:T(8,128)S(1)} collective-permute-done((f32[272,512]{1,0:T(8,128)S(1)}, f32[272,512]{1,0:T(8,128)S(1)}, u32[]{:S(2)}, u32[]{:S(2)}) %collective-permute-start.4) | collective-permute-done | bytes 557088 | tf_op jit(solution)/shard_map/ppermute | solution.py:319
  66.7 0.0 all-to-all-done.got
  66.7 2.2 %column_product.1 = (f32[16,40,128]{2,1,0:T(8,128)S(1)}, f32[8,128]{1,0:T(8,128)S(1)}, f32[64,128]{1,0:T(8,128)S(1)}) custom-call(f32[32,40,128]{2,1,0:T(8,128)S(1)} %all-to-all-done.got, f32[272,512]{1,0:T(8,128)S(1)} %maximum_maximum_fusion.mine, f32[272,512]{1,0:T(8,128)S(1)} %collective-permute-done.2.mine_b, ...), custom_call_target="tpu_custom_call" | custom-call | tf_op jit(solution)/shard_map/column_product/pallas_call | solution.py:172
  68.8 19.7 %all_to_all.20.got = f32[16,40,128]{2,1,0:T(8,128)S(1)} all-to-all(f32[16,40,128]{2,1,0:T(8,128)S(1)} %get-tuple-element.19), channel_id=1, replica_groups={{0,16,2,18,4,20,6,22,8,24,10,26,12,28,14,30},{1,17,3,19,5,21,7,23,9,25,..., dimensions={0} | all-to-all | bytes 655360 | tf_op jit(solution)/shard_map/all_to_all | solution.py:328
  88.5 1.5 %diag_operand.1 = (f32[1,32,256]{2,1,0:T(8,128)}, f32[32,8,128]{2,1,0:T(8,128)S(1)}) custom-call(s32[1,64]{1,0:T(1,128)S(1)} %copy-done.5, f32[1,256,512]{2,1,0:T(8,128)S(1)} %copy-done, f32[16,40,128]{2,1,0:T(8,128)S(1)} %all_to_all.20.got, f32[8,128]{1,0:T(8,128)S(1)} %get-tuple-element.20.cross_pair, f32[64,128]{1,0:T(8,128)S(1)} %get-tuple-element.21.stride), custom_call_target="tpu_custom_call" | custom-call | tf_op jit(solution)/shard_map/diag_operand/pallas_call | solution.py:221
  90.0 18.7 %all_to_all.21.got = f32[32,8,128]{2,1,0:T(8,128)S(1)} all-to-all(f32[32,8,128]{2,1,0:T(8,128)S(1)} %get-tuple-element.23), channel_id=1, replica_groups=mesh['prow'=32,'pcol'=16] {'prow'}, dimensions={0} | all-to-all | bytes 262144 | tf_op jit(solution)/shard_map/all_to_all | solution.py:330
  108.7 0.7 total_operand.1
  109.4 5.0 %all-to-all-start.3 = ((f32[32,4,128]{2,1,0:T(4,128)}), f32[32,4,128]{2,1,0:T(4,128)S(1)}, u32[]{:S(2)}, u32[]{:S(2)}) async-start(f32[32,4,128]{2,1,0:T(4,128)} %get-tuple-element.26), calls=%async_computation.3 | async-start | bytes 131072 | tf_op jit(solution)/shard_map/all_to_all | solution.py:332
  114.4 1.9 %collective-permute-start.5 = (f32[32,256]{1,0:T(8,128)S(1)}, f32[32,256]{1,0:T(8,128)S(1)}, u32[]{:S(2)}, u32[]{:S(2)}) collective-permute-start(f32[32,256]{1,0:T(8,128)S(1)} %get-tuple-element.25), channel_id=1, source_target_pairs={{0,1},{1,0},{2,3},{3,2},{4,5},{5,4},{6,7},{7,6},{8,9},{9,8},{10,11... | collective-permute-start | bytes 98312 | tf_op jit(solution)/shard_map/ppermute | solution.py:333
  116.3 1.2 collective-permute-done.5.taken
  117.5 0.0 copy-start.4
  117.5 1.4 %cross_lines.1 = f32[1,32,512]{2,1,0:T(8,128)} custom-call(f32[32,256]{1,0:T(8,128)S(1)} %get-tuple-element.24.keep, f32[32,256]{1,0:T(8,128)S(1)} %collective-permute-done.5.taken), custom_call_target="tpu_custom_call" | custom-call | tf_op jit(solution)/shard_map/cross_lines/pallas_call | solution.py:274
  118.9 4.4 %all-to-all-done.3.got = f32[32,4,128]{2,1,0:T(4,128)S(1)} async-done(((f32[32,4,128]{2,1,0:T(4,128)}), f32[32,4,128]{2,1,0:T(4,128)S(1)}, u32[]{:S(2)}, u32[]{:S(2)}) %all-to-all-start.3) | async-done | bytes 65568 | tf_op jit(solution)/shard_map/all_to_all | solution.py:332
  123.3 0.0 copy-done.4
  123.3 0.7 last_step.1
  (2 shorter events, 0.0 us)
Async XLA Ops:
  0.6 10.2 %copy-start.5 = (s32[1,64]{1,0:T(1,128)S(1)}, s32[1,64]{1,0:T(1,128)}, u32[]{:S(2)}) copy-start(s32[1,64]{1,0:T(1,128)} %slots.5) | copy-start | bytes 772
  0.6 10.2 %copy-start.1 = (f32[1,16,512]{2,1,0:T(8,128)S(1)}, f32[1,16,512]{2,1,0:T(8,128)}, u32[]{:S(2)}) copy-start(f32[1,16,512]{2,1,0:T(8,128)} %prev.5) | copy-start | bytes 98308
  0.7 10.2 %copy-start = (f32[1,256,512]{2,1,0:T(8,128)S(1)}, f32[1,256,512]{2,1,0:T(8,128)}, u32[]{:S(2)}) copy-start(f32[1,256,512]{2,1,0:T(8,128)} %panel.5) | copy-start | bytes 1572868
  0.7 10.2 %copy-start.2 = (f32[32,256]{1,0:T(8,128)S(1)}, f32[32,256]{1,0:T(8,128)}, u32[]{:S(2)}) copy-start(f32[32,256]{1,0:T(8,128)} %top_column) | copy-start | bytes 98308
  2.7 13.5 %collective-permute-start = (f32[40,256]{1,0:T(8,128)}, f32[40,256]{1,0:T(8,128)S(1)}, u32[]{:S(2)}, u32[]{:S(2)}) collective-permute-start(f32[40,256]{1,0:T(8,128)} %own_piece.1), channel_id=1, source_target_pairs={{0,64},{1,65},{2,80},{3,81},{4,96},{5,97},{6,112},{7,113},{8,0},{9... | collective-permute-start | bytes 122888 | tf_op jit(solution)/shard_map/ppermute | solution.py:308
  10.9 0.8 copy-start.3
  13.1 3.1 %collective-permute-start.1 = (f32[32,256]{1,0:T(8,128)S(1)}, f32[32,256]{1,0:T(8,128)S(1)}, u32[]{:S(2)}, u32[]{:S(2)}) collective-permute-start(f32[32,256]{1,0:T(8,128)S(1)} %get-tuple-element.18), channel_id=1, source_target_pairs={{0,1},{1,0},{2,3},{3,2},{4,5},{5,4},{6,7},{7,6},{8,9},{9,8},{10,11... | collective-permute-start | bytes 98312 | tf_op jit(solution)/shard_map/ppermute | solution.py:315
  17.2 18.0 %copy-start.6 = (f32[256,512]{1,0:T(8,128)S(1)}, f32[256,512]{1,0:T(8,128)}, u32[]{:S(2)}) copy-start(f32[256,512]{1,0:T(8,128)} %param.7) | copy-start | bytes 1572868
  17.2 49.5 %all-to-all-start = ((f32[32,40,128]{2,1,0:T(8,128)}), f32[32,40,128]{2,1,0:T(8,128)S(1)}, u32[]{:S(2)}, u32[]{:S(2)}) async-start(f32[32,40,128]{2,1,0:T(8,128)} %gather_operand.1), calls=%async_computation | async-start | bytes 1310720 | tf_op jit(solution)/shard_map/all_to_all | solution.py:318
  35.2 27.6 %collective-permute-start.3 = (f32[272,512]{1,0:T(8,128)S(1)}, f32[272,512]{1,0:T(8,128)S(1)}, u32[]{:S(2)}, u32[]{:S(2)}) collective-permute-start(f32[272,512]{1,0:T(8,128)S(1)} %maximum_maximum_fusion.mine), channel_id=1, source_target_pairs={{0,16},{16,0},{32,48},{48,32},{64,80},{80,64},{96,112},{112,96},{1... | collective-permute-start | bytes 1671176 | tf_op jit(solution)/shard_map/ppermute | solution.py:311
  38.6 26.2 %collective-permute-start.2 = (f32[272,512]{1,0:T(8,128)S(1)}, f32[272,512]{1,0:T(8,128)S(1)}, u32[]{:S(2)}, u32[]{:S(2)}) collective-permute-start(f32[272,512]{1,0:T(8,128)S(1)} %maximum_maximum_fusion.mine), channel_id=1, source_target_pairs={{0,1},{1,0},{2,3},{3,2},{4,5},{5,4},{6,7},{7,6},{8,9},{9,8},{10,11... | collective-permute-start | bytes 1671176 | tf_op jit(solution)/shard_map/ppermute | solution.py:312
  62.8 3.8 %collective-permute-start.4 = (f32[272,512]{1,0:T(8,128)S(1)}, f32[272,512]{1,0:T(8,128)S(1)}, u32[]{:S(2)}, u32[]{:S(2)}) collective-permute-start(f32[272,512]{1,0:T(8,128)S(1)} %collective-permute-done.3.next_z), channel_id=1, source_target_pairs={{0,1},{1,0},{2,3},{3,2},{4,5},{5,4},{6,7},{7,6},{8,9},{9,8},{10,11... | collective-permute-start | bytes 1671176 | tf_op jit(solution)/shard_map/ppermute | solution.py:319
  109.4 13.9 %all-to-all-start.3 = ((f32[32,4,128]{2,1,0:T(4,128)}), f32[32,4,128]{2,1,0:T(4,128)S(1)}, u32[]{:S(2)}, u32[]{:S(2)}) async-start(f32[32,4,128]{2,1,0:T(4,128)} %get-tuple-element.26), calls=%async_computation.3 | async-start | bytes 131072 | tf_op jit(solution)/shard_map/all_to_all | solution.py:332
  114.4 3.1 %collective-permute-start.5 = (f32[32,256]{1,0:T(8,128)S(1)}, f32[32,256]{1,0:T(8,128)S(1)}, u32[]{:S(2)}, u32[]{:S(2)}) collective-permute-start(f32[32,256]{1,0:T(8,128)S(1)} %get-tuple-element.25), channel_id=1, source_target_pairs={{0,1},{1,0},{2,3},{3,2},{4,5},{5,4},{6,7},{7,6},{8,9},{9,8},{10,11... | collective-permute-start | bytes 98312 | tf_op jit(solution)/shard_map/ppermute | solution.py:333
  117.5 5.8 %copy-start.4 = (f32[1,32,512]{2,1,0:T(8,128)S(1)}, f32[1,32,512]{2,1,0:T(8,128)}, u32[]{:S(2)}) copy-start(f32[1,32,512]{2,1,0:T(8,128)} %pivot.1) | copy-start | bytes 196612

commit v7 on v6

--- a/solution.py
+++ b/solution.py
@@ -13,6 +13,10 @@
 
 highest = lax.Precision.HIGHEST
 kernel_params = pltpu.CompilerParams(vmem_limit_bytes=16 << 20)
+
+
+def half_of(row):
+    return (row // 8) % 2
 
 
 def spread_pairs():
@@ -115,7 +119,8 @@
     mine, others = cross_own[...], cross_other[...]
     pair = [jnp.where(core == 0, mine, others), jnp.where(core == 0, others, mine)]
     for k in range(ROWS):
-        out[k, :36, :] = spread[:36, 128 * (k % 2) : 128 * (k % 2) + 128]
+        span = slice(128 * half_of(k), 128 * half_of(k) + 128)
+        out[k, :36, :] = spread[:36, span]
         for lane in range(2):
             for who in range(2):
                 at = 36 + 2 * who + lane
@@ -141,10 +146,10 @@
     )(spread, cross_own, cross_other, prev_panel)
 
 
-def product_kernel(got, mine, mine_b, next_z, next_zb, out, cross_pair, stride, prev_rows):
-    row = lax.axis_index("prow")
-    core = lax.axis_index("pcol") % 2
-    half = row % 2
+def product_kernel(got, mine, mine_b, next_x, next_xb, out, cross_pair, stride, prev_rows):
+    row = lax.axis_index("prow")
+    core = lax.axis_index("pcol") % 2
+    half = half_of(row)
     strided = row // 16
     for k in range(COLS):
         stride[4 * k : 4 * k + 4, :] = got[2 * k + strided, 32:36, :]
@@ -158,7 +163,7 @@
     pad = jnp.zeros((4, 128), jnp.float32)
     cross = jnp.concatenate([sums[4:8], pad], 0)
     cross_pair[...] = cross
-    for left, right, which in ((mine, mine_b, half), (next_z, next_zb, 1 - half)):
+    for left, right, which in ((mine, mine_b, half), (next_x, next_xb, 1 - half)):
         top = jnp.concatenate([left[256:, :256], left[256:, 256:], right[256:, :256], right[256:, 256:]], 0)
         part = dot(left[:256, :], own) + dot(right[:256, :], other) + dot(top.T, prev)
         part = part.T
@@ -168,7 +173,7 @@
             out[2 * y + which, 32:, :] = cross
 
 
-def column_product(got, mine, mine_b, next_z, next_zb):
+def column_product(got, mine, mine_b, next_x, next_xb):
     return pl.pallas_call(
         product_kernel,
         out_shape=(
@@ -181,12 +186,12 @@
         scratch_shapes=[pltpu.VMEM((64, 128), jnp.float32)],
         compiler_params=kernel_params,
         name="column_product",
-    )(got, mine, mine_b, next_z, next_zb)
+    )(got, mine, mine_b, next_x, next_xb)
 
 
 def diag_kernel(slots, panel, got, cross_pair, stride, fresh_out, out, columns):
     row = lax.axis_index("prow")
-    half = row % 2
+    half = half_of(row)
     y = lax.axis_index("pcol") // 2
     fresh = []
     for h in range(2):
@@ -301,14 +306,14 @@
 
 def step(pool_inverse, panel_blocks, prev_panel, pivot_inverse, top_column, top_diag, slot_blocks):
     core_swap = [(i, i ^ 1) for i in range(COLS)]
-    row_swap = [(i, i ^ 1) for i in range(ROWS)]
+    row_swap = [(i, i ^ 8) for i in range(ROWS)]
 
     sent = own_piece(slot_blocks, panel_blocks, prev_panel)
     sent, top_column = lax.optimization_barrier((sent, top_column))
     spread = lax.ppermute(sent, ("prow", "pcol"), spread_pairs())
 
     blocks = jnp.concatenate([pool_inverse, jnp.concatenate([top_column[:16], top_column[16:]], 1)], 0)
-    blocks_z = lax.ppermute(blocks, "prow", row_swap)
+    blocks_x = lax.ppermute(blocks, "prow", row_swap)
     blocks_b = lax.ppermute(blocks, "pcol", core_swap)
 
     cross_own, cross_sent = cross_rows(slot_blocks, panel_blocks, top_column, top_diag, prev_panel)
@@ -316,13 +321,13 @@
 
     send = gather_operand(spread, cross_own, cross_other, prev_panel)
     got = lax.all_to_all(send, "prow", 0, 0, tiled=True)
-    blocks_zb = lax.ppermute(blocks_z, "pcol", core_swap)
-
-    send, cross_pair, stride = column_product(got, blocks, blocks_b, blocks_z, blocks_zb)
+    blocks_xb = lax.ppermute(blocks_x, "pcol", core_swap)
+
+    send, cross_pair, stride = column_product(got, blocks, blocks_b, blocks_x, blocks_xb)
     groups = [
-        [(x * 8 + 2 * z + h) * COLS + 2 * i + k for i in range(YS) for h in range(2)]
-        for x in range(4)
-        for z in range(4)
+        [((2 * x + h) * 8 + z) * COLS + 2 * i + k for i in range(YS) for h in range(2)]
+        for x in range(2)
+        for z in range(8)
         for k in range(2)
     ]
     got = lax.all_to_all(send, ("prow", "pcol"), 0, 0, tiled=True, axis_index_groups=groups)

time: 125 us -> 118 us (0.944)
  waiting for transfers between devices: 31 us -> 25.7 us
    ppermute x2, waiting for transfers between devices: 24.2 us -> 19 us  [the longest x1 17.1 us: step(): blocks_x = lax.ppermute(blocks, 'prow', row_swap)]
where the time goes in v7:
time: 118 us
  starting transfers between devices  40.8 us (35%)
  blocking collectives  38.5 us (33%)
  waiting for transfers between devices  25.7 us (22%)
  Pallas kernels  10.8 us (9%)
    all_to_all x1, blocking collectives, step(): lax.all_to_all(send, ('prow', 'pcol'), 0, 0, tiled=True, axis_index_group...  19.7 us
    all_to_all x1, blocking collectives, step(): got = lax.all_to_all(send, 'prow', 0, 0, tiled=True)  18.8 us
    all_to_all x1, starting transfers between devices, step(): got = lax.all_to_all(send, 'prow', 0, 0, tiled=True)  17.9 us
    ppermute x1, waiting for transfers between devices, step(): blocks_x = lax.ppermute(blocks, 'prow', row_swap)  17.1 us
    ppermute x1, starting transfers between devices, step(): spread = lax.ppermute(sent, ('prow', 'pcol'), spread_pairs())  8.09 us
    all_to_all x1, starting transfers between devices, step(): got = lax.all_to_all(total, 'prow', 0, 0, tiled=True)  4.96 us
    all_to_all x1, waiting for transfers between devices, step(): got = lax.all_to_all(total, 'prow', 0, 0, tiled=True)  4.36 us
  transfers between devices with their start and end apart: 8, of which 5 were waited for; matrix products, arithmetic and copies ran while one was open for 0% of the time, Pallas kernels for 2%

profile of v7, /device:TPU:2, one launch (start us, length us, event | category | flops | bytes accessed | tf_op | source)
XLA Modules:
  0.0 117.6 jit_solution(7875295639745935871)
XLA Ops:
  0.6 0.0 copy-start.5
  0.6 0.0 copy-start.1
  0.7 0.0 copy-start
  0.7 0.0 copy-start.2
  0.7 2.0 %own_piece.1 = f32[40,256]{1,0:T(8,128)} custom-call(s32[1,64]{1,0:T(1,128)} %slots.5, f32[1,256,512]{2,1,0:T(8,128)} %panel.5, f32[1,16,512]{2,1,0:T(8,128)} %prev.5), custom_call_target="tpu_custom_call" | custom-call | tf_op jit(solution)/shard_map/own_piece/pallas_call | solution.py:67
  2.7 8.1 %collective-permute-start = (f32[40,256]{1,0:T(8,128)}, f32[40,256]{1,0:T(8,128)S(1)}, u32[]{:S(2)}, u32[]{:S(2)}) collective-permute-start(f32[40,256]{1,0:T(8,128)} %own_piece.1), channel_id=1, source_target_pairs={{0,64},{1,65},{2,80},{3,81},{4,96},{5,97},{6,112},{7,113},{8,0},{9... | collective-permute-start | bytes 122888 | tf_op jit(solution)/shard_map/ppermute | solution.py:313
  10.8 0.0 copy-done.5
  10.8 0.0 copy-done.1
  10.8 0.0 copy-done
  10.8 0.0 copy-done.2
  10.9 0.0 copy-start.3
  10.9 0.8 copy-done.3
  11.7 1.4 %cross_rows.1 = (f32[32,256]{1,0:T(8,128)S(1)}, f32[32,256]{1,0:T(8,128)S(1)}) custom-call(s32[1,64]{1,0:T(1,128)S(1)} %copy-done.5, f32[1,256,512]{2,1,0:T(8,128)S(1)} %copy-done, f32[32,256]{1,0:T(8,128)S(1)} %copy-done.2, f32[32,512]{1,0:T(8,128)S(1)} %copy-done.3, f32[1,16,512]{2,1,0:T(8,128)S(1)} %copy-done.1), custom_call_target="tpu_custom_call" | custom-call | tf_op jit(solution)/shard_map/cross_rows/pallas_call | solution.py:103
  13.1 1.9 %collective-permute-start.1 = (f32[32,256]{1,0:T(8,128)S(1)}, f32[32,256]{1,0:T(8,128)S(1)}, u32[]{:S(2)}, u32[]{:S(2)}) collective-permute-start(f32[32,256]{1,0:T(8,128)S(1)} %get-tuple-element.18), channel_id=1, source_target_pairs={{0,1},{1,0},{2,3},{3,2},{4,5},{5,4},{6,7},{7,6},{8,9},{9,8},{10,11... | collective-permute-start | bytes 98312 | tf_op jit(solution)/shard_map/ppermute | solution.py:320
  15.0 1.2 collective-permute-done.1.cross_other
  16.2 0.0 collective-permute-done.spread
  16.2 0.9 gather_operand.1
  17.2 0.0 copy-start.6
  17.2 17.9 %all-to-all-start = ((f32[32,40,128]{2,1,0:T(8,128)}), f32[32,40,128]{2,1,0:T(8,128)S(1)}, u32[]{:S(2)}, u32[]{:S(2)}) async-start(f32[32,40,128]{2,1,0:T(8,128)} %gather_operand.1), calls=%async_computation | async-start | bytes 1310720 | tf_op jit(solution)/shard_map/all_to_all | solution.py:323
  35.1 0.0 copy-done.6
  35.2 2.1 %collective-permute-start.3 = (f32[272,512]{1,0:T(8,128)S(1)}, f32[272,512]{1,0:T(8,128)S(1)}, u32[]{:S(2)}, u32[]{:S(2)}) collective-permute-start(f32[272,512]{1,0:T(8,128)S(1)} %maximum_maximum_fusion.mine), channel_id=1, source_target_pairs={{0,128},{16,144},{32,160},{48,176},{64,192},{80,208},{96,224},{112... | collective-permute-start | bytes 1671176 | tf_op jit(solution)/shard_map/ppermute | solution.py:316
  37.3 1.9 %collective-permute-start.2 = (f32[272,512]{1,0:T(8,128)S(1)}, f32[272,512]{1,0:T(8,128)S(1)}, u32[]{:S(2)}, u32[]{:S(2)}) collective-permute-start(f32[272,512]{1,0:T(8,128)S(1)} %maximum_maximum_fusion.mine), channel_id=1, source_target_pairs={{0,1},{1,0},{2,3},{3,2},{4,5},{5,4},{6,7},{7,6},{8,9},{9,8},{10,11... | collective-permute-start | bytes 1671176 | tf_op jit(solution)/shard_map/ppermute | solution.py:317
  39.3 17.1 %collective-permute-done.3.next_x = f32[272,512]{1,0:T(8,128)S(1)} collective-permute-done((f32[272,512]{1,0:T(8,128)S(1)}, f32[272,512]{1,0:T(8,128)S(1)}, u32[]{:S(2)}, u32[]{:S(2)}) %collective-permute-start.3) | collective-permute-done | bytes 557088 | tf_op jit(solution)/shard_map/ppermute | solution.py:316
  56.3 1.9 %collective-permute-start.4 = (f32[272,512]{1,0:T(8,128)S(1)}, f32[272,512]{1,0:T(8,128)S(1)}, u32[]{:S(2)}, u32[]{:S(2)}) collective-permute-start(f32[272,512]{1,0:T(8,128)S(1)} %collective-permute-done.3.next_x), channel_id=1, source_target_pairs={{0,1},{1,0},{2,3},{3,2},{4,5},{5,4},{6,7},{7,6},{8,9},{9,8},{10,11... | collective-permute-start | bytes 1671176 | tf_op jit(solution)/shard_map/ppermute | solution.py:324
  58.2 0.0 collective-permute-done.2.mine_b
  58.2 1.9 %collective-permute-done.4.next_xb = f32[272,512]{1,0:T(8,128)S(1)} collective-permute-done((f32[272,512]{1,0:T(8,128)S(1)}, f32[272,512]{1,0:T(8,128)S(1)}, u32[]{:S(2)}, u32[]{:S(2)}) %collective-permute-start.4) | collective-permute-done | bytes 557088 | tf_op jit(solution)/shard_map/ppermute | solution.py:324
  60.1 0.0 all-to-all-done.got
  60.2 2.2 %column_product.1 = (f32[16,40,128]{2,1,0:T(8,128)S(1)}, f32[8,128]{1,0:T(8,128)S(1)}, f32[64,128]{1,0:T(8,128)S(1)}) custom-call(f32[32,40,128]{2,1,0:T(8,128)S(1)} %all-to-all-done.got, f32[272,512]{1,0:T(8,128)S(1)} %maximum_maximum_fusion.mine, f32[272,512]{1,0:T(8,128)S(1)} %collective-permute-done.2.mine_b, ...), custom_call_target="tpu_custom_call" | custom-call | tf_op jit(solution)/shard_map/column_product/pallas_call | solution.py:177
  62.3 19.7 %all_to_all.20.got = f32[16,40,128]{2,1,0:T(8,128)S(1)} all-to-all(f32[16,40,128]{2,1,0:T(8,128)S(1)} %get-tuple-element.19), channel_id=1, replica_groups={{0,128,2,130,4,132,6,134,8,136,10,138,12,140,14,142},{1,129,3,131,5,133..., dimensions={0} | all-to-all | bytes 655360 | tf_op jit(solution)/shard_map/all_to_all | solution.py:333
  82.1 1.4 %diag_operand.1 = (f32[1,32,256]{2,1,0:T(8,128)}, f32[32,8,128]{2,1,0:T(8,128)S(1)}) custom-call(s32[1,64]{1,0:T(1,128)S(1)} %copy-done.5, f32[1,256,512]{2,1,0:T(8,128)S(1)} %copy-done, f32[16,40,128]{2,1,0:T(8,128)S(1)} %all_to_all.20.got, f32[8,128]{1,0:T(8,128)S(1)} %get-tuple-element.20.cross_pair, f32[64,128]{1,0:T(8,128)S(1)} %get-tuple-element.21.stride), custom_call_target="tpu_custom_call" | custom-call | tf_op jit(solution)/shard_map/diag_operand/pallas_call | solution.py:226
  83.5 18.8 %all_to_all.21.got = f32[32,8,128]{2,1,0:T(8,128)S(1)} all-to-all(f32[32,8,128]{2,1,0:T(8,128)S(1)} %get-tuple-element.23), channel_id=1, replica_groups=mesh['prow'=32,'pcol'=16] {'prow'}, dimensions={0} | all-to-all | bytes 262144 | tf_op jit(solution)/shard_map/all_to_all | solution.py:335
  102.3 0.7 total_operand.1
  103.0 5.0 %all-to-all-start.3 = ((f32[32,4,128]{2,1,0:T(4,128)}), f32[32,4,128]{2,1,0:T(4,128)S(1)}, u32[]{:S(2)}, u32[]{:S(2)}) async-start(f32[32,4,128]{2,1,0:T(4,128)} %get-tuple-element.26), calls=%async_computation.3 | async-start | bytes 131072 | tf_op jit(solution)/shard_map/all_to_all | solution.py:337
  108.0 1.9 %collective-permute-start.5 = (f32[32,256]{1,0:T(8,128)S(1)}, f32[32,256]{1,0:T(8,128)S(1)}, u32[]{:S(2)}, u32[]{:S(2)}) collective-permute-start(f32[32,256]{1,0:T(8,128)S(1)} %get-tuple-element.25), channel_id=1, source_target_pairs={{0,1},{1,0},{2,3},{3,2},{4,5},{5,4},{6,7},{7,6},{8,9},{9,8},{10,11... | collective-permute-start | bytes 98312 | tf_op jit(solution)/shard_map/ppermute | solution.py:338
  109.9 1.2 collective-permute-done.5.taken
  111.1 0.0 copy-start.4
  111.1 1.4 %cross_lines.1 = f32[1,32,512]{2,1,0:T(8,128)} custom-call(f32[32,256]{1,0:T(8,128)S(1)} %get-tuple-element.24.keep, f32[32,256]{1,0:T(8,128)S(1)} %collective-permute-done.5.taken), custom_call_target="tpu_custom_call" | custom-call | tf_op jit(solution)/shard_map/cross_lines/pallas_call | solution.py:279
  112.5 4.4 %all-to-all-done.3.got = f32[32,4,128]{2,1,0:T(4,128)S(1)} async-done(((f32[32,4,128]{2,1,0:T(4,128)}), f32[32,4,128]{2,1,0:T(4,128)S(1)}, u32[]{:S(2)}, u32[]{:S(2)}) %all-to-all-start.3) | async-done | bytes 65568 | tf_op jit(solution)/shard_map/all_to_all | solution.py:337
  116.9 0.0 copy-done.4
  116.9 0.7 last_step.1
  (2 shorter events, 0.0 us)
Async XLA Ops:
  0.6 10.2 %copy-start.5 = (s32[1,64]{1,0:T(1,128)S(1)}, s32[1,64]{1,0:T(1,128)}, u32[]{:S(2)}) copy-start(s32[1,64]{1,0:T(1,128)} %slots.5) | copy-start | bytes 772
  0.6 10.2 %copy-start.1 = (f32[1,16,512]{2,1,0:T(8,128)S(1)}, f32[1,16,512]{2,1,0:T(8,128)}, u32[]{:S(2)}) copy-start(f32[1,16,512]{2,1,0:T(8,128)} %prev.5) | copy-start | bytes 98308
  0.7 10.2 %copy-start = (f32[1,256,512]{2,1,0:T(8,128)S(1)}, f32[1,256,512]{2,1,0:T(8,128)}, u32[]{:S(2)}) copy-start(f32[1,256,512]{2,1,0:T(8,128)} %panel.5) | copy-start | bytes 1572868
  0.7 10.2 %copy-start.2 = (f32[32,256]{1,0:T(8,128)S(1)}, f32[32,256]{1,0:T(8,128)}, u32[]{:S(2)}) copy-start(f32[32,256]{1,0:T(8,128)} %top_column) | copy-start | bytes 98308
  2.7 13.5 %collective-permute-start = (f32[40,256]{1,0:T(8,128)}, f32[40,256]{1,0:T(8,128)S(1)}, u32[]{:S(2)}, u32[]{:S(2)}) collective-permute-start(f32[40,256]{1,0:T(8,128)} %own_piece.1), channel_id=1, source_target_pairs={{0,64},{1,65},{2,80},{3,81},{4,96},{5,97},{6,112},{7,113},{8,0},{9... | collective-permute-start | bytes 122888 | tf_op jit(solution)/shard_map/ppermute | solution.py:313
  10.9 0.8 copy-start.3
  13.1 3.1 %collective-permute-start.1 = (f32[32,256]{1,0:T(8,128)S(1)}, f32[32,256]{1,0:T(8,128)S(1)}, u32[]{:S(2)}, u32[]{:S(2)}) collective-permute-start(f32[32,256]{1,0:T(8,128)S(1)} %get-tuple-element.18), channel_id=1, source_target_pairs={{0,1},{1,0},{2,3},{3,2},{4,5},{5,4},{6,7},{7,6},{8,9},{9,8},{10,11... | collective-permute-start | bytes 98312 | tf_op jit(solution)/shard_map/ppermute | solution.py:320
  17.2 18.0 %copy-start.6 = (f32[256,512]{1,0:T(8,128)S(1)}, f32[256,512]{1,0:T(8,128)}, u32[]{:S(2)}) copy-start(f32[256,512]{1,0:T(8,128)} %param.7) | copy-start | bytes 1572868
  17.2 43.0 %all-to-all-start = ((f32[32,40,128]{2,1,0:T(8,128)}), f32[32,40,128]{2,1,0:T(8,128)S(1)}, u32[]{:S(2)}, u32[]{:S(2)}) async-start(f32[32,40,128]{2,1,0:T(8,128)} %gather_operand.1), calls=%async_computation | async-start | bytes 1310720 | tf_op jit(solution)/shard_map/all_to_all | solution.py:323
  35.2 21.1 %collective-permute-start.3 = (f32[272,512]{1,0:T(8,128)S(1)}, f32[272,512]{1,0:T(8,128)S(1)}, u32[]{:S(2)}, u32[]{:S(2)}) collective-permute-start(f32[272,512]{1,0:T(8,128)S(1)} %maximum_maximum_fusion.mine), channel_id=1, source_target_pairs={{0,128},{16,144},{32,160},{48,176},{64,192},{80,208},{96,224},{112... | collective-permute-start | bytes 1671176 | tf_op jit(solution)/shard_map/ppermute | solution.py:316
  37.3 20.9 %collective-permute-start.2 = (f32[272,512]{1,0:T(8,128)S(1)}, f32[272,512]{1,0:T(8,128)S(1)}, u32[]{:S(2)}, u32[]{:S(2)}) collective-permute-start(f32[272,512]{1,0:T(8,128)S(1)} %maximum_maximum_fusion.mine), channel_id=1, source_target_pairs={{0,1},{1,0},{2,3},{3,2},{4,5},{5,4},{6,7},{7,6},{8,9},{9,8},{10,11... | collective-permute-start | bytes 1671176 | tf_op jit(solution)/shard_map/ppermute | solution.py:317
  56.3 3.8 %collective-permute-start.4 = (f32[272,512]{1,0:T(8,128)S(1)}, f32[272,512]{1,0:T(8,128)S(1)}, u32[]{:S(2)}, u32[]{:S(2)}) collective-permute-start(f32[272,512]{1,0:T(8,128)S(1)} %collective-permute-done.3.next_x), channel_id=1, source_target_pairs={{0,1},{1,0},{2,3},{3,2},{4,5},{5,4},{6,7},{7,6},{8,9},{9,8},{10,11... | collective-permute-start | bytes 1671176 | tf_op jit(solution)/shard_map/ppermute | solution.py:324
  103.0 13.9 %all-to-all-start.3 = ((f32[32,4,128]{2,1,0:T(4,128)}), f32[32,4,128]{2,1,0:T(4,128)S(1)}, u32[]{:S(2)}, u32[]{:S(2)}) async-start(f32[32,4,128]{2,1,0:T(4,128)} %get-tuple-element.26), calls=%async_computation.3 | async-start | bytes 131072 | tf_op jit(solution)/shard_map/all_to_all | solution.py:337
  108.0 3.1 %collective-permute-start.5 = (f32[32,256]{1,0:T(8,128)S(1)}, f32[32,256]{1,0:T(8,128)S(1)}, u32[]{:S(2)}, u32[]{:S(2)}) collective-permute-start(f32[32,256]{1,0:T(8,128)S(1)} %get-tuple-element.25), channel_id=1, source_target_pairs={{0,1},{1,0},{2,3},{3,2},{4,5},{5,4},{6,7},{7,6},{8,9},{9,8},{10,11... | collective-permute-start | bytes 98312 | tf_op jit(solution)/shard_map/ppermute | solution.py:338
  111.1 5.8 %copy-start.4 = (f32[1,32,512]{2,1,0:T(8,128)S(1)}, f32[1,32,512]{2,1,0:T(8,128)}, u32[]{:S(2)}) copy-start(f32[1,32,512]{2,1,0:T(8,128)} %pivot.1) | copy-start | bytes 196612

commit v8 on v6

--- a/solution.py
+++ b/solution.py
@@ -11,8 +11,13 @@
 COLS = 16
 YS = 8
 
+
 highest = lax.Precision.HIGHEST
 kernel_params = pltpu.CompilerParams(vmem_limit_bytes=16 << 20)
+
+
+def half_of(row):
+    return row % 2
 
 
 def spread_pairs():
@@ -39,37 +44,40 @@
 def piece_kernel(slots, panel, prev, out, ids, buffer, rows, sems):
     row = lax.axis_index("prow")
     col = lax.axis_index("pcol")
-    piece = (col // 2 + 16 - row // 4 - 4 + row % 8) % 8
-    offset = 32 * (piece % 4)
+    target = (col // 2 + 16 - row // 4 - 4 + row % 8) % 8
     copies = [
-        pltpu.make_async_copy(panel.at[0, pl.ds(BLK * k + offset, 32), :], buffer.at[k], sems.at[k]) for k in range(2)
+        pltpu.make_async_copy(panel.at[0], buffer, sems.at[0]),
+        pltpu.make_async_copy(prev.at[0], rows, sems.at[1]),
+        pltpu.make_async_copy(slots, ids, sems.at[2]),
     ]
-    copies.append(pltpu.make_async_copy(prev.at[0], rows, sems.at[2]))
-    copies.append(pltpu.make_async_copy(slots, ids, sems.at[3]))
     for copy in copies:
         copy.start()
-    wanted = 2 * row + piece // 4
-    columns = select_columns(col % 2)
+    source = lax.broadcasted_iota(jnp.int32, (512, 128), 0)
+    n = lax.broadcasted_iota(jnp.int32, (512, 128), 1)
+    wanted = 64 * (n // 16) + 32 * (col % 2) + 16 * half_of(target) + n % 16
+    columns = (source == wanted).astype(jnp.float32)
     for copy in copies:
         copy.wait()
-    rolled = pltpu.roll(rows[...], (16 - 4 * (piece // 2)) % 16, 0)
-    zero = jnp.zeros((32, 512), jnp.float32)
-    chunk = jnp.where(ids[0, 2 * row] == wanted, buffer[0], zero)
-    chunk = jnp.where(ids[0, 2 * row + 1] == wanted, buffer[1], chunk)
-    out[...] = dot(jnp.concatenate([chunk, rolled[:8]], 0), columns)
+    picked = dot(buffer[...], columns)
+    zero = jnp.zeros((BLK, 128), jnp.float32)
+    low = jnp.where(ids[0, 2 * row] == 2 * row, picked[:BLK], zero)
+    high = jnp.where(ids[0, 2 * row + 1] == 2 * row + 1, picked[BLK:], zero)
+    out[:BLK, :] = low
+    out[BLK : 2 * BLK, :] = jnp.where(ids[0, 2 * row] == 2 * row + 1, picked[:BLK], high)
+    out[2 * BLK :, :] = dot(rows[...], columns)
 
 
 def own_piece(slot_blocks, panel_blocks, prev_panel):
     return pl.pallas_call(
         piece_kernel,
-        out_shape=jax.ShapeDtypeStruct((40, 256), jnp.float32),
+        out_shape=jax.ShapeDtypeStruct((272, 128), jnp.float32),
         in_specs=[pl.BlockSpec(memory_space=pltpu.HBM)] * 3,
         out_specs=pl.BlockSpec(memory_space=pltpu.VMEM),
         scratch_shapes=[
             pltpu.SMEM((1, 64), jnp.int32),
-            pltpu.VMEM((2, 32, 512), jnp.float32),
+            pltpu.VMEM((256, 512), jnp.float32),
             pltpu.VMEM((16, 512), jnp.float32),
-            pltpu.SemaphoreType.DMA((4,)),
+            pltpu.SemaphoreType.DMA((3,)),
         ],
         name="own_piece",
     )(slot_blocks, panel_blocks, prev_panel)
@@ -109,52 +117,43 @@
     )(slot_blocks, panel_blocks, top_column, top_diag, prev_panel)
 
 
-def gather_kernel(spread, cross_own, cross_other, prev, out):
-    row = lax.axis_index("prow")
+def rows_kernel(cross_own, cross_other, prev, out):
     core = lax.axis_index("pcol") % 2
     mine, others = cross_own[...], cross_other[...]
     pair = [jnp.where(core == 0, mine, others), jnp.where(core == 0, others, mine)]
     for k in range(ROWS):
-        out[k, :36, :] = spread[:36, 128 * (k % 2) : 128 * (k % 2) + 128]
-        for lane in range(2):
-            for who in range(2):
-                at = 36 + 2 * who + lane
-                out[k, at : at + 1, :] = pair[who][k : k + 1, 128 * lane : 128 * lane + 128]
-    for parity in range(2):
-
-        @pl.when(row % 2 == parity)
-        def _():
-            for k in range(16):
-                for lane in range(4):
-                    span = slice(128 * lane, 128 * lane + 128)
-                    out[16 * parity + k, 32 + lane : 33 + lane, :] = prev[0, k : k + 1, span]
-
-
-def gather_operand(spread, cross_own, cross_other, prev_panel):
-    return pl.pallas_call(
-        gather_kernel,
-        out_shape=jax.ShapeDtypeStruct((ROWS, 40, 128), jnp.float32),
-        in_specs=[pl.BlockSpec(memory_space=pltpu.VMEM)] * 4,
+        for lane in range(4):
+            span = slice(128 * lane, 128 * lane + 128)
+            out[k, lane : lane + 1, :] = prev[0, k % 16 : k % 16 + 1, span]
+            part = pair[lane // 2][k : k + 1, 128 * (lane % 2) : 128 * (lane % 2) + 128]
+            out[k, 4 + lane : 5 + lane, :] = part
+
+
+def rows_operand(cross_own, cross_other, prev_panel):
+    return pl.pallas_call(
+        rows_kernel,
+        out_shape=jax.ShapeDtypeStruct((ROWS, 8, 128), jnp.float32),
+        in_specs=[pl.BlockSpec(memory_space=pltpu.VMEM)] * 3,
         out_specs=pl.BlockSpec(memory_space=pltpu.VMEM),
         compiler_params=kernel_params,
-        name="gather_operand",
-    )(spread, cross_own, cross_other, prev_panel)
-
-
-def product_kernel(got, mine, mine_b, next_z, next_zb, out, cross_pair, stride, prev_rows):
+        name="rows_operand",
+    )(cross_own, cross_other, prev_panel)
+
+
+def product_kernel(own0, from1, from3, from2, rows, mine, mine_b, next_z, next_zb, out, cross_pair, stride, got):
     row = lax.axis_index("prow")
     core = lax.axis_index("pcol") % 2
-    half = row % 2
-    strided = row // 16
+    half = half_of(row)
+    for shift, part in ((0, own0), (1, from1), (3, from3), (2, from2)):
+        got[(row // 8 + 4 - shift) % 4] = part[...]
     for k in range(COLS):
-        stride[4 * k : 4 * k + 4, :] = got[2 * k + strided, 32:36, :]
-        prev_rows[4 * k : 4 * k + 4, :] = got[2 * k + 1 - strided, 32:36, :]
-    own = got[pl.ds(16 * core, 16), :32, :].reshape(512, 128)
-    other = got[pl.ds(16 - 16 * core, 16), :32, :].reshape(512, 128)
-    own_prev = prev_rows[pl.ds(pl.multiple_of(32 * core, 32), 32), :]
-    other_prev = prev_rows[pl.ds(pl.multiple_of(32 - 32 * core, 32), 32), :]
+        stride[4 * k : 4 * k + 4, :] = rows[2 * k + row // 16, :4, :]
+    own = got[pl.ds(2 * core, 2), : 2 * BLK, :].reshape(512, 128)
+    other = got[pl.ds(2 - 2 * core, 2), : 2 * BLK, :].reshape(512, 128)
+    own_prev = got[pl.ds(2 * core, 2), 2 * BLK :, :].reshape(32, 128)
+    other_prev = got[pl.ds(2 - 2 * core, 2), 2 * BLK :, :].reshape(32, 128)
     prev = jnp.concatenate([own_prev, other_prev], 0)
-    sums = -jnp.sum(got[:, 32:40, :], 0)
+    sums = -jnp.sum(rows[...], 0)
     pad = jnp.zeros((4, 128), jnp.float32)
     cross = jnp.concatenate([sums[4:8], pad], 0)
     cross_pair[...] = cross
@@ -168,7 +167,7 @@
             out[2 * y + which, 32:, :] = cross
 
 
-def column_product(got, mine, mine_b, next_z, next_zb):
+def column_product(own0, from1, from3, from2, rows, mine, mine_b, next_z, next_zb):
     return pl.pallas_call(
         product_kernel,
         out_shape=(
@@ -176,17 +175,17 @@
             jax.ShapeDtypeStruct((8, 128), jnp.float32),
             jax.ShapeDtypeStruct((64, 128), jnp.float32),
         ),
-        in_specs=[pl.BlockSpec(memory_space=pltpu.VMEM)] * 5,
+        in_specs=[pl.BlockSpec(memory_space=pltpu.VMEM)] * 9,
         out_specs=(pl.BlockSpec(memory_space=pltpu.VMEM),) * 3,
-        scratch_shapes=[pltpu.VMEM((64, 128), jnp.float32)],
+        scratch_shapes=[pltpu.VMEM((4, 272, 128), jnp.float32)],
         compiler_params=kernel_params,
         name="column_product",
-    )(got, mine, mine_b, next_z, next_zb)
+    )(own0, from1, from3, from2, rows, mine, mine_b, next_z, next_zb)
 
 
 def diag_kernel(slots, panel, got, cross_pair, stride, fresh_out, out, columns):
     row = lax.axis_index("prow")
-    half = row % 2
+    half = half_of(row)
     y = lax.axis_index("pcol") // 2
     fresh = []
     for h in range(2):
@@ -314,11 +313,13 @@
     cross_own, cross_sent = cross_rows(slot_blocks, panel_blocks, top_column, top_diag, prev_panel)
     cross_other = lax.ppermute(cross_sent, "pcol", core_swap)
 
-    send = gather_operand(spread, cross_own, cross_other, prev_panel)
-    got = lax.all_to_all(send, "prow", 0, 0, tiled=True)
+    rows = lax.all_to_all(rows_operand(cross_own, cross_other, prev_panel), "prow", 0, 0, tiled=True)
+    got = [spread]
+    for shift in (1, 3, 2):
+        got.append(lax.ppermute(spread, "prow", [(i, (i + 8 * shift) % ROWS) for i in range(ROWS)]))
     blocks_zb = lax.ppermute(blocks_z, "pcol", core_swap)
 
-    send, cross_pair, stride = column_product(got, blocks, blocks_b, blocks_z, blocks_zb)
+    send, cross_pair, stride = column_product(*got, rows, blocks, blocks_b, blocks_z, blocks_zb)
     groups = [
         [(x * 8 + 2 * z + h) * COLS + 2 * i + k for i in range(YS) for h in range(2)]
         for x in range(4)

time: 125 us -> 137 us (1.096)
  starting transfers between devices: 42 us -> 61.2 us
  waiting for transfers between devices: 31 us -> 19.8 us
  blocking collectives: 38.4 us -> 42.9 us
    ppermute x0 -> x3, starting transfers between devices: none -> 23.2 us  [step(): lax.ppermute(spread, 'prow', [(i, (i + 8 * shift) % ROWS) for i in range(...]
    ppermute x1, waiting for transfers between devices: 22.3 us -> 10.7 us  [step(): blocks_z = lax.ppermute(blocks, 'prow', row_swap)]
    all_to_all x1, blocking collectives: 19.7 us -> 27.8 us  [step(): lax.all_to_all(send, ('prow', 'pcol'), 0, 0, tiled=True, axis_index_group...]
    all_to_all x1, starting transfers between devices: 17.9 us -> 12.4 us  [step(): lax.all_to_all(rows_operand(cross_own, cross_other, prev_panel), 'prow',...]
    all_to_all x1, blocking collectives: 18.7 us -> 15.1 us  [step(): got = lax.all_to_all(send, 'prow', 0, 0, tiled=True)]
    ppermute x0 -> x3, waiting for transfers between devices: none -> 3.56 us  [step(): lax.ppermute(spread, 'prow', [(i, (i + 8 * shift) % ROWS) for i in range(...]
    ppermute x1, waiting for transfers between devices: 1.91 us -> 0.01 us  [step(): blocks_zb = lax.ppermute(blocks_z, 'pcol', core_swap)]
  transfers between devices with their start and end apart: 8 -> 11, of which waited for: 5 -> 5; matrix products, arithmetic and copies ran while one was open for 0% -> 0% of each run, Pallas kernels for 2% -> 3%
where the time goes in v8:
time: 137 us; the launch traced here: 136 us
  starting transfers between devices  61.2 us (45%)
  blocking collectives  42.9 us (31%)
  waiting for transfers between devices  19.8 us (14%)
  Pallas kernels  11 us (8%)
    all_to_all x1, blocking collectives, step(): lax.all_to_all(send, ('prow', 'pcol'), 0, 0, tiled=True, axis_index_group...  27.8 us
    ppermute x3, starting transfers between devices, step(): lax.ppermute(spread, 'prow', [(i, (i + 8 * shift) % ROWS) for i in range(...  23.2 us
    all_to_all x1, blocking collectives, step(): got = lax.all_to_all(send, 'prow', 0, 0, tiled=True)  15.1 us
    all_to_all x1, starting transfers between devices, step(): lax.all_to_all(rows_operand(cross_own, cross_other, prev_panel), 'prow',...  12.4 us
    ppermute x1, waiting for transfers between devices, step(): blocks_z = lax.ppermute(blocks, 'prow', row_swap)  10.7 us
    ppermute x1, starting transfers between devices, step(): spread = lax.ppermute(sent, ('prow', 'pcol'), spread_pairs())  8.09 us
    all_to_all x1, starting transfers between devices, step(): got = lax.all_to_all(total, 'prow', 0, 0, tiled=True)  4.97 us
    ppermute x1, starting transfers between devices, step(): blocks_z = lax.ppermute(blocks, 'prow', row_swap)  4.42 us
  transfers between devices with their start and end apart: 11, of which 5 were waited for; matrix products, arithmetic and copies ran while one was open for 0% of the time, Pallas kernels for 3%

profile of v8, /device:TPU:2, one launch (start us, length us, event | category | flops | bytes accessed | tf_op | source)
XLA Modules:
  0.0 135.9 jit_solution(9852345074606198808)
XLA Ops:
  0.6 0.0 copy-start.2
  0.6 0.0 copy-start.6
  0.6 2.5 %own_piece.1 = f32[272,128]{1,0:T(8,128)} custom-call(s32[1,64]{1,0:T(1,128)} %slots.5, f32[1,256,512]{2,1,0:T(8,128)} %panel.5, f32[1,16,512]{2,1,0:T(8,128)} %prev.5), custom_call_target="tpu_custom_call" | custom-call | tf_op jit(solution)/shard_map/own_piece/pallas_call | solution.py:71
  3.1 0.0 copy-done.2
  3.1 0.0 copy-done.6
  3.2 0.0 copy-start
  3.2 0.0 copy-start.1
  3.2 0.0 copy-start.3
  3.2 0.0 copy-start.5
  3.2 0.0 copy-start.7
  3.3 4.4 %collective-permute-start.6 = (f32[272,512]{1,0:T(8,128)S(1)}, f32[272,512]{1,0:T(8,128)S(1)}, u32[]{:S(2)}, u32[]{:S(2)}) collective-permute-start(f32[272,512]{1,0:T(8,128)S(1)} %maximum_maximum_fusion.mine), channel_id=1, source_target_pairs={{0,16},{16,0},{32,48},{48,32},{64,80},{80,64},{96,112},{112,96},{1... | collective-permute-start | bytes 1671176 | tf_op jit(solution)/shard_map/ppermute | solution.py:310
  7.7 1.9 %collective-permute-start.5 = (f32[272,512]{1,0:T(8,128)S(1)}, f32[272,512]{1,0:T(8,128)S(1)}, u32[]{:S(2)}, u32[]{:S(2)}) collective-permute-start(f32[272,512]{1,0:T(8,128)S(1)} %maximum_maximum_fusion.mine), channel_id=1, source_target_pairs={{0,1},{1,0},{2,3},{3,2},{4,5},{5,4},{6,7},{7,6},{8,9},{9,8},{10,11... | collective-permute-start | bytes 1671176 | tf_op jit(solution)/shard_map/ppermute | solution.py:311
  9.6 10.7 %collective-permute-done.6.next_z = f32[272,512]{1,0:T(8,128)S(1)} collective-permute-done((f32[272,512]{1,0:T(8,128)S(1)}, f32[272,512]{1,0:T(8,128)S(1)}, u32[]{:S(2)}, u32[]{:S(2)}) %collective-permute-start.6) | collective-permute-done | bytes 557088 | tf_op jit(solution)/shard_map/ppermute | solution.py:310
  20.3 1.9 %collective-permute-start.7 = (f32[272,512]{1,0:T(8,128)S(1)}, f32[272,512]{1,0:T(8,128)S(1)}, u32[]{:S(2)}, u32[]{:S(2)}) collective-permute-start(f32[272,512]{1,0:T(8,128)S(1)} %collective-permute-done.6.next_z), channel_id=1, source_target_pairs={{0,1},{1,0},{2,3},{3,2},{4,5},{5,4},{6,7},{7,6},{8,9},{9,8},{10,11... | collective-permute-start | bytes 1671176 | tf_op jit(solution)/shard_map/ppermute | solution.py:320
  22.2 0.0 copy-done
  22.2 0.0 copy-done.1
  22.2 0.0 copy-done.3
  22.2 0.0 copy-done.5
  22.2 1.4 %cross_rows.1 = (f32[32,256]{1,0:T(8,128)S(1)}, f32[32,256]{1,0:T(8,128)S(1)}) custom-call(s32[1,64]{1,0:T(1,128)S(1)} %copy-done.5, f32[1,256,512]{2,1,0:T(8,128)S(1)} %copy-done, f32[32,256]{1,0:T(8,128)S(1)} %copy-done.2, f32[32,512]{1,0:T(8,128)S(1)} %copy-done.3, f32[1,16,512]{2,1,0:T(8,128)S(1)} %copy-done.1), custom_call_target="tpu_custom_call" | custom-call | tf_op jit(solution)/shard_map/cross_rows/pallas_call | solution.py:107
  23.7 2.4 %collective-permute-start.4 = (f32[32,256]{1,0:T(8,128)S(1)}, f32[32,256]{1,0:T(8,128)S(1)}, u32[]{:S(2)}, u32[]{:S(2)}) collective-permute-start(f32[32,256]{1,0:T(8,128)S(1)} %get-tuple-element.18), channel_id=1, source_target_pairs={{0,1},{1,0},{2,3},{3,2},{4,5},{5,4},{6,7},{7,6},{8,9},{9,8},{10,11... | collective-permute-start | bytes 98312 | tf_op jit(solution)/shard_map/ppermute | solution.py:314
  26.1 0.0 copy-done.7
  26.1 8.1 %collective-permute-start = (f32[272,128]{1,0:T(8,128)S(1)}, f32[272,128]{1,0:T(8,128)S(1)}, u32[]{:S(2)}, u32[]{:S(2)}) collective-permute-start(f32[272,128]{1,0:T(8,128)S(1)} %copy-done.7), channel_id=1, source_target_pairs={{0,64},{1,65},{2,80},{3,81},{4,96},{5,97},{6,112},{7,113},{8,0},{9... | collective-permute-start | bytes 417800 | tf_op jit(solution)/shard_map/ppermute | solution.py:307
  34.2 0.0 collective-permute-done.4.cross_other
  34.2 0.7 rows_operand.1
  34.9 12.4 %all-to-all-start = ((f32[32,8,128]{2,1,0:T(8,128)}), f32[32,8,128]{2,1,0:T(8,128)S(1)}, u32[]{:S(2)}, u32[]{:S(2)}) async-start(f32[32,8,128]{2,1,0:T(8,128)} %rows_operand.1), calls=%async_computation | async-start | bytes 262144 | tf_op jit(solution)/shard_map/all_to_all | solution.py:316
  47.3 0.0 collective-permute-done.own0
  47.3 9.9 %collective-permute-start.3 = (f32[272,128]{1,0:T(8,128)S(1)}, f32[272,128]{1,0:T(8,128)S(1)}, u32[]{:S(2)}, u32[]{:S(2)}) collective-permute-start(f32[272,128]{1,0:T(8,128)S(1)} %collective-permute-done.own0), channel_id=1, source_target_pairs={{0,256},{16,272},{32,288},{48,304},{64,320},{80,336},{96,352},{112... | collective-permute-start | bytes 417800 | tf_op jit(solution)/shard_map/ppermute | solution.py:319
  57.2 10.0 %collective-permute-start.2 = (f32[272,128]{1,0:T(8,128)S(1)}, f32[272,128]{1,0:T(8,128)S(1)}, u32[]{:S(2)}, u32[]{:S(2)}) collective-permute-start(f32[272,128]{1,0:T(8,128)S(1)} %collective-permute-done.own0), channel_id=1, source_target_pairs={{0,384},{16,400},{32,416},{48,432},{64,448},{80,464},{96,480},{112... | collective-permute-start | bytes 417800 | tf_op jit(solution)/shard_map/ppermute | solution.py:319
  67.1 3.4 %collective-permute-start.1 = (f32[272,128]{1,0:T(8,128)S(1)}, f32[272,128]{1,0:T(8,128)S(1)}, u32[]{:S(2)}, u32[]{:S(2)}) collective-permute-start(f32[272,128]{1,0:T(8,128)S(1)} %collective-permute-done.own0), channel_id=1, source_target_pairs={{0,128},{16,144},{32,160},{48,176},{64,192},{80,208},{96,224},{112... | collective-permute-start | bytes 417800 | tf_op jit(solution)/shard_map/ppermute | solution.py:319
  70.5 0.0 collective-permute-done.3.from2
  70.5 1.1 collective-permute-done.2.from3
  71.6 2.5 %collective-permute-done.1.from1 = f32[272,128]{1,0:T(8,128)S(1)} collective-permute-done((f32[272,128]{1,0:T(8,128)S(1)}, f32[272,128]{1,0:T(8,128)S(1)}, u32[]{:S(2)}, u32[]{:S(2)}) %collective-permute-start.1) | collective-permute-done | bytes 139296 | tf_op jit(solution)/shard_map/ppermute | solution.py:319
  74.1 0.0 all-to-all-done.rows
  74.1 0.0 collective-permute-done.5.mine_b
  74.1 0.0 collective-permute-done.7.next_zb
  74.1 2.2 %column_product.1 = (f32[16,40,128]{2,1,0:T(8,128)S(1)}, f32[8,128]{1,0:T(8,128)S(1)}, f32[64,128]{1,0:T(8,128)S(1)}) custom-call(f32[272,128]{1,0:T(8,128)S(1)} %collective-permute-done.own0, f32[272,128]{1,0:T(8,128)S(1)} %collective-permute-done.1.from1, f32[272,128]{1,0:T(8,128)S(1)} %collective-permute-done.2.from3, ...), custom_call_target="tpu_custom_call" | custom-call | tf_op jit(solution)/shard_map/column_product/pallas_call | solution.py:171
  76.3 27.8 %all_to_all.20.got = f32[16,40,128]{2,1,0:T(8,128)S(1)} all-to-all(f32[16,40,128]{2,1,0:T(8,128)S(1)} %get-tuple-element.19), channel_id=1, replica_groups={{0,16,2,18,4,20,6,22,8,24,10,26,12,28,14,30},{1,17,3,19,5,21,7,23,9,25,..., dimensions={0} | all-to-all | bytes 655360 | tf_op jit(solution)/shard_map/all_to_all | solution.py:329
  104.1 1.4 %diag_operand.1 = (f32[1,32,256]{2,1,0:T(8,128)}, f32[32,8,128]{2,1,0:T(8,128)S(1)}) custom-call(s32[1,64]{1,0:T(1,128)S(1)} %copy-done.5, f32[1,256,512]{2,1,0:T(8,128)S(1)} %copy-done, f32[16,40,128]{2,1,0:T(8,128)S(1)} %all_to_all.20.got, f32[8,128]{1,0:T(8,128)S(1)} %get-tuple-element.20.cross_pair, f32[64,128]{1,0:T(8,128)S(1)} %get-tuple-element.21.stride), custom_call_target="tpu_custom_call" | custom-call | tf_op jit(solution)/shard_map/diag_operand/pallas_call | solution.py:220
  105.6 15.1 %all_to_all.21.got = f32[32,8,128]{2,1,0:T(8,128)S(1)} all-to-all(f32[32,8,128]{2,1,0:T(8,128)S(1)} %get-tuple-element.23), channel_id=1, replica_groups=mesh['prow'=32,'pcol'=16] {'prow'}, dimensions={0} | all-to-all | bytes 262144 | tf_op jit(solution)/shard_map/all_to_all | solution.py:331
  120.7 0.7 total_operand.1
  121.3 5.0 %all-to-all-start.3 = ((f32[32,4,128]{2,1,0:T(4,128)}), f32[32,4,128]{2,1,0:T(4,128)S(1)}, u32[]{:S(2)}, u32[]{:S(2)}) async-start(f32[32,4,128]{2,1,0:T(4,128)} %get-tuple-element.26), calls=%async_computation.3 | async-start | bytes 131072 | tf_op jit(solution)/shard_map/all_to_all | solution.py:333
  126.3 1.9 %collective-permute-start.8 = (f32[32,256]{1,0:T(8,128)S(1)}, f32[32,256]{1,0:T(8,128)S(1)}, u32[]{:S(2)}, u32[]{:S(2)}) collective-permute-start(f32[32,256]{1,0:T(8,128)S(1)} %get-tuple-element.25), channel_id=1, source_target_pairs={{0,1},{1,0},{2,3},{3,2},{4,5},{5,4},{6,7},{7,6},{8,9},{9,8},{10,11... | collective-permute-start | bytes 98312 | tf_op jit(solution)/shard_map/ppermute | solution.py:334
  128.3 1.2 collective-permute-done.8.taken
  129.4 0.0 copy-start.4
  129.4 1.4 %cross_lines.1 = f32[1,32,512]{2,1,0:T(8,128)} custom-call(f32[32,256]{1,0:T(8,128)S(1)} %get-tuple-element.24.keep, f32[32,256]{1,0:T(8,128)S(1)} %collective-permute-done.8.taken), custom_call_target="tpu_custom_call" | custom-call | tf_op jit(solution)/shard_map/cross_lines/pallas_call | solution.py:273
  130.9 4.4 %all-to-all-done.3.got = f32[32,4,128]{2,1,0:T(4,128)S(1)} async-done(((f32[32,4,128]{2,1,0:T(4,128)}), f32[32,4,128]{2,1,0:T(4,128)S(1)}, u32[]{:S(2)}, u32[]{:S(2)}) %all-to-all-start.3) | async-done | bytes 65568 | tf_op jit(solution)/shard_map/all_to_all | solution.py:333
  135.2 0.0 copy-done.4
  135.2 0.7 last_step.1
  (2 shorter events, 0.0 us)
Async XLA Ops:
  0.6 2.5 %copy-start.2 = (f32[32,256]{1,0:T(8,128)S(1)}, f32[32,256]{1,0:T(8,128)}, u32[]{:S(2)}) copy-start(f32[32,256]{1,0:T(8,128)} %top_column) | copy-start | bytes 98308
  0.6 2.5 %copy-start.6 = (f32[256,512]{1,0:T(8,128)S(1)}, f32[256,512]{1,0:T(8,128)}, u32[]{:S(2)}) copy-start(f32[256,512]{1,0:T(8,128)} %param.7) | copy-start | bytes 1572868
  3.2 19.1 %copy-start = (f32[1,256,512]{2,1,0:T(8,128)S(1)}, f32[1,256,512]{2,1,0:T(8,128)}, u32[]{:S(2)}) copy-start(f32[1,256,512]{2,1,0:T(8,128)} %panel.5) | copy-start | bytes 1572868
  3.2 19.1 %copy-start.1 = (f32[1,16,512]{2,1,0:T(8,128)S(1)}, f32[1,16,512]{2,1,0:T(8,128)}, u32[]{:S(2)}) copy-start(f32[1,16,512]{2,1,0:T(8,128)} %prev.5) | copy-start | bytes 98308
  3.2 19.0 %copy-start.3 = (f32[32,512]{1,0:T(8,128)S(1)}, f32[32,512]{1,0:T(8,128)}, u32[]{:S(2)}) copy-start(f32[32,512]{1,0:T(8,128)} %top_diag.1) | copy-start | bytes 196612
  3.2 19.0 %copy-start.5 = (s32[1,64]{1,0:T(1,128)S(1)}, s32[1,64]{1,0:T(1,128)}, u32[]{:S(2)}) copy-start(s32[1,64]{1,0:T(1,128)} %slots.5) | copy-start | bytes 772
  3.2 22.8 %copy-start.7 = (f32[272,128]{1,0:T(8,128)S(1)}, f32[272,128]{1,0:T(8,128)}, u32[]{:S(2)}) copy-start(f32[272,128]{1,0:T(8,128)} %own_piece.1) | copy-start | bytes 417796
  3.3 17.0 %collective-permute-start.6 = (f32[272,512]{1,0:T(8,128)S(1)}, f32[272,512]{1,0:T(8,128)S(1)}, u32[]{:S(2)}, u32[]{:S(2)}) collective-permute-start(f32[272,512]{1,0:T(8,128)S(1)} %maximum_maximum_fusion.mine), channel_id=1, source_target_pairs={{0,16},{16,0},{32,48},{48,32},{64,80},{80,64},{96,112},{112,96},{1... | collective-permute-start | bytes 1671176 | tf_op jit(solution)/shard_map/ppermute | solution.py:310
  7.7 66.4 %collective-permute-start.5 = (f32[272,512]{1,0:T(8,128)S(1)}, f32[272,512]{1,0:T(8,128)S(1)}, u32[]{:S(2)}, u32[]{:S(2)}) collective-permute-start(f32[272,512]{1,0:T(8,128)S(1)} %maximum_maximum_fusion.mine), channel_id=1, source_target_pairs={{0,1},{1,0},{2,3},{3,2},{4,5},{5,4},{6,7},{7,6},{8,9},{9,8},{10,11... | collective-permute-start | bytes 1671176 | tf_op jit(solution)/shard_map/ppermute | solution.py:311
  20.3 53.8 %collective-permute-start.7 = (f32[272,512]{1,0:T(8,128)S(1)}, f32[272,512]{1,0:T(8,128)S(1)}, u32[]{:S(2)}, u32[]{:S(2)}) collective-permute-start(f32[272,512]{1,0:T(8,128)S(1)} %collective-permute-done.6.next_z), channel_id=1, source_target_pairs={{0,1},{1,0},{2,3},{3,2},{4,5},{5,4},{6,7},{7,6},{8,9},{9,8},{10,11... | collective-permute-start | bytes 1671176 | tf_op jit(solution)/shard_map/ppermute | solution.py:320
  23.7 10.5 %collective-permute-start.4 = (f32[32,256]{1,0:T(8,128)S(1)}, f32[32,256]{1,0:T(8,128)S(1)}, u32[]{:S(2)}, u32[]{:S(2)}) collective-permute-start(f32[32,256]{1,0:T(8,128)S(1)} %get-tuple-element.18), channel_id=1, source_target_pairs={{0,1},{1,0},{2,3},{3,2},{4,5},{5,4},{6,7},{7,6},{8,9},{9,8},{10,11... | collective-permute-start | bytes 98312 | tf_op jit(solution)/shard_map/ppermute | solution.py:314
  26.1 21.2 %collective-permute-start = (f32[272,128]{1,0:T(8,128)S(1)}, f32[272,128]{1,0:T(8,128)S(1)}, u32[]{:S(2)}, u32[]{:S(2)}) collective-permute-start(f32[272,128]{1,0:T(8,128)S(1)} %copy-done.7), channel_id=1, source_target_pairs={{0,64},{1,65},{2,80},{3,81},{4,96},{5,97},{6,112},{7,113},{8,0},{9... | collective-permute-start | bytes 417800 | tf_op jit(solution)/shard_map/ppermute | solution.py:307
  34.9 39.2 %all-to-all-start = ((f32[32,8,128]{2,1,0:T(8,128)}), f32[32,8,128]{2,1,0:T(8,128)S(1)}, u32[]{:S(2)}, u32[]{:S(2)}) async-start(f32[32,8,128]{2,1,0:T(8,128)} %rows_operand.1), calls=%async_computation | async-start | bytes 262144 | tf_op jit(solution)/shard_map/all_to_all | solution.py:316
  47.3 23.2 %collective-permute-start.3 = (f32[272,128]{1,0:T(8,128)S(1)}, f32[272,128]{1,0:T(8,128)S(1)}, u32[]{:S(2)}, u32[]{:S(2)}) collective-permute-start(f32[272,128]{1,0:T(8,128)S(1)} %collective-permute-done.own0), channel_id=1, source_target_pairs={{0,256},{16,272},{32,288},{48,304},{64,320},{80,336},{96,352},{112... | collective-permute-start | bytes 417800 | tf_op jit(solution)/shard_map/ppermute | solution.py:319
  57.2 14.4 %collective-permute-start.2 = (f32[272,128]{1,0:T(8,128)S(1)}, f32[272,128]{1,0:T(8,128)S(1)}, u32[]{:S(2)}, u32[]{:S(2)}) collective-permute-start(f32[272,128]{1,0:T(8,128)S(1)} %collective-permute-done.own0), channel_id=1, source_target_pairs={{0,384},{16,400},{32,416},{48,432},{64,448},{80,464},{96,480},{112... | collective-permute-start | bytes 417800 | tf_op jit(solution)/shard_map/ppermute | solution.py:319
  67.1 6.9 %collective-permute-start.1 = (f32[272,128]{1,0:T(8,128)S(1)}, f32[272,128]{1,0:T(8,128)S(1)}, u32[]{:S(2)}, u32[]{:S(2)}) collective-permute-start(f32[272,128]{1,0:T(8,128)S(1)} %collective-permute-done.own0), channel_id=1, source_target_pairs={{0,128},{16,144},{32,160},{48,176},{64,192},{80,208},{96,224},{112... | collective-permute-start | bytes 417800 | tf_op jit(solution)/shard_map/ppermute | solution.py:319
  121.3 13.9 %all-to-all-start.3 = ((f32[32,4,128]{2,1,0:T(4,128)}), f32[32,4,128]{2,1,0:T(4,128)S(1)}, u32[]{:S(2)}, u32[]{:S(2)}) async-start(f32[32,4,128]{2,1,0:T(4,128)} %get-tuple-element.26), calls=%async_computation.3 | async-start | bytes 131072 | tf_op jit(solution)/shard_map/all_to_all | solution.py:333
  126.3 3.1 %collective-permute-start.8 = (f32[32,256]{1,0:T(8,128)S(1)}, f32[32,256]{1,0:T(8,128)S(1)}, u32[]{:S(2)}, u32[]{:S(2)}) collective-permute-start(f32[32,256]{1,0:T(8,128)S(1)} %get-tuple-element.25), channel_id=1, source_target_pairs={{0,1},{1,0},{2,3},{3,2},{4,5},{5,4},{6,7},{7,6},{8,9},{9,8},{10,11... | collective-permute-start | bytes 98312 | tf_op jit(solution)/shard_map/ppermute | solution.py:334
  129.4 5.8 %copy-start.4 = (f32[1,32,512]{2,1,0:T(8,128)S(1)}, f32[1,32,512]{2,1,0:T(8,128)}, u32[]{:S(2)}) copy-start(f32[1,32,512]{2,1,0:T(8,128)} %pivot.1) | copy-start | bytes 196612

commit v9 on v7

--- a/solution.py
+++ b/solution.py
@@ -216,10 +216,10 @@
         picked = columns[2 + h, pl.ds(pl.multiple_of(16 * y, 16), 16), :]
         own.append(dot(picked[:, :16], rows))
     part = part + jnp.concatenate(own, 0)
-    for k in range(ROWS):
+    for x in range(4):
         for lane in range(4):
-            out[k, lane : lane + 1, :] = part[k : k + 1, 128 * lane : 128 * lane + 128]
-        out[k, 4:8, :] = cross_pair[:4, :]
+            out[x, 8 * lane : 8 * lane + 8, :] = part[8 * x : 8 * x + 8, 128 * lane : 128 * lane + 128]
+        out[x, 32:, :] = cross_pair[...]
 
 
 def diag_operand(slot_blocks, panel_blocks, got, cross_pair, stride):
@@ -227,7 +227,7 @@
         diag_kernel,
         out_shape=(
             jax.ShapeDtypeStruct((1, 32, 256), jnp.float32),
-            jax.ShapeDtypeStruct((ROWS, 8, 128), jnp.float32),
+            jax.ShapeDtypeStruct((4, 40, 128), jnp.float32),
         ),
         in_specs=[pl.BlockSpec(memory_space=pltpu.SMEM)] + [pl.BlockSpec(memory_space=pltpu.VMEM)] * 4,
         out_specs=(pl.BlockSpec(memory_space=pltpu.VMEM),) * 2,
@@ -237,14 +237,36 @@
     )(slot_blocks, panel_blocks, got, cross_pair, stride)
 
 
+def middle_kernel(got, out):
+    total = jnp.sum(got[:, :32, :], 0)
+    for z in range(8):
+        out[z, :32, :] = total
+        for x in range(4):
+            out[z, 32 + 4 * x : 36 + 4 * x, :] = got[x, 32:36, :]
+
+
+def middle_operand(got):
+    return pl.pallas_call(
+        middle_kernel,
+        out_shape=jax.ShapeDtypeStruct((8, 48, 128), jnp.float32),
+        in_specs=[pl.BlockSpec(memory_space=pltpu.VMEM)],
+        out_specs=pl.BlockSpec(memory_space=pltpu.VMEM),
+        compiler_params=kernel_params,
+        name="middle_operand",
+    )(got)
+
+
 def total_kernel(got, out, keep, give):
     core = lax.axis_index("pcol") % 2
-    total = jnp.sum(got[:, :4, :], 0)
+    total = jnp.sum(got[:, :32, :], 0)
+    for x in range(4):
+        out[x] = total
     for k in range(ROWS):
-        out[k] = total
+        at = 32 + 4 * (k // 8)
         for lane in range(2):
             span = slice(128 * lane, 128 * lane + 128)
-            first, second = got[k, 4 + lane : 5 + lane, :], got[k, 6 + lane : 7 + lane, :]
+            first = got[k % 8, at + lane : at + lane + 1, :]
+            second = got[k % 8, at + lane + 2 : at + lane + 3, :]
             keep[k : k + 1, span] = jnp.where(core == 0, first, second)
             give[k : k + 1, span] = jnp.where(core == 0, second, first)
 
@@ -253,7 +275,7 @@
     return pl.pallas_call(
         total_kernel,
         out_shape=(
-            jax.ShapeDtypeStruct((ROWS, 4, 128), jnp.float32),
+            jax.ShapeDtypeStruct((4, 32, 128), jnp.float32),
             jax.ShapeDtypeStruct((32, 256), jnp.float32),
             jax.ShapeDtypeStruct((32, 256), jnp.float32),
         ),
@@ -287,10 +309,10 @@
 
 
 def last_kernel(got, pivot, out):
-    for k in range(ROWS):
+    for x in range(4):
         for lane in range(4):
-            span = slice(128 * lane, 128 * lane + 128)
-            out[0, k : k + 1, span] = pivot[0, k : k + 1, span] - got[k, lane : lane + 1, :]
+            rows, span = slice(8 * x, 8 * x + 8), slice(128 * lane, 128 * lane + 128)
+            out[0, rows, span] = pivot[0, rows, span] - got[x, 8 * lane : 8 * lane + 8, :]
 
 
 def last_step(got, pivot_inverse):
@@ -332,9 +354,12 @@
     ]
     got = lax.all_to_all(send, ("prow", "pcol"), 0, 0, tiled=True, axis_index_groups=groups)
     fresh, send = diag_operand(slot_blocks, panel_blocks, got, cross_pair, stride)
-    got = lax.all_to_all(send, "prow", 0, 0, tiled=True)
+    along_x = [[x * 8 + z for x in range(4)] for z in range(8)]
+    along_z = [[x * 8 + z for z in range(8)] for x in range(4)]
+    got = lax.all_to_all(send, "prow", 0, 0, tiled=True, axis_index_groups=along_x)
+    got = lax.all_to_all(middle_operand(got), "prow", 0, 0, tiled=True, axis_index_groups=along_z)
     total, keep, give = total_operand(got)
-    got = lax.all_to_all(total, "prow", 0, 0, tiled=True)
+    got = lax.all_to_all(total, "prow", 0, 0, tiled=True, axis_index_groups=along_x)
     taken = lax.ppermute(give, "pcol", core_swap)
     cross_out = cross_lines(keep, taken)
     return fresh, cross_out, last_step(got, pivot_inverse)

time: 118 us -> 121 us (1.025)
  the two profiles are of different devices: /device:TPU:2 before, /device:TPU:1 now
where the time goes in v9:
time: 121 us; the launch traced here: 120 us
  starting transfers between devices  48 us (40%)
  blocking collectives  40.9 us (34%)
  waiting for transfers between devices  18.5 us (15%)
  Pallas kernels  10.8 us (9%)
    all_to_all x1, blocking collectives, step(): lax.all_to_all(send, ('prow', 'pcol'), 0, 0, tiled=True, axis_index_group...  18.5 us
    ppermute x1, waiting for transfers between devices, step(): blocks_x = lax.ppermute(blocks, 'prow', row_swap)  15.2 us
    all_to_all x1, blocking collectives, step(): lax.all_to_all(middle_operand(got), 'prow', 0, 0, tiled=True, axis_index_...  14.3 us
    all_to_all x1, starting transfers between devices, step(): got = lax.all_to_all(send, 'prow', 0, 0, tiled=True)  14.2 us
    ppermute x1, starting transfers between devices, step(): spread = lax.ppermute(sent, ('prow', 'pcol'), spread_pairs())  11.5 us
    all_to_all x1, blocking collectives, step(): lax.all_to_all(send, 'prow', 0, 0, tiled=True, axis_index_groups=along_x)  8.13 us
    ppermute x1, starting transfers between devices, step(): taken = lax.ppermute(give, 'pcol', core_swap)  6.44 us
    ppermute x1, starting transfers between devices, step(): blocks_b = lax.ppermute(blocks, 'pcol', core_swap)  3.42 us
  transfers between devices with their start and end apart: 8, of which 4 were waited for; matrix products, arithmetic and copies ran while one was open for 0% of the time, Pallas kernels for 2%

profile of v9, /device:TPU:1, one launch (start us, length us, event | category | flops | bytes accessed | tf_op | source)
XLA Modules:
  0.0 119.9 jit_solution(6972781232029186800)
XLA Ops:
  0.6 0.0 copy-start.5
  0.6 0.0 copy-start.1
  0.7 0.0 copy-start
  0.7 0.0 copy-start.2
  0.7 2.0 %own_piece.1 = f32[40,256]{1,0:T(8,128)} custom-call(s32[1,64]{1,0:T(1,128)} %slots.5, f32[1,256,512]{2,1,0:T(8,128)} %panel.5, f32[1,16,512]{2,1,0:T(8,128)} %prev.5), custom_call_target="tpu_custom_call" | custom-call | tf_op jit(solution)/shard_map/own_piece/pallas_call | solution.py:67
  2.7 11.5 %collective-permute-start = (f32[40,256]{1,0:T(8,128)}, f32[40,256]{1,0:T(8,128)S(1)}, u32[]{:S(2)}, u32[]{:S(2)}) collective-permute-start(f32[40,256]{1,0:T(8,128)} %own_piece.1), channel_id=1, source_target_pairs={{0,64},{1,65},{2,80},{3,81},{4,96},{5,97},{6,112},{7,113},{8,0},{9... | collective-permute-start | bytes 122888 | tf_op jit(solution)/shard_map/ppermute | solution.py:335
  14.2 0.0 copy-done.5
  14.2 0.0 copy-done.1
  14.2 0.0 copy-done
  14.2 0.0 copy-done.2
  14.2 0.0 copy-start.3
  14.2 0.8 copy-done.3
  15.1 1.4 %cross_rows.1 = (f32[32,256]{1,0:T(8,128)S(1)}, f32[32,256]{1,0:T(8,128)S(1)}) custom-call(s32[1,64]{1,0:T(1,128)S(1)} %copy-done.5, f32[1,256,512]{2,1,0:T(8,128)S(1)} %copy-done, f32[32,256]{1,0:T(8,128)S(1)} %copy-done.2, f32[32,512]{1,0:T(8,128)S(1)} %copy-done.3, f32[1,16,512]{2,1,0:T(8,128)S(1)} %copy-done.1), custom_call_target="tpu_custom_call" | custom-call | tf_op jit(solution)/shard_map/cross_rows/pallas_call | solution.py:103
  16.5 2.9 %collective-permute-start.1 = (f32[32,256]{1,0:T(8,128)S(1)}, f32[32,256]{1,0:T(8,128)S(1)}, u32[]{:S(2)}, u32[]{:S(2)}) collective-permute-start(f32[32,256]{1,0:T(8,128)S(1)} %get-tuple-element.18), channel_id=1, source_target_pairs={{0,1},{1,0},{2,3},{3,2},{4,5},{5,4},{6,7},{7,6},{8,9},{9,8},{10,11... | collective-permute-start | bytes 98312 | tf_op jit(solution)/shard_map/ppermute | solution.py:342
  19.4 0.8 collective-permute-done.1.cross_other
  20.2 0.0 collective-permute-done.spread
  20.2 0.9 gather_operand.1
  21.1 0.0 copy-start.6
  21.1 14.2 %all-to-all-start = ((f32[32,40,128]{2,1,0:T(8,128)}), f32[32,40,128]{2,1,0:T(8,128)S(1)}, u32[]{:S(2)}, u32[]{:S(2)}) async-start(f32[32,40,128]{2,1,0:T(8,128)} %gather_operand.1), calls=%async_computation | async-start | bytes 1310720 | tf_op jit(solution)/shard_map/all_to_all | solution.py:345
  35.4 0.0 copy-done.6
  35.4 3.1 %collective-permute-start.3 = (f32[272,512]{1,0:T(8,128)S(1)}, f32[272,512]{1,0:T(8,128)S(1)}, u32[]{:S(2)}, u32[]{:S(2)}) collective-permute-start(f32[272,512]{1,0:T(8,128)S(1)} %maximum_maximum_fusion.mine), channel_id=1, source_target_pairs={{0,128},{16,144},{32,160},{48,176},{64,192},{80,208},{96,224},{112... | collective-permute-start | bytes 1671176 | tf_op jit(solution)/shard_map/ppermute | solution.py:338
  38.6 3.4 %collective-permute-start.2 = (f32[272,512]{1,0:T(8,128)S(1)}, f32[272,512]{1,0:T(8,128)S(1)}, u32[]{:S(2)}, u32[]{:S(2)}) collective-permute-start(f32[272,512]{1,0:T(8,128)S(1)} %maximum_maximum_fusion.mine), channel_id=1, source_target_pairs={{0,1},{1,0},{2,3},{3,2},{4,5},{5,4},{6,7},{7,6},{8,9},{9,8},{10,11... | collective-permute-start | bytes 1671176 | tf_op jit(solution)/shard_map/ppermute | solution.py:339
  42.0 15.2 %collective-permute-done.3.next_x = f32[272,512]{1,0:T(8,128)S(1)} collective-permute-done((f32[272,512]{1,0:T(8,128)S(1)}, f32[272,512]{1,0:T(8,128)S(1)}, u32[]{:S(2)}, u32[]{:S(2)}) %collective-permute-start.3) | collective-permute-done | bytes 557088 | tf_op jit(solution)/shard_map/ppermute | solution.py:338
  57.2 3.1 %collective-permute-start.4 = (f32[272,512]{1,0:T(8,128)S(1)}, f32[272,512]{1,0:T(8,128)S(1)}, u32[]{:S(2)}, u32[]{:S(2)}) collective-permute-start(f32[272,512]{1,0:T(8,128)S(1)} %collective-permute-done.3.next_x), channel_id=1, source_target_pairs={{0,1},{1,0},{2,3},{3,2},{4,5},{5,4},{6,7},{7,6},{8,9},{9,8},{10,11... | collective-permute-start | bytes 1671176 | tf_op jit(solution)/shard_map/ppermute | solution.py:346
  60.4 0.0 collective-permute-done.2.mine_b
  60.4 1.6 %collective-permute-done.4.next_xb = f32[272,512]{1,0:T(8,128)S(1)} collective-permute-done((f32[272,512]{1,0:T(8,128)S(1)}, f32[272,512]{1,0:T(8,128)S(1)}, u32[]{:S(2)}, u32[]{:S(2)}) %collective-permute-start.4) | collective-permute-done | bytes 557088 | tf_op jit(solution)/shard_map/ppermute | solution.py:346
  62.0 0.0 all-to-all-done.got
  62.0 2.2 %column_product.1 = (f32[16,40,128]{2,1,0:T(8,128)S(1)}, f32[8,128]{1,0:T(8,128)S(1)}, f32[64,128]{1,0:T(8,128)S(1)}) custom-call(f32[32,40,128]{2,1,0:T(8,128)S(1)} %all-to-all-done.got, f32[272,512]{1,0:T(8,128)S(1)} %maximum_maximum_fusion.mine, f32[272,512]{1,0:T(8,128)S(1)} %collective-permute-done.2.mine_b, ...), custom_call_target="tpu_custom_call" | custom-call | tf_op jit(solution)/shard_map/column_product/pallas_call | solution.py:177
  64.1 18.5 %all_to_all.25.got = f32[16,40,128]{2,1,0:T(8,128)S(1)} all-to-all(f32[16,40,128]{2,1,0:T(8,128)S(1)} %get-tuple-element.19), channel_id=1, replica_groups={{0,128,2,130,4,132,6,134,8,136,10,138,12,140,14,142},{1,129,3,131,5,133..., dimensions={0} | all-to-all | bytes 655360 | tf_op jit(solution)/shard_map/all_to_all | solution.py:355
  82.7 1.4 %diag_operand.1 = (f32[1,32,256]{2,1,0:T(8,128)}, f32[4,40,128]{2,1,0:T(8,128)S(1)}) custom-call(s32[1,64]{1,0:T(1,128)S(1)} %copy-done.5, f32[1,256,512]{2,1,0:T(8,128)S(1)} %copy-done, f32[16,40,128]{2,1,0:T(8,128)S(1)} %all_to_all.25.got, f32[8,128]{1,0:T(8,128)S(1)} %get-tuple-element.20.cross_pair, f32[64,128]{1,0:T(8,128)S(1)} %get-tuple-element.21.stride), custom_call_target="tpu_custom_call" | custom-call | tf_op jit(solution)/shard_map/diag_operand/pallas_call | solution.py:226
  84.1 8.1 %all_to_all.26.got = f32[4,40,128]{2,1,0:T(8,128)S(1)} all-to-all(f32[4,40,128]{2,1,0:T(8,128)S(1)} %get-tuple-element.23), channel_id=1, replica_groups={{0,128,256,384},{16,144,272,400},{32,160,288,416},{48,176,304,432},{64,..., dimensions={0} | all-to-all | bytes 163840 | tf_op jit(solution)/shard_map/all_to_all | solution.py:359
  92.3 14.3 %all_to_all.27.got = f32[8,48,128]{2,1,0:T(8,128)S(1)} all-to-all(f32[8,48,128]{2,1,0:T(8,128)S(1)} %middle_operand.1), channel_id=1, replica_groups={{0,16,32,48,64,80,96,112},{128,144,160,176,192,208,224,240},{256,272,28..., dimensions={0} | all-to-all | bytes 393216 | tf_op jit(solution)/shard_map/all_to_all | solution.py:360
  106.5 0.7 total_operand.1
  107.2 3.3 %all-to-all-start.4 = ((f32[4,32,128]{2,1,0:T(8,128)}), f32[4,32,128]{2,1,0:T(8,128)S(1)}, u32[]{:S(2)}, u32[]{:S(2)}) async-start(f32[4,32,128]{2,1,0:T(8,128)} %get-tuple-element.26), calls=%async_computation.4 | async-start | bytes 131072 | tf_op jit(solution)/shard_map/all_to_all | solution.py:362
  110.5 6.4 %collective-permute-start.5 = (f32[32,256]{1,0:T(8,128)S(1)}, f32[32,256]{1,0:T(8,128)S(1)}, u32[]{:S(2)}, u32[]{:S(2)}) collective-permute-start(f32[32,256]{1,0:T(8,128)S(1)} %get-tuple-element.25), channel_id=1, source_target_pairs={{0,1},{1,0},{2,3},{3,2},{4,5},{5,4},{6,7},{7,6},{8,9},{9,8},{10,11... | collective-permute-start | bytes 98312 | tf_op jit(solution)/shard_map/ppermute | solution.py:363
  117.0 0.8 collective-permute-done.5.taken
  117.8 0.0 copy-start.4
  117.8 1.4 %cross_lines.1 = f32[1,32,512]{2,1,0:T(8,128)} custom-call(f32[32,256]{1,0:T(8,128)S(1)} %get-tuple-element.24.keep, f32[32,256]{1,0:T(8,128)S(1)} %collective-permute-done.5.taken), custom_call_target="tpu_custom_call" | custom-call | tf_op jit(solution)/shard_map/cross_lines/pallas_call | solution.py:301
  119.2 0.0 all-to-all-done.4.got
  119.3 0.0 copy-done.4
  119.3 0.6 last_step.1
  (3 shorter events, 0.1 us)
Async XLA Ops:
  0.6 13.6 %copy-start.5 = (s32[1,64]{1,0:T(1,128)S(1)}, s32[1,64]{1,0:T(1,128)}, u32[]{:S(2)}) copy-start(s32[1,64]{1,0:T(1,128)} %slots.5) | copy-start | bytes 772
  0.6 13.6 %copy-start.1 = (f32[1,16,512]{2,1,0:T(8,128)S(1)}, f32[1,16,512]{2,1,0:T(8,128)}, u32[]{:S(2)}) copy-start(f32[1,16,512]{2,1,0:T(8,128)} %prev.5) | copy-start | bytes 98308
  0.7 13.6 %copy-start = (f32[1,256,512]{2,1,0:T(8,128)S(1)}, f32[1,256,512]{2,1,0:T(8,128)}, u32[]{:S(2)}) copy-start(f32[1,256,512]{2,1,0:T(8,128)} %panel.5) | copy-start | bytes 1572868
  0.7 13.6 %copy-start.2 = (f32[32,256]{1,0:T(8,128)S(1)}, f32[32,256]{1,0:T(8,128)}, u32[]{:S(2)}) copy-start(f32[32,256]{1,0:T(8,128)} %top_column) | copy-start | bytes 98308
  2.7 17.5 %collective-permute-start = (f32[40,256]{1,0:T(8,128)}, f32[40,256]{1,0:T(8,128)S(1)}, u32[]{:S(2)}, u32[]{:S(2)}) collective-permute-start(f32[40,256]{1,0:T(8,128)} %own_piece.1), channel_id=1, source_target_pairs={{0,64},{1,65},{2,80},{3,81},{4,96},{5,97},{6,112},{7,113},{8,0},{9... | collective-permute-start | bytes 122888 | tf_op jit(solution)/shard_map/ppermute | solution.py:335
  14.2 0.8 copy-start.3
  16.5 3.7 %collective-permute-start.1 = (f32[32,256]{1,0:T(8,128)S(1)}, f32[32,256]{1,0:T(8,128)S(1)}, u32[]{:S(2)}, u32[]{:S(2)}) collective-permute-start(f32[32,256]{1,0:T(8,128)S(1)} %get-tuple-element.18), channel_id=1, source_target_pairs={{0,1},{1,0},{2,3},{3,2},{4,5},{5,4},{6,7},{7,6},{8,9},{9,8},{10,11... | collective-permute-start | bytes 98312 | tf_op jit(solution)/shard_map/ppermute | solution.py:342
  21.1 14.2 %copy-start.6 = (f32[256,512]{1,0:T(8,128)S(1)}, f32[256,512]{1,0:T(8,128)}, u32[]{:S(2)}) copy-start(f32[256,512]{1,0:T(8,128)} %param.7) | copy-start | bytes 1572868
  21.1 40.8 %all-to-all-start = ((f32[32,40,128]{2,1,0:T(8,128)}), f32[32,40,128]{2,1,0:T(8,128)S(1)}, u32[]{:S(2)}, u32[]{:S(2)}) async-start(f32[32,40,128]{2,1,0:T(8,128)} %gather_operand.1), calls=%async_computation | async-start | bytes 1310720 | tf_op jit(solution)/shard_map/all_to_all | solution.py:345
  35.4 21.8 %collective-permute-start.3 = (f32[272,512]{1,0:T(8,128)S(1)}, f32[272,512]{1,0:T(8,128)S(1)}, u32[]{:S(2)}, u32[]{:S(2)}) collective-permute-start(f32[272,512]{1,0:T(8,128)S(1)} %maximum_maximum_fusion.mine), channel_id=1, source_target_pairs={{0,128},{16,144},{32,160},{48,176},{64,192},{80,208},{96,224},{112... | collective-permute-start | bytes 1671176 | tf_op jit(solution)/shard_map/ppermute | solution.py:338
  38.6 21.8 %collective-permute-start.2 = (f32[272,512]{1,0:T(8,128)S(1)}, f32[272,512]{1,0:T(8,128)S(1)}, u32[]{:S(2)}, u32[]{:S(2)}) collective-permute-start(f32[272,512]{1,0:T(8,128)S(1)} %maximum_maximum_fusion.mine), channel_id=1, source_target_pairs={{0,1},{1,0},{2,3},{3,2},{4,5},{5,4},{6,7},{7,6},{8,9},{9,8},{10,11... | collective-permute-start | bytes 1671176 | tf_op jit(solution)/shard_map/ppermute | solution.py:339
  57.2 4.7 %collective-permute-start.4 = (f32[272,512]{1,0:T(8,128)S(1)}, f32[272,512]{1,0:T(8,128)S(1)}, u32[]{:S(2)}, u32[]{:S(2)}) collective-permute-start(f32[272,512]{1,0:T(8,128)S(1)} %collective-permute-done.3.next_x), channel_id=1, source_target_pairs={{0,1},{1,0},{2,3},{3,2},{4,5},{5,4},{6,7},{7,6},{8,9},{9,8},{10,11... | collective-permute-start | bytes 1671176 | tf_op jit(solution)/shard_map/ppermute | solution.py:346
  107.2 12.0 %all-to-all-start.4 = ((f32[4,32,128]{2,1,0:T(8,128)}), f32[4,32,128]{2,1,0:T(8,128)S(1)}, u32[]{:S(2)}, u32[]{:S(2)}) async-start(f32[4,32,128]{2,1,0:T(8,128)} %get-tuple-element.26), calls=%async_computation.4 | async-start | bytes 131072 | tf_op jit(solution)/shard_map/all_to_all | solution.py:362
  110.5 7.3 %collective-permute-start.5 = (f32[32,256]{1,0:T(8,128)S(1)}, f32[32,256]{1,0:T(8,128)S(1)}, u32[]{:S(2)}, u32[]{:S(2)}) collective-permute-start(f32[32,256]{1,0:T(8,128)S(1)} %get-tuple-element.25), channel_id=1, source_target_pairs={{0,1},{1,0},{2,3},{3,2},{4,5},{5,4},{6,7},{7,6},{8,9},{9,8},{10,11... | collective-permute-start | bytes 98312 | tf_op jit(solution)/shard_map/ppermute | solution.py:363
  117.8 1.4 %copy-start.4 = (f32[1,32,512]{2,1,0:T(8,128)S(1)}, f32[1,32,512]{2,1,0:T(8,128)}, u32[]{:S(2)}) copy-start(f32[1,32,512]{2,1,0:T(8,128)} %pivot.1) | copy-start | bytes 196612

commit v10 on v7

--- a/solution.py
+++ b/solution.py
@@ -19,13 +19,25 @@
     return (row // 8) % 2
 
 
+def piece_of(row, col):
+    d = (col // 2 + 8 - row // 4) % 8
+    x = (row // 8 + ((0xEC46 >> (2 * d)) & 3)) % 4
+    far = (0x87 >> d) & 1
+    near_e = 1 - (row % 4) // 2
+    return 2 * x + (near_e + far) % 2
+
+
+def holder_of(y, q, x):
+    return 8 * x + (4 * (y % 2) + 6 + 2 * q) % 8
+
+
 def spread_pairs():
     pairs = []
     for row in range(ROWS):
         for col in range(COLS):
-            y, q, z = row // 4, row % 4, row % 8
-            t = (col // 2 - y - 4 + z) % 8
-            pairs.append((row * COLS + col, (8 * q + t) * COLS + 2 * y + col % 2))
+            t = piece_of(row, col)
+            target = holder_of(row // 4, row % 4, t // 2) + t % 2
+            pairs.append((row * COLS + col, target * COLS + 2 * (row // 4) + col % 2))
     return pairs
 
 
@@ -43,7 +55,7 @@
 def piece_kernel(slots, panel, prev, out, ids, buffer, rows, sems):
     row = lax.axis_index("prow")
     col = lax.axis_index("pcol")
-    piece = (col // 2 + 16 - row // 4 - 4 + row % 8) % 8
+    piece = piece_of(row, col)
     offset = 32 * (piece % 4)
     copies = [
         pltpu.make_async_copy(panel.at[0, pl.ds(BLK * k + offset, 32), :], buffer.at[k], sems.at[k]) for k in range(2)
@@ -146,16 +158,21 @@
     )(spread, cross_own, cross_other, prev_panel)
 
 
-def product_kernel(got, mine, mine_b, next_x, next_xb, out, cross_pair, stride, prev_rows):
-    row = lax.axis_index("prow")
-    core = lax.axis_index("pcol") % 2
+def product_kernel(got, mine, mine_b, next_x, next_xb, out, cross_pair, stride, prev_rows, pieces):
+    row = lax.axis_index("prow")
+    core = lax.axis_index("pcol") % 2
+    y = lax.axis_index("pcol") // 2
     half = half_of(row)
     strided = row // 16
     for k in range(COLS):
         stride[4 * k : 4 * k + 4, :] = got[2 * k + strided, 32:36, :]
-        prev_rows[4 * k : 4 * k + 4, :] = got[2 * k + 1 - strided, 32:36, :]
-    own = got[pl.ds(16 * core, 16), :32, :].reshape(512, 128)
-    other = got[pl.ds(16 - 16 * core, 16), :32, :].reshape(512, 128)
+    for q in range(4):
+        for x in range(4):
+            at = holder_of(y, q, x)
+            prev_rows[16 * q + 4 * x : 16 * q + 4 * x + 4, :] = got[at + 1 - strided, 32:36, :]
+            pieces[256 * q + 64 * x : 256 * q + 64 * x + 64, :] = got[pl.ds(at, 2), :32, :].reshape(64, 128)
+    own = pieces[pl.ds(pl.multiple_of(512 * core, 512), 512), :]
+    other = pieces[pl.ds(pl.multiple_of(512 - 512 * core, 512), 512), :]
     own_prev = prev_rows[pl.ds(pl.multiple_of(32 * core, 32), 32), :]
     other_prev = prev_rows[pl.ds(pl.multiple_of(32 - 32 * core, 32), 32), :]
     prev = jnp.concatenate([own_prev, other_prev], 0)
@@ -167,10 +184,10 @@
         top = jnp.concatenate([left[256:, :256], left[256:, 256:], right[256:, :256], right[256:, 256:]], 0)
         part = dot(left[:256, :], own) + dot(right[:256, :], other) + dot(top.T, prev)
         part = part.T
-        for y in range(YS):
-            out[2 * y + which, :16, :] = part[16 * y : 16 * y + 16, :128]
-            out[2 * y + which, 16:32, :] = part[16 * y : 16 * y + 16, 128:]
-            out[2 * y + which, 32:, :] = cross
+        for k in range(YS):
+            out[2 * k + which, :16, :] = part[16 * k : 16 * k + 16, :128]
+            out[2 * k + which, 16:32, :] = part[16 * k : 16 * k + 16, 128:]
+            out[2 * k + which, 32:, :] = cross
 
 
 def column_product(got, mine, mine_b, next_x, next_xb):
@@ -183,7 +200,7 @@
         ),
         in_specs=[pl.BlockSpec(memory_space=pltpu.VMEM)] * 5,
         out_specs=(pl.BlockSpec(memory_space=pltpu.VMEM),) * 3,
-        scratch_shapes=[pltpu.VMEM((64, 128), jnp.float32)],
+        scratch_shapes=[pltpu.VMEM((64, 128), jnp.float32), pltpu.VMEM((1024, 128), jnp.float32)],
         compiler_params=kernel_params,
         name="column_product",
     )(got, mine, mine_b, next_x, next_xb)

time: 118 us -> 115 us (0.975)
  starting transfers between devices: 40.8 us -> 38.4 us
  blocking collectives: 38.5 us -> 37.2 us
    all_to_all x1, starting transfers between devices: 17.9 us -> 9.05 us  [step(): got = lax.all_to_all(send, 'prow', 0, 0, tiled=True)]
    ppermute x1, starting transfers between devices: 8.09 us -> 14.5 us  [step(): spread = lax.ppermute(sent, ('prow', 'pcol'), spread_pairs())]
    all_to_all x1, blocking collectives: 19.7 us -> 18.3 us  [step(): lax.all_to_all(send, ('prow', 'pcol'), 0, 0, tiled=True, axis_index_group...]
  transfers between devices with their start and end apart: 8 -> 8, of which waited for: 5 -> 5; matrix products, arithmetic and copies ran while one was open for 0% -> 0% of each run, Pallas kernels for 2% -> 3%
where the time goes in v10:
time: 115 us; the launch traced here: 114 us
  starting transfers between devices  38.4 us (33%)
  blocking collectives  37.2 us (32%)
  waiting for transfers between devices  25.9 us (23%)
  Pallas kernels  10.9 us (9%)
    all_to_all x1, blocking collectives, step(): got = lax.all_to_all(send, 'prow', 0, 0, tiled=True)  18.9 us
    all_to_all x1, blocking collectives, step(): lax.all_to_all(send, ('prow', 'pcol'), 0, 0, tiled=True, axis_index_group...  18.3 us
    ppermute x1, waiting for transfers between devices, step(): blocks_x = lax.ppermute(blocks, 'prow', row_swap)  17.2 us
    ppermute x1, starting transfers between devices, step(): spread = lax.ppermute(sent, ('prow', 'pcol'), spread_pairs())  14.5 us
    all_to_all x1, starting transfers between devices, step(): got = lax.all_to_all(send, 'prow', 0, 0, tiled=True)  9.05 us
    all_to_all x1, starting transfers between devices, step(): got = lax.all_to_all(total, 'prow', 0, 0, tiled=True)  4.96 us
    all_to_all x1, waiting for transfers between devices, step(): got = lax.all_to_all(total, 'prow', 0, 0, tiled=True)  4.35 us
  transfers between devices with their start and end apart: 8, of which 5 were waited for; matrix products, arithmetic and copies ran while one was open for 0% of the time, Pallas kernels for 3%

profile of v10, /device:TPU:2, one launch (start us, length us, event | category | flops | bytes accessed | tf_op | source)
XLA Modules:
  0.0 114.0 jit_solution(4039664941215466420)
XLA Ops:
  0.6 0.0 copy-start.5
  0.6 0.0 copy-start.1
  0.7 0.0 copy-start
  0.7 0.0 copy-start.2
  0.7 2.1 %own_piece.1 = f32[40,256]{1,0:T(8,128)} custom-call(s32[1,64]{1,0:T(1,128)} %slots.5, f32[1,256,512]{2,1,0:T(8,128)} %panel.5, f32[1,16,512]{2,1,0:T(8,128)} %prev.5), custom_call_target="tpu_custom_call" | custom-call | tf_op jit(solution)/shard_map/own_piece/pallas_call | solution.py:79
  2.7 14.5 %collective-permute-start = (f32[40,256]{1,0:T(8,128)}, f32[40,256]{1,0:T(8,128)S(1)}, u32[]{:S(2)}, u32[]{:S(2)}) collective-permute-start(f32[40,256]{1,0:T(8,128)} %own_piece.1), channel_id=1, source_target_pairs={{0,352},{1,353},{2,224},{3,225},{4,96},{5,97},{6,240},{7,241},{8,1... | collective-permute-start | bytes 122888 | tf_op jit(solution)/shard_map/ppermute | solution.py:330
  17.3 0.0 copy-done.5
  17.3 0.0 copy-done.1
  17.3 0.0 copy-done
  17.3 0.0 copy-done.2
  17.3 0.0 copy-start.3
  17.3 0.8 copy-done.3
  18.2 1.4 %cross_rows.1 = (f32[32,256]{1,0:T(8,128)S(1)}, f32[32,256]{1,0:T(8,128)S(1)}) custom-call(s32[1,64]{1,0:T(1,128)S(1)} %copy-done.5, f32[1,256,512]{2,1,0:T(8,128)S(1)} %copy-done, f32[32,256]{1,0:T(8,128)S(1)} %copy-done.2, f32[32,512]{1,0:T(8,128)S(1)} %copy-done.3, f32[1,16,512]{2,1,0:T(8,128)S(1)} %copy-done.1), custom_call_target="tpu_custom_call" | custom-call | tf_op jit(solution)/shard_map/cross_rows/pallas_call | solution.py:115
  19.6 1.9 %collective-permute-start.1 = (f32[32,256]{1,0:T(8,128)S(1)}, f32[32,256]{1,0:T(8,128)S(1)}, u32[]{:S(2)}, u32[]{:S(2)}) collective-permute-start(f32[32,256]{1,0:T(8,128)S(1)} %get-tuple-element.18), channel_id=1, source_target_pairs={{0,1},{1,0},{2,3},{3,2},{4,5},{5,4},{6,7},{7,6},{8,9},{9,8},{10,11... | collective-permute-start | bytes 98312 | tf_op jit(solution)/shard_map/ppermute | solution.py:337
  21.5 1.2 %collective-permute-done.1.cross_other = f32[32,256]{1,0:T(8,128)S(1)} collective-permute-done((f32[32,256]{1,0:T(8,128)S(1)}, f32[32,256]{1,0:T(8,128)S(1)}, u32[]{:S(2)}, u32[]{:S(2)}) %collective-permute-start.1) | collective-permute-done | bytes 32800 | tf_op jit(solution)/shard_map/ppermute | solution.py:337
  22.7 0.0 collective-permute-done.spread
  22.7 0.9 gather_operand.1
  23.6 0.0 copy-start.6
  23.6 9.0 %all-to-all-start = ((f32[32,40,128]{2,1,0:T(8,128)}), f32[32,40,128]{2,1,0:T(8,128)S(1)}, u32[]{:S(2)}, u32[]{:S(2)}) async-start(f32[32,40,128]{2,1,0:T(8,128)} %gather_operand.1), calls=%async_computation | async-start | bytes 1310720 | tf_op jit(solution)/shard_map/all_to_all | solution.py:340
  32.7 0.0 copy-done.6
  32.7 2.1 %collective-permute-start.3 = (f32[272,512]{1,0:T(8,128)S(1)}, f32[272,512]{1,0:T(8,128)S(1)}, u32[]{:S(2)}, u32[]{:S(2)}) collective-permute-start(f32[272,512]{1,0:T(8,128)S(1)} %maximum_maximum_fusion.mine), channel_id=1, source_target_pairs={{0,128},{16,144},{32,160},{48,176},{64,192},{80,208},{96,224},{112... | collective-permute-start | bytes 1671176 | tf_op jit(solution)/shard_map/ppermute | solution.py:333
  34.9 1.9 %collective-permute-start.2 = (f32[272,512]{1,0:T(8,128)S(1)}, f32[272,512]{1,0:T(8,128)S(1)}, u32[]{:S(2)}, u32[]{:S(2)}) collective-permute-start(f32[272,512]{1,0:T(8,128)S(1)} %maximum_maximum_fusion.mine), channel_id=1, source_target_pairs={{0,1},{1,0},{2,3},{3,2},{4,5},{5,4},{6,7},{7,6},{8,9},{9,8},{10,11... | collective-permute-start | bytes 1671176 | tf_op jit(solution)/shard_map/ppermute | solution.py:334
  36.8 17.2 %collective-permute-done.3.next_x = f32[272,512]{1,0:T(8,128)S(1)} collective-permute-done((f32[272,512]{1,0:T(8,128)S(1)}, f32[272,512]{1,0:T(8,128)S(1)}, u32[]{:S(2)}, u32[]{:S(2)}) %collective-permute-start.3) | collective-permute-done | bytes 557088 | tf_op jit(solution)/shard_map/ppermute | solution.py:333
  54.1 1.9 %collective-permute-start.4 = (f32[272,512]{1,0:T(8,128)S(1)}, f32[272,512]{1,0:T(8,128)S(1)}, u32[]{:S(2)}, u32[]{:S(2)}) collective-permute-start(f32[272,512]{1,0:T(8,128)S(1)} %collective-permute-done.3.next_x), channel_id=1, source_target_pairs={{0,1},{1,0},{2,3},{3,2},{4,5},{5,4},{6,7},{7,6},{8,9},{9,8},{10,11... | collective-permute-start | bytes 1671176 | tf_op jit(solution)/shard_map/ppermute | solution.py:341
  56.0 0.0 collective-permute-done.2.mine_b
  56.0 1.9 %collective-permute-done.4.next_xb = f32[272,512]{1,0:T(8,128)S(1)} collective-permute-done((f32[272,512]{1,0:T(8,128)S(1)}, f32[272,512]{1,0:T(8,128)S(1)}, u32[]{:S(2)}, u32[]{:S(2)}) %collective-permute-start.4) | collective-permute-done | bytes 557088 | tf_op jit(solution)/shard_map/ppermute | solution.py:341
  57.9 0.0 all-to-all-done.got
  57.9 2.2 %column_product.1 = (f32[16,40,128]{2,1,0:T(8,128)S(1)}, f32[8,128]{1,0:T(8,128)S(1)}, f32[64,128]{1,0:T(8,128)S(1)}) custom-call(f32[32,40,128]{2,1,0:T(8,128)S(1)} %all-to-all-done.got, f32[272,512]{1,0:T(8,128)S(1)} %maximum_maximum_fusion.mine, f32[272,512]{1,0:T(8,128)S(1)} %collective-permute-done.2.mine_b, ...), custom_call_target="tpu_custom_call" | custom-call | tf_op jit(solution)/shard_map/column_product/pallas_call | solution.py:194
  60.1 18.3 %all_to_all.20.got = f32[16,40,128]{2,1,0:T(8,128)S(1)} all-to-all(f32[16,40,128]{2,1,0:T(8,128)S(1)} %get-tuple-element.19), channel_id=1, replica_groups={{0,128,2,130,4,132,6,134,8,136,10,138,12,140,14,142},{1,129,3,131,5,133..., dimensions={0} | all-to-all | bytes 655360 | tf_op jit(solution)/shard_map/all_to_all | solution.py:350
  78.4 1.4 %diag_operand.1 = (f32[1,32,256]{2,1,0:T(8,128)}, f32[32,8,128]{2,1,0:T(8,128)S(1)}) custom-call(s32[1,64]{1,0:T(1,128)S(1)} %copy-done.5, f32[1,256,512]{2,1,0:T(8,128)S(1)} %copy-done, f32[16,40,128]{2,1,0:T(8,128)S(1)} %all_to_all.20.got, f32[8,128]{1,0:T(8,128)S(1)} %get-tuple-element.20.cross_pair, f32[64,128]{1,0:T(8,128)S(1)} %get-tuple-element.21.stride), custom_call_target="tpu_custom_call" | custom-call | tf_op jit(solution)/shard_map/diag_operand/pallas_call | solution.py:243
  79.8 18.9 %all_to_all.21.got = f32[32,8,128]{2,1,0:T(8,128)S(1)} all-to-all(f32[32,8,128]{2,1,0:T(8,128)S(1)} %get-tuple-element.23), channel_id=1, replica_groups=mesh['prow'=32,'pcol'=16] {'prow'}, dimensions={0} | all-to-all | bytes 262144 | tf_op jit(solution)/shard_map/all_to_all | solution.py:352
  98.7 0.7 total_operand.1
  99.4 5.0 %all-to-all-start.3 = ((f32[32,4,128]{2,1,0:T(4,128)}), f32[32,4,128]{2,1,0:T(4,128)S(1)}, u32[]{:S(2)}, u32[]{:S(2)}) async-start(f32[32,4,128]{2,1,0:T(4,128)} %get-tuple-element.26), calls=%async_computation.3 | async-start | bytes 131072 | tf_op jit(solution)/shard_map/all_to_all | solution.py:354
  104.4 1.9 %collective-permute-start.5 = (f32[32,256]{1,0:T(8,128)S(1)}, f32[32,256]{1,0:T(8,128)S(1)}, u32[]{:S(2)}, u32[]{:S(2)}) collective-permute-start(f32[32,256]{1,0:T(8,128)S(1)} %get-tuple-element.25), channel_id=1, source_target_pairs={{0,1},{1,0},{2,3},{3,2},{4,5},{5,4},{6,7},{7,6},{8,9},{9,8},{10,11... | collective-permute-start | bytes 98312 | tf_op jit(solution)/shard_map/ppermute | solution.py:355
  106.3 1.2 %collective-permute-done.5.taken = f32[32,256]{1,0:T(8,128)S(1)} collective-permute-done((f32[32,256]{1,0:T(8,128)S(1)}, f32[32,256]{1,0:T(8,128)S(1)}, u32[]{:S(2)}, u32[]{:S(2)}) %collective-permute-start.5) | collective-permute-done | bytes 32800 | tf_op jit(solution)/shard_map/ppermute | solution.py:355
  107.5 0.0 copy-start.4
  107.5 1.4 %cross_lines.1 = f32[1,32,512]{2,1,0:T(8,128)} custom-call(f32[32,256]{1,0:T(8,128)S(1)} %get-tuple-element.24.keep, f32[32,256]{1,0:T(8,128)S(1)} %collective-permute-done.5.taken), custom_call_target="tpu_custom_call" | custom-call | tf_op jit(solution)/shard_map/cross_lines/pallas_call | solution.py:296
  108.9 4.4 %all-to-all-done.3.got = f32[32,4,128]{2,1,0:T(4,128)S(1)} async-done(((f32[32,4,128]{2,1,0:T(4,128)}), f32[32,4,128]{2,1,0:T(4,128)S(1)}, u32[]{:S(2)}, u32[]{:S(2)}) %all-to-all-start.3) | async-done | bytes 65568 | tf_op jit(solution)/shard_map/all_to_all | solution.py:354
  113.3 0.0 copy-done.4
  113.3 0.7 last_step.1
  (2 shorter events, 0.0 us)
Async XLA Ops:
  0.6 16.6 %copy-start.5 = (s32[1,64]{1,0:T(1,128)S(1)}, s32[1,64]{1,0:T(1,128)}, u32[]{:S(2)}) copy-start(s32[1,64]{1,0:T(1,128)} %slots.5) | copy-start | bytes 772
  0.6 16.6 %copy-start.1 = (f32[1,16,512]{2,1,0:T(8,128)S(1)}, f32[1,16,512]{2,1,0:T(8,128)}, u32[]{:S(2)}) copy-start(f32[1,16,512]{2,1,0:T(8,128)} %prev.5) | copy-start | bytes 98308
  0.7 16.6 %copy-start = (f32[1,256,512]{2,1,0:T(8,128)S(1)}, f32[1,256,512]{2,1,0:T(8,128)}, u32[]{:S(2)}) copy-start(f32[1,256,512]{2,1,0:T(8,128)} %panel.5) | copy-start | bytes 1572868
  0.7 16.6 %copy-start.2 = (f32[32,256]{1,0:T(8,128)S(1)}, f32[32,256]{1,0:T(8,128)}, u32[]{:S(2)}) copy-start(f32[32,256]{1,0:T(8,128)} %top_column) | copy-start | bytes 98308
  2.7 19.9 %collective-permute-start = (f32[40,256]{1,0:T(8,128)}, f32[40,256]{1,0:T(8,128)S(1)}, u32[]{:S(2)}, u32[]{:S(2)}) collective-permute-start(f32[40,256]{1,0:T(8,128)} %own_piece.1), channel_id=1, source_target_pairs={{0,352},{1,353},{2,224},{3,225},{4,96},{5,97},{6,240},{7,241},{8,1... | collective-permute-start | bytes 122888 | tf_op jit(solution)/shard_map/ppermute | solution.py:330
  17.3 0.8 copy-start.3
  19.6 3.1 %collective-permute-start.1 = (f32[32,256]{1,0:T(8,128)S(1)}, f32[32,256]{1,0:T(8,128)S(1)}, u32[]{:S(2)}, u32[]{:S(2)}) collective-permute-start(f32[32,256]{1,0:T(8,128)S(1)} %get-tuple-element.18), channel_id=1, source_target_pairs={{0,1},{1,0},{2,3},{3,2},{4,5},{5,4},{6,7},{7,6},{8,9},{9,8},{10,11... | collective-permute-start | bytes 98312 | tf_op jit(solution)/shard_map/ppermute | solution.py:337
  23.6 9.1 %copy-start.6 = (f32[256,512]{1,0:T(8,128)S(1)}, f32[256,512]{1,0:T(8,128)}, u32[]{:S(2)}) copy-start(f32[256,512]{1,0:T(8,128)} %param.7) | copy-start | bytes 1572868
  23.6 34.3 %all-to-all-start = ((f32[32,40,128]{2,1,0:T(8,128)}), f32[32,40,128]{2,1,0:T(8,128)S(1)}, u32[]{:S(2)}, u32[]{:S(2)}) async-start(f32[32,40,128]{2,1,0:T(8,128)} %gather_operand.1), calls=%async_computation | async-start | bytes 1310720 | tf_op jit(solution)/shard_map/all_to_all | solution.py:340
  32.7 21.3 %collective-permute-start.3 = (f32[272,512]{1,0:T(8,128)S(1)}, f32[272,512]{1,0:T(8,128)S(1)}, u32[]{:S(2)}, u32[]{:S(2)}) collective-permute-start(f32[272,512]{1,0:T(8,128)S(1)} %maximum_maximum_fusion.mine), channel_id=1, source_target_pairs={{0,128},{16,144},{32,160},{48,176},{64,192},{80,208},{96,224},{112... | collective-permute-start | bytes 1671176 | tf_op jit(solution)/shard_map/ppermute | solution.py:333
  34.9 21.1 %collective-permute-start.2 = (f32[272,512]{1,0:T(8,128)S(1)}, f32[272,512]{1,0:T(8,128)S(1)}, u32[]{:S(2)}, u32[]{:S(2)}) collective-permute-start(f32[272,512]{1,0:T(8,128)S(1)} %maximum_maximum_fusion.mine), channel_id=1, source_target_pairs={{0,1},{1,0},{2,3},{3,2},{4,5},{5,4},{6,7},{7,6},{8,9},{9,8},{10,11... | collective-permute-start | bytes 1671176 | tf_op jit(solution)/shard_map/ppermute | solution.py:334
  54.1 3.8 %collective-permute-start.4 = (f32[272,512]{1,0:T(8,128)S(1)}, f32[272,512]{1,0:T(8,128)S(1)}, u32[]{:S(2)}, u32[]{:S(2)}) collective-permute-start(f32[272,512]{1,0:T(8,128)S(1)} %collective-permute-done.3.next_x), channel_id=1, source_target_pairs={{0,1},{1,0},{2,3},{3,2},{4,5},{5,4},{6,7},{7,6},{8,9},{9,8},{10,11... | collective-permute-start | bytes 1671176 | tf_op jit(solution)/shard_map/ppermute | solution.py:341
  99.4 13.9 %all-to-all-start.3 = ((f32[32,4,128]{2,1,0:T(4,128)}), f32[32,4,128]{2,1,0:T(4,128)S(1)}, u32[]{:S(2)}, u32[]{:S(2)}) async-start(f32[32,4,128]{2,1,0:T(4,128)} %get-tuple-element.26), calls=%async_computation.3 | async-start | bytes 131072 | tf_op jit(solution)/shard_map/all_to_all | solution.py:354
  104.4 3.1 %collective-permute-start.5 = (f32[32,256]{1,0:T(8,128)S(1)}, f32[32,256]{1,0:T(8,128)S(1)}, u32[]{:S(2)}, u32[]{:S(2)}) collective-permute-start(f32[32,256]{1,0:T(8,128)S(1)} %get-tuple-element.25), channel_id=1, source_target_pairs={{0,1},{1,0},{2,3},{3,2},{4,5},{5,4},{6,7},{7,6},{8,9},{9,8},{10,11... | collective-permute-start | bytes 98312 | tf_op jit(solution)/shard_map/ppermute | solution.py:355
  107.5 5.8 %copy-start.4 = (f32[1,32,512]{2,1,0:T(8,128)S(1)}, f32[1,32,512]{2,1,0:T(8,128)}, u32[]{:S(2)}) copy-start(f32[1,32,512]{2,1,0:T(8,128)} %pivot.1) | copy-start | bytes 196612

commit v11 on v10

--- a/solution.py
+++ b/solution.py
@@ -52,7 +52,7 @@
     return jnp.dot(left, right, precision=highest, preferred_element_type=jnp.float32)
 
 
-def piece_kernel(slots, panel, prev, out, ids, buffer, rows, sems):
+def piece_kernel(slots, panel, prev, top_diag, out, diag_out, ids, buffer, rows, sems):
     row = lax.axis_index("prow")
     col = lax.axis_index("pcol")
     piece = piece_of(row, col)
@@ -62,6 +62,7 @@
     ]
     copies.append(pltpu.make_async_copy(prev.at[0], rows, sems.at[2]))
     copies.append(pltpu.make_async_copy(slots, ids, sems.at[3]))
+    copies.append(pltpu.make_async_copy(top_diag.at[:, pl.ds(BLK * (row // 8), BLK)], diag_out, sems.at[4]))
     for copy in copies:
         copy.start()
     wanted = 2 * row + piece // 4
@@ -75,20 +76,23 @@
     out[...] = dot(jnp.concatenate([chunk, rolled[:8]], 0), columns)
 
 
-def own_piece(slot_blocks, panel_blocks, prev_panel):
+def own_piece(slot_blocks, panel_blocks, prev_panel, top_diag):
     return pl.pallas_call(
         piece_kernel,
-        out_shape=jax.ShapeDtypeStruct((40, 256), jnp.float32),
-        in_specs=[pl.BlockSpec(memory_space=pltpu.HBM)] * 3,
-        out_specs=pl.BlockSpec(memory_space=pltpu.VMEM),
+        out_shape=(
+            jax.ShapeDtypeStruct((40, 256), jnp.float32),
+            jax.ShapeDtypeStruct((32, BLK), jnp.float32),
+        ),
+        in_specs=[pl.BlockSpec(memory_space=pltpu.HBM)] * 4,
+        out_specs=(pl.BlockSpec(memory_space=pltpu.VMEM),) * 2,
         scratch_shapes=[
             pltpu.SMEM((1, 64), jnp.int32),
             pltpu.VMEM((2, 32, 512), jnp.float32),
             pltpu.VMEM((16, 512), jnp.float32),
-            pltpu.SemaphoreType.DMA((4,)),
+            pltpu.SemaphoreType.DMA((5,)),
         ],
         name="own_piece",
-    )(slot_blocks, panel_blocks, prev_panel)
+    )(slot_blocks, panel_blocks, prev_panel, top_diag)
 
 
 def factor_halves(slots, panel, row):
@@ -103,7 +107,7 @@
     row = lax.axis_index("prow")
     core = lax.axis_index("pcol") % 2
     low, high = factor_halves(slots, panel, row)
-    diag = pltpu.roll(top_diag[...], (512 - 16 * row) % 512, 1)[:, :16]
+    diag = pltpu.roll(top_diag[...], (BLK - 16 * (row % 8)) % BLK, 1)[:, :16]
     part = dot(top_column[:, :BLK], low) + dot(top_column[:, BLK:], high) + dot(diag, prev[0])
     shifted = jnp.where(core == 0, pltpu.roll(part, 480, 1), pltpu.roll(part, 32, 1))
     both = dot(jnp.concatenate([part, shifted], 0), select_columns(core))
@@ -325,7 +329,7 @@
     core_swap = [(i, i ^ 1) for i in range(COLS)]
     row_swap = [(i, i ^ 8) for i in range(ROWS)]
 
-    sent = own_piece(slot_blocks, panel_blocks, prev_panel)
+    sent, diag_slice = own_piece(slot_blocks, panel_blocks, prev_panel, top_diag)
     sent, top_column = lax.optimization_barrier((sent, top_column))
     spread = lax.ppermute(sent, ("prow", "pcol"), spread_pairs())
 
@@ -333,7 +337,7 @@
     blocks_x = lax.ppermute(blocks, "prow", row_swap)
     blocks_b = lax.ppermute(blocks, "pcol", core_swap)
 
-    cross_own, cross_sent = cross_rows(slot_blocks, panel_blocks, top_column, top_diag, prev_panel)
+    cross_own, cross_sent = cross_rows(slot_blocks, panel_blocks, top_column, diag_slice, prev_panel)
     cross_other = lax.ppermute(cross_sent, "pcol", core_swap)
 
     send = gather_operand(spread, cross_own, cross_other, prev_panel)

time: 115 us -> 115 us (level)
  transfers between devices with their start and end apart: 8 -> 8, of which waited for: 5 -> 5; matrix products, arithmetic and copies ran while one was open for 0% -> 0% of each run, Pallas kernels for 3% -> 2%
where the time goes in v11:
time: 115 us; the launch traced here: 114 us
  starting transfers between devices  38.5 us (33%)
  blocking collectives  37.2 us (32%)
  waiting for transfers between devices  25.9 us (23%)
  Pallas kernels  10.9 us (9%)
    all_to_all x1, blocking collectives, step(): got = lax.all_to_all(send, 'prow', 0, 0, tiled=True)  18.9 us
    all_to_all x1, blocking collectives, step(): lax.all_to_all(send, ('prow', 'pcol'), 0, 0, tiled=True, axis_index_group...  18.3 us
    ppermute x1, waiting for transfers between devices, step(): blocks_x = lax.ppermute(blocks, 'prow', row_swap)  17.2 us
    ppermute x1, starting transfers between devices, step(): spread = lax.ppermute(sent, ('prow', 'pcol'), spread_pairs())  14.5 us
    all_to_all x1, starting transfers between devices, step(): got = lax.all_to_all(send, 'prow', 0, 0, tiled=True)  9.18 us
    all_to_all x1, starting transfers between devices, step(): got = lax.all_to_all(total, 'prow', 0, 0, tiled=True)  4.96 us
    all_to_all x1, waiting for transfers between devices, step(): got = lax.all_to_all(total, 'prow', 0, 0, tiled=True)  4.35 us
  transfers between devices with their start and end apart: 8, of which 5 were waited for; matrix products, arithmetic and copies ran while one was open for 0% of the time, Pallas kernels for 2%

profile of v11, /device:TPU:2, one launch (start us, length us, event | category | flops | bytes accessed | tf_op | source)
XLA Modules:
  0.0 114.0 jit_solution(7702221646216121037)
XLA Ops:
  0.6 0.0 copy-start.1
  0.6 0.0 copy-start
  0.7 0.0 copy-start.2
  0.7 2.1 %own_piece.1 = (f32[40,256]{1,0:T(8,128)}, f32[32,128]{1,0:T(8,128)}) custom-call(s32[1,64]{1,0:T(1,128)} %slots.5, f32[1,256,512]{2,1,0:T(8,128)} %panel.5, f32[1,16,512]{2,1,0:T(8,128)} %prev.5, f32[32,512]{1,0:T(8,128)} %top_diag.1), custom_call_target="tpu_custom_call" | custom-call | tf_op jit(solution)/shard_map/own_piece/pallas_call | solution.py:80
  2.7 0.0 copy-start.5
  2.7 14.5 %collective-permute-start = (f32[40,256]{1,0:T(8,128)}, f32[40,256]{1,0:T(8,128)S(1)}, u32[]{:S(2)}, u32[]{:S(2)}) collective-permute-start(f32[40,256]{1,0:T(8,128)} %get-tuple-element.18), channel_id=1, source_target_pairs={{0,352},{1,353},{2,224},{3,225},{4,96},{5,97},{6,240},{7,241},{8,1... | collective-permute-start | bytes 122888 | tf_op jit(solution)/shard_map/ppermute | solution.py:334
  17.3 0.0 copy-done.1
  17.3 0.0 copy-done
  17.3 0.0 copy-done.2
  17.3 0.0 copy-done.5
  17.3 0.0 copy-start.4
  17.3 0.7 copy-done.4
  18.0 1.4 %cross_rows.1 = (f32[32,256]{1,0:T(8,128)S(1)}, f32[32,256]{1,0:T(8,128)S(1)}) custom-call(s32[1,64]{1,0:T(1,128)S(1)} %copy-done.5, f32[1,256,512]{2,1,0:T(8,128)S(1)} %copy-done, f32[32,256]{1,0:T(8,128)S(1)} %copy-done.2, f32[32,128]{1,0:T(8,128)S(1)} %copy-done.4, f32[1,16,512]{2,1,0:T(8,128)S(1)} %copy-done.1), custom_call_target="tpu_custom_call" | custom-call | tf_op jit(solution)/shard_map/cross_rows/pallas_call | solution.py:119
  19.5 1.9 %collective-permute-start.1 = (f32[32,256]{1,0:T(8,128)S(1)}, f32[32,256]{1,0:T(8,128)S(1)}, u32[]{:S(2)}, u32[]{:S(2)}) collective-permute-start(f32[32,256]{1,0:T(8,128)S(1)} %get-tuple-element.22), channel_id=1, source_target_pairs={{0,1},{1,0},{2,3},{3,2},{4,5},{5,4},{6,7},{7,6},{8,9},{9,8},{10,11... | collective-permute-start | bytes 98312 | tf_op jit(solution)/shard_map/ppermute | solution.py:341
  21.4 1.2 %collective-permute-done.1.cross_other = f32[32,256]{1,0:T(8,128)S(1)} collective-permute-done((f32[32,256]{1,0:T(8,128)S(1)}, f32[32,256]{1,0:T(8,128)S(1)}, u32[]{:S(2)}, u32[]{:S(2)}) %collective-permute-start.1) | collective-permute-done | bytes 32800 | tf_op jit(solution)/shard_map/ppermute | solution.py:341
  22.6 0.0 collective-permute-done.spread
  22.6 1.0 gather_operand.1
  23.5 0.0 copy-start.6
  23.5 9.2 %all-to-all-start = ((f32[32,40,128]{2,1,0:T(8,128)}), f32[32,40,128]{2,1,0:T(8,128)S(1)}, u32[]{:S(2)}, u32[]{:S(2)}) async-start(f32[32,40,128]{2,1,0:T(8,128)} %gather_operand.1), calls=%async_computation | async-start | bytes 1310720 | tf_op jit(solution)/shard_map/all_to_all | solution.py:344
  32.7 0.0 copy-done.6
  32.8 2.1 %collective-permute-start.3 = (f32[272,512]{1,0:T(8,128)S(1)}, f32[272,512]{1,0:T(8,128)S(1)}, u32[]{:S(2)}, u32[]{:S(2)}) collective-permute-start(f32[272,512]{1,0:T(8,128)S(1)} %maximum_maximum_fusion.mine), channel_id=1, source_target_pairs={{0,128},{16,144},{32,160},{48,176},{64,192},{80,208},{96,224},{112... | collective-permute-start | bytes 1671176 | tf_op jit(solution)/shard_map/ppermute | solution.py:337
  34.9 1.9 %collective-permute-start.2 = (f32[272,512]{1,0:T(8,128)S(1)}, f32[272,512]{1,0:T(8,128)S(1)}, u32[]{:S(2)}, u32[]{:S(2)}) collective-permute-start(f32[272,512]{1,0:T(8,128)S(1)} %maximum_maximum_fusion.mine), channel_id=1, source_target_pairs={{0,1},{1,0},{2,3},{3,2},{4,5},{5,4},{6,7},{7,6},{8,9},{9,8},{10,11... | collective-permute-start | bytes 1671176 | tf_op jit(solution)/shard_map/ppermute | solution.py:338
  36.8 17.2 %collective-permute-done.3.next_x = f32[272,512]{1,0:T(8,128)S(1)} collective-permute-done((f32[272,512]{1,0:T(8,128)S(1)}, f32[272,512]{1,0:T(8,128)S(1)}, u32[]{:S(2)}, u32[]{:S(2)}) %collective-permute-start.3) | collective-permute-done | bytes 557088 | tf_op jit(solution)/shard_map/ppermute | solution.py:337
  54.1 1.9 %collective-permute-start.4 = (f32[272,512]{1,0:T(8,128)S(1)}, f32[272,512]{1,0:T(8,128)S(1)}, u32[]{:S(2)}, u32[]{:S(2)}) collective-permute-start(f32[272,512]{1,0:T(8,128)S(1)} %collective-permute-done.3.next_x), channel_id=1, source_target_pairs={{0,1},{1,0},{2,3},{3,2},{4,5},{5,4},{6,7},{7,6},{8,9},{9,8},{10,11... | collective-permute-start | bytes 1671176 | tf_op jit(solution)/shard_map/ppermute | solution.py:345
  56.0 0.0 collective-permute-done.2.mine_b
  56.0 1.9 %collective-permute-done.4.next_xb = f32[272,512]{1,0:T(8,128)S(1)} collective-permute-done((f32[272,512]{1,0:T(8,128)S(1)}, f32[272,512]{1,0:T(8,128)S(1)}, u32[]{:S(2)}, u32[]{:S(2)}) %collective-permute-start.4) | collective-permute-done | bytes 557088 | tf_op jit(solution)/shard_map/ppermute | solution.py:345
  57.9 0.0 all-to-all-done.got
  57.9 2.2 %column_product.1 = (f32[16,40,128]{2,1,0:T(8,128)S(1)}, f32[8,128]{1,0:T(8,128)S(1)}, f32[64,128]{1,0:T(8,128)S(1)}) custom-call(f32[32,40,128]{2,1,0:T(8,128)S(1)} %all-to-all-done.got, f32[272,512]{1,0:T(8,128)S(1)} %maximum_maximum_fusion.mine, f32[272,512]{1,0:T(8,128)S(1)} %collective-permute-done.2.mine_b, ...), custom_call_target="tpu_custom_call" | custom-call | tf_op jit(solution)/shard_map/column_product/pallas_call | solution.py:198
  60.1 18.3 %all_to_all.20.got = f32[16,40,128]{2,1,0:T(8,128)S(1)} all-to-all(f32[16,40,128]{2,1,0:T(8,128)S(1)} %get-tuple-element.23), channel_id=1, replica_groups={{0,128,2,130,4,132,6,134,8,136,10,138,12,140,14,142},{1,129,3,131,5,133..., dimensions={0} | all-to-all | bytes 655360 | tf_op jit(solution)/shard_map/all_to_all | solution.py:354
  78.4 1.4 %diag_operand.1 = (f32[1,32,256]{2,1,0:T(8,128)}, f32[32,8,128]{2,1,0:T(8,128)S(1)}) custom-call(s32[1,64]{1,0:T(1,128)S(1)} %copy-done.5, f32[1,256,512]{2,1,0:T(8,128)S(1)} %copy-done, f32[16,40,128]{2,1,0:T(8,128)S(1)} %all_to_all.20.got, f32[8,128]{1,0:T(8,128)S(1)} %get-tuple-element.24.cross_pair, f32[64,128]{1,0:T(8,128)S(1)} %get-tuple-element.25.stride), custom_call_target="tpu_custom_call" | custom-call | tf_op jit(solution)/shard_map/diag_operand/pallas_call | solution.py:247
  79.8 18.9 %all_to_all.21.got = f32[32,8,128]{2,1,0:T(8,128)S(1)} all-to-all(f32[32,8,128]{2,1,0:T(8,128)S(1)} %get-tuple-element.27), channel_id=1, replica_groups=mesh['prow'=32,'pcol'=16] {'prow'}, dimensions={0} | all-to-all | bytes 262144 | tf_op jit(solution)/shard_map/all_to_all | solution.py:356
  98.7 0.7 total_operand.1
  99.4 5.0 %all-to-all-start.3 = ((f32[32,4,128]{2,1,0:T(4,128)}), f32[32,4,128]{2,1,0:T(4,128)S(1)}, u32[]{:S(2)}, u32[]{:S(2)}) async-start(f32[32,4,128]{2,1,0:T(4,128)} %get-tuple-element.30), calls=%async_computation.3 | async-start | bytes 131072 | tf_op jit(solution)/shard_map/all_to_all | solution.py:358
  104.4 1.9 %collective-permute-start.5 = (f32[32,256]{1,0:T(8,128)S(1)}, f32[32,256]{1,0:T(8,128)S(1)}, u32[]{:S(2)}, u32[]{:S(2)}) collective-permute-start(f32[32,256]{1,0:T(8,128)S(1)} %get-tuple-element.29), channel_id=1, source_target_pairs={{0,1},{1,0},{2,3},{3,2},{4,5},{5,4},{6,7},{7,6},{8,9},{9,8},{10,11... | collective-permute-start | bytes 98312 | tf_op jit(solution)/shard_map/ppermute | solution.py:359
  106.3 1.2 %collective-permute-done.5.taken = f32[32,256]{1,0:T(8,128)S(1)} collective-permute-done((f32[32,256]{1,0:T(8,128)S(1)}, f32[32,256]{1,0:T(8,128)S(1)}, u32[]{:S(2)}, u32[]{:S(2)}) %collective-permute-start.5) | collective-permute-done | bytes 32800 | tf_op jit(solution)/shard_map/ppermute | solution.py:359
  107.5 0.0 copy-start.3
  107.5 1.4 %cross_lines.1 = f32[1,32,512]{2,1,0:T(8,128)} custom-call(f32[32,256]{1,0:T(8,128)S(1)} %get-tuple-element.28.keep, f32[32,256]{1,0:T(8,128)S(1)} %collective-permute-done.5.taken), custom_call_target="tpu_custom_call" | custom-call | tf_op jit(solution)/shard_map/cross_lines/pallas_call | solution.py:300
  108.9 4.4 %all-to-all-done.3.got = f32[32,4,128]{2,1,0:T(4,128)S(1)} async-done(((f32[32,4,128]{2,1,0:T(4,128)}), f32[32,4,128]{2,1,0:T(4,128)S(1)}, u32[]{:S(2)}, u32[]{:S(2)}) %all-to-all-start.3) | async-done | bytes 65568 | tf_op jit(solution)/shard_map/all_to_all | solution.py:358
  113.3 0.0 copy-done.3
  113.3 0.7 last_step.1
  (2 shorter events, 0.0 us)
Async XLA Ops:
  0.6 16.7 %copy-start.1 = (f32[1,16,512]{2,1,0:T(8,128)S(1)}, f32[1,16,512]{2,1,0:T(8,128)}, u32[]{:S(2)}) copy-start(f32[1,16,512]{2,1,0:T(8,128)} %prev.5) | copy-start | bytes 98308
  0.6 16.7 %copy-start = (f32[1,256,512]{2,1,0:T(8,128)S(1)}, f32[1,256,512]{2,1,0:T(8,128)}, u32[]{:S(2)}) copy-start(f32[1,256,512]{2,1,0:T(8,128)} %panel.5) | copy-start | bytes 1572868
  0.7 16.7 %copy-start.2 = (f32[32,256]{1,0:T(8,128)S(1)}, f32[32,256]{1,0:T(8,128)}, u32[]{:S(2)}) copy-start(f32[32,256]{1,0:T(8,128)} %top_column) | copy-start | bytes 98308
  2.7 14.6 %copy-start.5 = (s32[1,64]{1,0:T(1,128)S(1)}, s32[1,64]{1,0:T(1,128)}, u32[]{:S(2)}) copy-start(s32[1,64]{1,0:T(1,128)} %slots.5) | copy-start | bytes 772
  2.7 19.8 %collective-permute-start = (f32[40,256]{1,0:T(8,128)}, f32[40,256]{1,0:T(8,128)S(1)}, u32[]{:S(2)}, u32[]{:S(2)}) collective-permute-start(f32[40,256]{1,0:T(8,128)} %get-tuple-element.18), channel_id=1, source_target_pairs={{0,352},{1,353},{2,224},{3,225},{4,96},{5,97},{6,240},{7,241},{8,1... | collective-permute-start | bytes 122888 | tf_op jit(solution)/shard_map/ppermute | solution.py:334
  17.3 0.7 copy-start.4
  19.5 3.1 %collective-permute-start.1 = (f32[32,256]{1,0:T(8,128)S(1)}, f32[32,256]{1,0:T(8,128)S(1)}, u32[]{:S(2)}, u32[]{:S(2)}) collective-permute-start(f32[32,256]{1,0:T(8,128)S(1)} %get-tuple-element.22), channel_id=1, source_target_pairs={{0,1},{1,0},{2,3},{3,2},{4,5},{5,4},{6,7},{7,6},{8,9},{9,8},{10,11... | collective-permute-start | bytes 98312 | tf_op jit(solution)/shard_map/ppermute | solution.py:341
  23.5 9.2 %copy-start.6 = (f32[256,512]{1,0:T(8,128)S(1)}, f32[256,512]{1,0:T(8,128)}, u32[]{:S(2)}) copy-start(f32[256,512]{1,0:T(8,128)} %param.7) | copy-start | bytes 1572868
  23.5 34.4 %all-to-all-start = ((f32[32,40,128]{2,1,0:T(8,128)}), f32[32,40,128]{2,1,0:T(8,128)S(1)}, u32[]{:S(2)}, u32[]{:S(2)}) async-start(f32[32,40,128]{2,1,0:T(8,128)} %gather_operand.1), calls=%async_computation | async-start | bytes 1310720 | tf_op jit(solution)/shard_map/all_to_all | solution.py:344
  32.8 21.3 %collective-permute-start.3 = (f32[272,512]{1,0:T(8,128)S(1)}, f32[272,512]{1,0:T(8,128)S(1)}, u32[]{:S(2)}, u32[]{:S(2)}) collective-permute-start(f32[272,512]{1,0:T(8,128)S(1)} %maximum_maximum_fusion.mine), channel_id=1, source_target_pairs={{0,128},{16,144},{32,160},{48,176},{64,192},{80,208},{96,224},{112... | collective-permute-start | bytes 1671176 | tf_op jit(solution)/shard_map/ppermute | solution.py:337
  34.9 21.1 %collective-permute-start.2 = (f32[272,512]{1,0:T(8,128)S(1)}, f32[272,512]{1,0:T(8,128)S(1)}, u32[]{:S(2)}, u32[]{:S(2)}) collective-permute-start(f32[272,512]{1,0:T(8,128)S(1)} %maximum_maximum_fusion.mine), channel_id=1, source_target_pairs={{0,1},{1,0},{2,3},{3,2},{4,5},{5,4},{6,7},{7,6},{8,9},{9,8},{10,11... | collective-permute-start | bytes 1671176 | tf_op jit(solution)/shard_map/ppermute | solution.py:338
  54.1 3.8 %collective-permute-start.4 = (f32[272,512]{1,0:T(8,128)S(1)}, f32[272,512]{1,0:T(8,128)S(1)}, u32[]{:S(2)}, u32[]{:S(2)}) collective-permute-start(f32[272,512]{1,0:T(8,128)S(1)} %collective-permute-done.3.next_x), channel_id=1, source_target_pairs={{0,1},{1,0},{2,3},{3,2},{4,5},{5,4},{6,7},{7,6},{8,9},{9,8},{10,11... | collective-permute-start | bytes 1671176 | tf_op jit(solution)/shard_map/ppermute | solution.py:345
  99.4 13.9 %all-to-all-start.3 = ((f32[32,4,128]{2,1,0:T(4,128)}), f32[32,4,128]{2,1,0:T(4,128)S(1)}, u32[]{:S(2)}, u32[]{:S(2)}) async-start(f32[32,4,128]{2,1,0:T(4,128)} %get-tuple-element.30), calls=%async_computation.3 | async-start | bytes 131072 | tf_op jit(solution)/shard_map/all_to_all | solution.py:358
  104.4 3.1 %collective-permute-start.5 = (f32[32,256]{1,0:T(8,128)S(1)}, f32[32,256]{1,0:T(8,128)S(1)}, u32[]{:S(2)}, u32[]{:S(2)}) collective-permute-start(f32[32,256]{1,0:T(8,128)S(1)} %get-tuple-element.29), channel_id=1, source_target_pairs={{0,1},{1,0},{2,3},{3,2},{4,5},{5,4},{6,7},{7,6},{8,9},{9,8},{10,11... | collective-permute-start | bytes 98312 | tf_op jit(solution)/shard_map/ppermute | solution.py:359
  107.5 5.8 %copy-start.3 = (f32[1,32,512]{2,1,0:T(8,128)S(1)}, f32[1,32,512]{2,1,0:T(8,128)}, u32[]{:S(2)}) copy-start(f32[1,32,512]{2,1,0:T(8,128)} %pivot.1) | copy-start | bytes 196612
